TPU v7x, 512 devices: a whole 4x8x8 slice. The times are simulated.
512 devices in a mesh: ply: 16 (over z_hi, y), tile: 32 (over z_lo, x, core).
Axes of the slice: x: 4, y: 8, z: 8 (z_hi: 2, z_lo: 4; z = z_hi * 4 + z_lo), core: 2. Of those that a mesh axis runs over, the one named last changes fastest.
Arguments:
- scaled_warmth: float32 [64, 256, 1024], P('ply', 'tile'), may hold values from 0.9 to 1.1
- crosslink_fraction: float32 [64, 256, 1024], P('ply', 'tile'), may hold values from 0 to 0.4
- fluid_stress: float32 [64, 256, 1024], P('ply', 'tile'), may hold values from 0 to 1
- preform_porosity_coefficient: float32 [64, 256, 1024], P('ply', 'tile'), may hold values from 0.02 to 0.2
- wetted_flags: int32 [64, 256, 1024], P('ply', 'tile'), may hold values 0 or 1
- injection_flags: int32 [64, 256, 1024], P('ply', 'tile'), may hold values 0 or 1
- outlet_flags: int32 [64, 256, 1024], P('ply', 'tile'), may hold values 0 or 1
Outputs:
- temperature_out: float32 [64, 256, 1024], P('ply', 'tile')
- cure_out: float32 [64, 256, 1024], P('ply', 'tile')
- pressure_out: float32 [64, 256, 1024], P('ply', 'tile')
- imbalance_record: float32 [2], replicated
All inputs are finite; a program needn't handle non-finite values. No bound on the sum of `wetted_flags` or of `injection_flags` or of `outlet_flags` on one device may be relied on, other than what follows from the above.
Results may differ from a plain program's by a relative error of at most 0.0003.
Values sent between devices are 32-bit elements; how exact they have to be, the bound alone decides.
No kernel may reach another device: no remote copies, remote signals or barrier semaphores. Data moves between devices by JAX's collectives and lax.ppermute only.
A program may use at most 64 MiB of HBM per device.

v0:
```python
import jax
import jax.numpy as jnp
from jax import lax
from jax.sharding import PartitionSpec as P

STEPS = 2
SWEEPS = 4


fluidity_barrier = 4.0
fluidity_gelation_coefficient = 2.0
arrhenius_prefactor = 0.2
arrhenius_barrier = 8.0
released_enthalpy = 0.3
diffusion_coefficient = 0.1
clock_step_size = 0.5
epsilon = 1e-06


def with_halo(cells, sides, width):
    for axis, dim in sides:
        count = lax.axis_size(axis)
        ends = count - 1
        head = lax.slice_in_dim(cells, 0, width, axis=dim)
        tail = lax.slice_in_dim(cells, cells.shape[dim] - width, cells.shape[dim], axis=dim)
        cells = jnp.concatenate(
            [
                lax.ppermute(tail, axis, [(i, (i + 1) % count) for i in range(ends)]),
                cells,
                lax.ppermute(head, axis, [((i + 1) % count, i) for i in range(ends)]),
            ],
            axis=dim,
        )
    return cells


def interior(array):
    return array[1:-1, 1:-1, 1:-1]


def nearby_sites(array):
    return [
        array[2:, 1:-1, 1:-1],
        array[:-2, 1:-1, 1:-1],
        array[1:-1, 2:, 1:-1],
        array[1:-1, :-2, 1:-1],
        array[1:-1, 1:-1, 2:],
        array[1:-1, 1:-1, :-2],
    ]


def pad_across(array, width):
    return jnp.pad(array, [(0, 0)] * (array.ndim - 1) + [(width, width)])


def face_mobility(mobility_pad):
    centre = interior(mobility_pad)
    result = []
    for beside in nearby_sites(mobility_pad):
        denom = centre + beside
        result.append(2.0 * centre * beside / jnp.where(denom > 0, denom, 1.0))
    return result


def jacobi_sweep(pressure_pad, boundary_sides, dry_site, fixed_value):
    beside = nearby_sites(pressure_pad)
    weighted = boundary_sides[0] * beside[0]
    diagonal_sum = boundary_sides[0]
    for iteration_counter in range(1, 6):
        weighted = weighted + boundary_sides[iteration_counter] * beside[iteration_counter]
        diagonal_sum = diagonal_sum + boundary_sides[iteration_counter]
    return jnp.where(
        dry_site > 0, weighted / jnp.where(dry_site > 0, diagonal_sum, 1.0), fixed_value
    )


def donor_advection(
    fluid_stress,
    scaled_warmth,
    crosslink_fraction,
    boundary_sides,
    nearby_stress,
    nearby_warmth,
    nearby_crosslink,
    wetted_status,
    nearby_wetted,
    dry_site,
):
    weighted = boundary_sides[0] * nearby_stress[0]
    diagonal_sum = boundary_sides[0]
    for iteration_counter in range(1, 6):
        weighted = weighted + boundary_sides[iteration_counter] * nearby_stress[iteration_counter]
        diagonal_sum = diagonal_sum + boundary_sides[iteration_counter]
    darcy_imbalance = dry_site * (weighted - diagonal_sum * fluid_stress)
    donor_warmth_advance = jnp.zeros_like(scaled_warmth)
    donor_crosslink_advance = jnp.zeros_like(scaled_warmth)
    diffusive_stream = jnp.zeros_like(scaled_warmth)
    for iteration_counter in range(6):
        inward_stream = (
            jnp.maximum(
                boundary_sides[iteration_counter]
                * (nearby_stress[iteration_counter] - fluid_stress),
                0.0,
            )
            * nearby_wetted[iteration_counter]
        )
        donor_warmth_advance = donor_warmth_advance + inward_stream * (
            nearby_warmth[iteration_counter] - scaled_warmth
        )
        donor_crosslink_advance = donor_crosslink_advance + inward_stream * (
            nearby_crosslink[iteration_counter] - crosslink_fraction
        )
        diffusive_stream = diffusive_stream + nearby_wetted[iteration_counter] * (
            nearby_warmth[iteration_counter] - scaled_warmth
        )
    crosslink_speed = (
        arrhenius_prefactor
        * jnp.exp(arrhenius_barrier * (1.0 - 1.0 / scaled_warmth))
        * (1.0 - crosslink_fraction)
    )
    advanced_warmth = scaled_warmth + wetted_status * clock_step_size * (
        donor_warmth_advance
        + diffusion_coefficient * diffusive_stream
        + released_enthalpy * crosslink_speed
    )
    advanced_crosslink = crosslink_fraction + wetted_status * clock_step_size * (
        donor_crosslink_advance + crosslink_speed
    )
    return (darcy_imbalance, advanced_warmth, advanced_crosslink)


def per_device(
    scaled_warmth,
    crosslink_fraction,
    fluid_stress,
    preform_porosity_coefficient,
    wetted_flags,
    injection_flags,
    outlet_flags,
):
    wetted_status = wetted_flags.astype(jnp.float32)
    inlet_cell = injection_flags.astype(jnp.float32)
    dry_site = wetted_status * (1.0 - inlet_cell) * (1.0 - outlet_flags.astype(jnp.float32))
    site_total = scaled_warmth.size * lax.axis_size("ply") * lax.axis_size("tile")
    fill_pad = pad_across(with_halo(wetted_flags, (("ply", 0), ("tile", 1)), 1), 1).astype(
        jnp.float32
    )
    nearby_wetted = nearby_sites(fill_pad)
    gathered_magnitudes = []
    for repeat in range(STEPS):
        fluid_conductance = preform_porosity_coefficient * jnp.exp(
            -(
                fluidity_barrier * (1.0 / scaled_warmth - 1.0)
                + fluidity_gelation_coefficient * crosslink_fraction
            )
        )
        mobility_pad = pad_across(with_halo(fluid_conductance, (("ply", 0), ("tile", 1)), 1), 1)
        boundary_sides = face_mobility(mobility_pad)
        for sweep_index in range(SWEEPS):
            pressure_pad = pad_across(with_halo(fluid_stress, (("ply", 0), ("tile", 1)), 1), 1)
            fluid_stress = jacobi_sweep(pressure_pad, boundary_sides, dry_site, inlet_cell)
        state_pad = with_halo(
            jnp.stack((fluid_stress, scaled_warmth, crosslink_fraction)),
            (("ply", 1), ("tile", 2)),
            1,
        )
        state_pad = pad_across(state_pad, 1)
        darcy_imbalance, scaled_warmth, crosslink_fraction = donor_advection(
            fluid_stress,
            scaled_warmth,
            crosslink_fraction,
            boundary_sides,
            nearby_sites(state_pad[0]),
            nearby_sites(state_pad[1]),
            nearby_sites(state_pad[2]),
            wetted_status,
            nearby_wetted,
            dry_site,
        )
        local_sum = jnp.sum(darcy_imbalance * darcy_imbalance)
        total = lax.psum(local_sum, ("ply", "tile"))
        gathered_magnitudes.append(jnp.sqrt(total / site_total + epsilon))
    imbalance_record = jnp.stack(gathered_magnitudes)
    return (scaled_warmth, crosslink_fraction, fluid_stress, imbalance_record)


def solution(mesh):
    return jax.shard_map(
        per_device,
        mesh=mesh,
        in_specs=(
            P("ply", "tile", None),
            P("ply", "tile", None),
            P("ply", "tile", None),
            P("ply", "tile", None),
            P("ply", "tile", None),
            P("ply", "tile", None),
            P("ply", "tile", None),
        ),
        out_specs=(P("ply", "tile", None), P("ply", "tile", None), P("ply", "tile", None), P()),
        check_vma=False,
    )
```

profile of v0, /device:TPU:1, one launch (start us, length us, event | category | flops | bytes accessed | tf_op | source)
XLA Modules:
  0.0 399.7 jit_solution(17340357588928965785)
XLA Ops:
  3.1 4.6 %collective-permute-start.2 = (f32[1,8,1024]{2,1,0:T(8,128)S(1)}, f32[1,8,1024]{2,1,0:T(8,128)S(1)}, u32[]{:S(2)}, u32[]{:S(2)}) collective-permute-start(f32[1,8,1024]{2,1,0:T(8,128)S(1)} %get-tuple-element.90), channel_id=1, source_target_pairs={{0,32},{32,64},{64,96},{96,128},{128,160},{160,192},{192,224},{224... | collective-permute-start | bytes 98312 | tf_op jit(solution)/shard_map/ppermute | solution.py:28
  8.6 3.4 collective-permute-start.3
  13.3 7.2 %collective-permute-start.4 = (f32[6,1,1024]{2,1,0:T(1,128)S(1)}, f32[6,1,1024]{2,1,0:T(1,128)S(1)}, u32[]{:S(2)}, u32[]{:S(2)}) collective-permute-start(f32[6,1,1024]{2,1,0:T(1,128)S(1)} %get-tuple-element.68), channel_id=1, source_target_pairs={{1,0},{2,1},{3,2},{4,3},{5,4},{6,5},{7,6},{8,7},{9,8},{10,9},{11,1... | collective-permute-start | bytes 73736 | tf_op jit(solution)/shard_map/ppermute | solution.py:30
  23.4 2.4 collective-permute-start.5
  25.8 3.2 collective-permute-start.7
  32.1 4.9 %collective-permute-start.9 = (f32[1,8,1024]{2,1,0:T(8,128)S(1)}, f32[1,8,1024]{2,1,0:T(8,128)S(1)}, u32[]{:S(2)}, u32[]{:S(2)}) collective-permute-start(f32[1,8,1024]{2,1,0:T(8,128)S(1)} %get-tuple-element.87), channel_id=1, source_target_pairs={{0,32},{32,64},{64,96},{96,128},{128,160},{160,192},{192,224},{224... | collective-permute-start | bytes 98312 | tf_op jit(solution)/shard_map/ppermute | solution.py:28
  37.0 3.4 collective-permute-start.24
  43.6 5.1 %collective-permute-start.11 = (f32[6,1,1024]{2,1,0:T(1,128)S(1)}, f32[6,1,1024]{2,1,0:T(1,128)S(1)}, u32[]{:S(2)}, u32[]{:S(2)}) collective-permute-start(f32[6,1,1024]{2,1,0:T(1,128)S(1)} %get-tuple-element.65), channel_id=1, source_target_pairs={{0,1},{1,2},{2,3},{3,4},{4,5},{5,6},{6,7},{7,8},{8,9},{9,10},{10,1... | collective-permute-start | bytes 73736 | tf_op jit(solution)/shard_map/ppermute | solution.py:28
  51.5 4.9 %collective-permute-start.13 = (f32[1,8,1024]{2,1,0:T(8,128)S(1)}, f32[1,8,1024]{2,1,0:T(8,128)S(1)}, u32[]{:S(2)}, u32[]{:S(2)}) collective-permute-start(f32[1,8,1024]{2,1,0:T(8,128)S(1)} %get-tuple-element.85), channel_id=1, source_target_pairs={{0,32},{32,64},{64,96},{96,128},{128,160},{160,192},{192,224},{224... | collective-permute-start | bytes 98312 | tf_op jit(solution)/shard_map/ppermute | solution.py:28
  59.4 5.1 %collective-permute-start.15 = (f32[6,1,1024]{2,1,0:T(1,128)S(1)}, f32[6,1,1024]{2,1,0:T(1,128)S(1)}, u32[]{:S(2)}, u32[]{:S(2)}) collective-permute-start(f32[6,1,1024]{2,1,0:T(1,128)S(1)} %get-tuple-element.63), channel_id=1, source_target_pairs={{0,1},{1,2},{2,3},{3,4},{4,5},{5,6},{6,7},{7,8},{8,9},{9,10},{10,1... | collective-permute-start | bytes 73736 | tf_op jit(solution)/shard_map/ppermute | solution.py:28
  67.2 4.6 %collective-permute-start.17 = (f32[1,8,1024]{2,1,0:T(8,128)S(1)}, f32[1,8,1024]{2,1,0:T(8,128)S(1)}, u32[]{:S(2)}, u32[]{:S(2)}) collective-permute-start(f32[1,8,1024]{2,1,0:T(8,128)S(1)} %get-tuple-element.83), channel_id=1, source_target_pairs={{0,32},{32,64},{64,96},{96,128},{128,160},{160,192},{192,224},{224... | collective-permute-start | bytes 98312 | tf_op jit(solution)/shard_map/ppermute | solution.py:28
  71.8 4.5 %collective-permute-start.26 = (s32[6,1,1024]{2,1,0:T(1,128)S(1)}, s32[6,1,1024]{2,1,0:T(1,128)S(1)}, u32[]{:S(2)}, u32[]{:S(2)}) collective-permute-start(s32[6,1,1024]{2,1,0:T(1,128)S(1)} %get-tuple-element.59), channel_id=1, source_target_pairs={{0,1},{1,2},{2,3},{3,4},{4,5},{5,6},{6,7},{7,8},{8,9},{9,10},{10,1... | collective-permute-start | bytes 73736 | tf_op jit(solution)/shard_map/ppermute | solution.py:28
  80.3 3.8 collective-permute-start.19
  85.6 3.6 collective-permute-start.20
  91.0 4.1 %collective-permute-done.21 = f32[3,1,8,1024]{3,2,1,0:T(8,128)S(1)} collective-permute-done((f32[3,1,8,1024]{3,2,1,0:T(8,128)S(1)}, f32[3,1,8,1024]{3,2,1,0:T(8,128)S(1)}, u32[]{:S(2)}, u32[]{:S(2)}) %collective-permute-start.21) | collective-permute-done | bytes 98336 | tf_op jit(solution)/shard_map/ppermute | solution.py:30
  95.1 5.2 %collective-permute-start.22 = (f32[3,6,1,1024]{3,2,1,0:T(1,128)S(1)}, f32[3,6,1,1024]{3,2,1,0:T(1,128)S(1)}, u32[]{:S(2)}, u32[]{:S(2)}) collective-permute-start(f32[3,6,1,1024]{3,2,1,0:T(1,128)S(1)} %get-tuple-element.43), channel_id=1, source_target_pairs={{0,1},{1,2},{2,3},{3,4},{4,5},{5,6},{6,7},{7,8},{8,9},{9,10},{10,1... | collective-permute-start | bytes 221192 | tf_op jit(solution)/shard_map/ppermute | solution.py:28
  103.6 7.0 %collective-permute-start.31 = (f32[1,8,1024]{2,1,0:T(8,128)S(1)}, f32[1,8,1024]{2,1,0:T(8,128)S(1)}, u32[]{:S(2)}, u32[]{:S(2)}) collective-permute-start(f32[1,8,1024]{2,1,0:T(8,128)S(1)} %get-tuple-element.79), channel_id=1, source_target_pairs={{0,32},{32,64},{64,96},{96,128},{128,160},{160,192},{192,224},{224... | collective-permute-start | bytes 98312 | tf_op jit(solution)/shard_map/ppermute | solution.py:28
  114.7 10.3 %collective-permute-start.30 = (f32[1,8,1024]{2,1,0:T(8,128)S(1)}, f32[1,8,1024]{2,1,0:T(8,128)S(1)}, u32[]{:S(2)}, u32[]{:S(2)}) collective-permute-start(f32[1,8,1024]{2,1,0:T(8,128)S(1)} %get-tuple-element.78), channel_id=1, source_target_pairs={{0,32},{32,64},{64,96},{96,128},{128,160},{160,192},{192,224},{224... | collective-permute-start | bytes 98312 | tf_op jit(solution)/shard_map/ppermute | solution.py:28
  127.0 4.2 %collective-permute-start.35 = (f32[6,1,1024]{2,1,0:T(1,128)S(1)}, f32[6,1,1024]{2,1,0:T(1,128)S(1)}, u32[]{:S(2)}, u32[]{:S(2)}) collective-permute-start(f32[6,1,1024]{2,1,0:T(1,128)S(1)} %get-tuple-element.57), channel_id=1, source_target_pairs={{0,1},{1,2},{2,3},{3,4},{4,5},{5,6},{6,7},{7,8},{8,9},{9,10},{10,1... | collective-permute-start | bytes 73736 | tf_op jit(solution)/shard_map/ppermute | solution.py:28
  133.2 3.6 collective-permute-start.34
  139.8 5.5 %collective-permute-start.37 = (f32[1,8,1024]{2,1,0:T(8,128)S(1)}, f32[1,8,1024]{2,1,0:T(8,128)S(1)}, u32[]{:S(2)}, u32[]{:S(2)}) collective-permute-start(f32[1,8,1024]{2,1,0:T(8,128)S(1)} %get-tuple-element.75), channel_id=1, source_target_pairs={{0,32},{32,64},{64,96},{96,128},{128,160},{160,192},{192,224},{224... | collective-permute-start | bytes 98312 | tf_op jit(solution)/shard_map/ppermute | solution.py:28
  148.3 5.1 %collective-permute-start.39 = (f32[6,1,1024]{2,1,0:T(1,128)S(1)}, f32[6,1,1024]{2,1,0:T(1,128)S(1)}, u32[]{:S(2)}, u32[]{:S(2)}) collective-permute-start(f32[6,1,1024]{2,1,0:T(1,128)S(1)} %get-tuple-element.53), channel_id=1, source_target_pairs={{0,1},{1,2},{2,3},{3,4},{4,5},{5,6},{6,7},{7,8},{8,9},{9,10},{10,1... | collective-permute-start | bytes 73736 | tf_op jit(solution)/shard_map/ppermute | solution.py:28
  156.1 9.1 %collective-permute-start.41 = (f32[1,8,1024]{2,1,0:T(8,128)S(1)}, f32[1,8,1024]{2,1,0:T(8,128)S(1)}, u32[]{:S(2)}, u32[]{:S(2)}) collective-permute-start(f32[1,8,1024]{2,1,0:T(8,128)S(1)} %get-tuple-element.73), channel_id=1, source_target_pairs={{0,32},{32,64},{64,96},{96,128},{128,160},{160,192},{192,224},{224... | collective-permute-start | bytes 98312 | tf_op jit(solution)/shard_map/ppermute | solution.py:28
  168.2 5.1 %collective-permute-start.43 = (f32[6,1,1024]{2,1,0:T(1,128)S(1)}, f32[6,1,1024]{2,1,0:T(1,128)S(1)}, u32[]{:S(2)}, u32[]{:S(2)}) collective-permute-start(f32[6,1,1024]{2,1,0:T(1,128)S(1)} %get-tuple-element.51), channel_id=1, source_target_pairs={{0,1},{1,2},{2,3},{3,4},{4,5},{5,6},{6,7},{7,8},{8,9},{9,10},{10,1... | collective-permute-start | bytes 73736 | tf_op jit(solution)/shard_map/ppermute | solution.py:28
  176.1 10.6 %collective-permute-start.45 = (f32[1,8,1024]{2,1,0:T(8,128)S(1)}, f32[1,8,1024]{2,1,0:T(8,128)S(1)}, u32[]{:S(2)}, u32[]{:S(2)}) collective-permute-start(f32[1,8,1024]{2,1,0:T(8,128)S(1)} %get-tuple-element.71), channel_id=1, source_target_pairs={{0,32},{32,64},{64,96},{96,128},{128,160},{160,192},{192,224},{224... | collective-permute-start | bytes 98312 | tf_op jit(solution)/shard_map/ppermute | solution.py:28
  189.6 5.1 %collective-permute-start.47 = (f32[6,1,1024]{2,1,0:T(1,128)S(1)}, f32[6,1,1024]{2,1,0:T(1,128)S(1)}, u32[]{:S(2)}, u32[]{:S(2)}) collective-permute-start(f32[6,1,1024]{2,1,0:T(1,128)S(1)} %get-tuple-element.49), channel_id=1, source_target_pairs={{0,1},{1,2},{2,3},{3,4},{4,5},{5,6},{6,7},{7,8},{8,9},{9,10},{10,1... | collective-permute-start | bytes 73736 | tf_op jit(solution)/shard_map/ppermute | solution.py:28
  196.2 5.9 %collective-permute-start.48 = (f32[3,1,8,1024]{3,2,1,0:T(8,128)S(1)}, f32[3,1,8,1024]{3,2,1,0:T(8,128)S(1)}, u32[]{:S(2)}, u32[]{:S(2)}) collective-permute-start(f32[3,1,8,1024]{3,2,1,0:T(8,128)S(1)} %get-tuple-element.45), channel_id=1, source_target_pairs={{0,32},{32,64},{64,96},{96,128},{128,160},{160,192},{192,224},{224... | collective-permute-start | bytes 294920 | tf_op jit(solution)/shard_map/ppermute | solution.py:28
  203.7 10.5 %collective-permute-done.49 = f32[3,1,8,1024]{3,2,1,0:T(8,128)S(1)} collective-permute-done((f32[3,1,8,1024]{3,2,1,0:T(8,128)S(1)}, f32[3,1,8,1024]{3,2,1,0:T(8,128)S(1)}, u32[]{:S(2)}, u32[]{:S(2)}) %collective-permute-start.49) | collective-permute-done | bytes 98336 | tf_op jit(solution)/shard_map/ppermute | solution.py:30
  214.3 5.4 %collective-permute-start.50 = (f32[3,6,1,1024]{3,2,1,0:T(1,128)S(1)}, f32[3,6,1,1024]{3,2,1,0:T(1,128)S(1)}, u32[]{:S(2)}, u32[]{:S(2)}) collective-permute-start(f32[3,6,1,1024]{3,2,1,0:T(1,128)S(1)} %get-tuple-element.41), channel_id=1, source_target_pairs={{0,1},{1,2},{2,3},{3,4},{4,5},{5,6},{6,7},{7,8},{8,9},{9,10},{10,1... | collective-permute-start | bytes 221192 | tf_op jit(solution)/shard_map/ppermute | solution.py:28
  219.7 2.1 collective-permute-start.51
  221.8 3.6 collective-permute-done.51
  227.1 168.3 %all-reduce.13 = (f32[]{:T(128)}, f32[]{:T(128)}) all-reduce(f32[]{:T(128)} %multiply_reduce_fusion, f32[]{:T(128)} %get-tuple-element.39), channel_id=1, replica_groups=mesh['ply'=16,'tile'=32] {'ply','tile'}, use_global_device_ids=true, to_apply=%region_3.4 | all-reduce | flops 2 | bytes 16 | tf_op jit(solution)/shard_map/psum | solution.py:181
  (153 shorter events, 65.6 us)
Async XLA Ops:
  1.8 11.4 %collective-permute-start = (f32[1,8,1024]{2,1,0:T(8,128)S(1)}, f32[1,8,1024]{2,1,0:T(8,128)S(1)}, u32[]{:S(2)}, u32[]{:S(2)}) collective-permute-start(f32[1,8,1024]{2,1,0:T(8,128)S(1)} %get-tuple-element.89), channel_id=1, source_target_pairs={{32,0},{64,32},{96,64},{128,96},{160,128},{192,160},{224,192},{256... | collective-permute-start | bytes 98312 | tf_op jit(solution)/shard_map/ppermute | solution.py:30
  3.1 10.1 %collective-permute-start.2 = (f32[1,8,1024]{2,1,0:T(8,128)S(1)}, f32[1,8,1024]{2,1,0:T(8,128)S(1)}, u32[]{:S(2)}, u32[]{:S(2)}) collective-permute-start(f32[1,8,1024]{2,1,0:T(8,128)S(1)} %get-tuple-element.90), channel_id=1, source_target_pairs={{0,32},{32,64},{64,96},{96,128},{128,160},{160,192},{192,224},{224... | collective-permute-start | bytes 98312 | tf_op jit(solution)/shard_map/ppermute | solution.py:28
  8.6 13.9 %collective-permute-start.3 = (f32[1,8,1024]{2,1,0:T(8,128)S(1)}, f32[1,8,1024]{2,1,0:T(8,128)S(1)}, u32[]{:S(2)}, u32[]{:S(2)}) collective-permute-start(f32[1,8,1024]{2,1,0:T(8,128)S(1)} %get-tuple-element.92), channel_id=1, source_target_pairs={{0,32},{32,64},{64,96},{96,128},{128,160},{160,192},{192,224},{224... | collective-permute-start | bytes 98312 | tf_op jit(solution)/shard_map/ppermute | solution.py:28
  11.9 11.4 %collective-permute-start.1 = (f32[1,8,1024]{2,1,0:T(8,128)S(1)}, f32[1,8,1024]{2,1,0:T(8,128)S(1)}, u32[]{:S(2)}, u32[]{:S(2)}) collective-permute-start(f32[1,8,1024]{2,1,0:T(8,128)S(1)} %get-tuple-element.91), channel_id=1, source_target_pairs={{32,0},{64,32},{96,64},{128,96},{160,128},{192,160},{224,192},{256... | collective-permute-start | bytes 98312 | tf_op jit(solution)/shard_map/ppermute | solution.py:30
  13.3 15.7 %collective-permute-start.4 = (f32[6,1,1024]{2,1,0:T(1,128)S(1)}, f32[6,1,1024]{2,1,0:T(1,128)S(1)}, u32[]{:S(2)}, u32[]{:S(2)}) collective-permute-start(f32[6,1,1024]{2,1,0:T(1,128)S(1)} %get-tuple-element.68), channel_id=1, source_target_pairs={{1,0},{2,1},{3,2},{4,3},{5,4},{6,5},{7,6},{8,7},{9,8},{10,9},{11,1... | collective-permute-start | bytes 73736 | tf_op jit(solution)/shard_map/ppermute | solution.py:30
  20.5 8.5 %collective-permute-start.6 = (f32[6,1,1024]{2,1,0:T(1,128)S(1)}, f32[6,1,1024]{2,1,0:T(1,128)S(1)}, u32[]{:S(2)}, u32[]{:S(2)}) collective-permute-start(f32[6,1,1024]{2,1,0:T(1,128)S(1)} %get-tuple-element.67), channel_id=1, source_target_pairs={{0,1},{1,2},{2,3},{3,4},{4,5},{5,6},{6,7},{7,8},{8,9},{9,10},{10,1... | collective-permute-start | bytes 73736 | tf_op jit(solution)/shard_map/ppermute | solution.py:28
  30.8 10.9 %collective-permute-start.8 = (f32[1,8,1024]{2,1,0:T(8,128)S(1)}, f32[1,8,1024]{2,1,0:T(8,128)S(1)}, u32[]{:S(2)}, u32[]{:S(2)}) collective-permute-start(f32[1,8,1024]{2,1,0:T(8,128)S(1)} %get-tuple-element.88), channel_id=1, source_target_pairs={{32,0},{64,32},{96,64},{128,96},{160,128},{192,160},{224,192},{256... | collective-permute-start | bytes 98312 | tf_op jit(solution)/shard_map/ppermute | solution.py:30
  32.1 9.6 %collective-permute-start.9 = (f32[1,8,1024]{2,1,0:T(8,128)S(1)}, f32[1,8,1024]{2,1,0:T(8,128)S(1)}, u32[]{:S(2)}, u32[]{:S(2)}) collective-permute-start(f32[1,8,1024]{2,1,0:T(8,128)S(1)} %get-tuple-element.87), channel_id=1, source_target_pairs={{0,32},{32,64},{64,96},{96,128},{128,160},{160,192},{192,224},{224... | collective-permute-start | bytes 98312 | tf_op jit(solution)/shard_map/ppermute | solution.py:28
  37.0 11.7 %collective-permute-start.24 = (s32[1,8,1024]{2,1,0:T(8,128)S(1)}, s32[1,8,1024]{2,1,0:T(8,128)S(1)}, u32[]{:S(2)}, u32[]{:S(2)}) collective-permute-start(s32[1,8,1024]{2,1,0:T(8,128)S(1)} %get-tuple-element.82), channel_id=1, source_target_pairs={{0,32},{32,64},{64,96},{96,128},{128,160},{160,192},{192,224},{224... | collective-permute-start | bytes 98312 | tf_op jit(solution)/shard_map/ppermute | solution.py:28
  40.4 24.1 %collective-permute-start.25 = (s32[1,8,1024]{2,1,0:T(8,128)S(1)}, s32[1,8,1024]{2,1,0:T(8,128)S(1)}, u32[]{:S(2)}, u32[]{:S(2)}) collective-permute-start(s32[1,8,1024]{2,1,0:T(8,128)S(1)} %get-tuple-element.81), channel_id=1, source_target_pairs={{32,0},{64,32},{96,64},{128,96},{160,128},{192,160},{224,192},{256... | collective-permute-start | bytes 98312 | tf_op jit(solution)/shard_map/ppermute | solution.py:30
  41.7 7.0 %collective-permute-start.10 = (f32[6,1,1024]{2,1,0:T(1,128)S(1)}, f32[6,1,1024]{2,1,0:T(1,128)S(1)}, u32[]{:S(2)}, u32[]{:S(2)}) collective-permute-start(f32[6,1,1024]{2,1,0:T(1,128)S(1)} %get-tuple-element.66), channel_id=1, source_target_pairs={{1,0},{2,1},{3,2},{4,3},{5,4},{6,5},{7,6},{8,7},{9,8},{10,9},{11,1... | collective-permute-start | bytes 73736 | tf_op jit(solution)/shard_map/ppermute | solution.py:30
  57.4 7.0 %collective-permute-start.14 = (f32[6,1,1024]{2,1,0:T(1,128)S(1)}, f32[6,1,1024]{2,1,0:T(1,128)S(1)}, u32[]{:S(2)}, u32[]{:S(2)}) collective-permute-start(f32[6,1,1024]{2,1,0:T(1,128)S(1)} %get-tuple-element.64), channel_id=1, source_target_pairs={{1,0},{2,1},{3,2},{4,3},{5,4},{6,5},{7,6},{8,7},{9,8},{10,9},{11,1... | collective-permute-start | bytes 73736 | tf_op jit(solution)/shard_map/ppermute | solution.py:30
  65.9 12.4 %collective-permute-start.16 = (f32[1,8,1024]{2,1,0:T(8,128)S(1)}, f32[1,8,1024]{2,1,0:T(8,128)S(1)}, u32[]{:S(2)}, u32[]{:S(2)}) collective-permute-start(f32[1,8,1024]{2,1,0:T(8,128)S(1)} %get-tuple-element.84), channel_id=1, source_target_pairs={{32,0},{64,32},{96,64},{128,96},{160,128},{192,160},{224,192},{256... | collective-permute-start | bytes 98312 | tf_op jit(solution)/shard_map/ppermute | solution.py:30
  67.2 11.1 %collective-permute-start.17 = (f32[1,8,1024]{2,1,0:T(8,128)S(1)}, f32[1,8,1024]{2,1,0:T(8,128)S(1)}, u32[]{:S(2)}, u32[]{:S(2)}) collective-permute-start(f32[1,8,1024]{2,1,0:T(8,128)S(1)} %get-tuple-element.83), channel_id=1, source_target_pairs={{0,32},{32,64},{64,96},{96,128},{128,160},{160,192},{192,224},{224... | collective-permute-start | bytes 98312 | tf_op jit(solution)/shard_map/ppermute | solution.py:28
  71.8 12.2 %collective-permute-start.26 = (s32[6,1,1024]{2,1,0:T(1,128)S(1)}, s32[6,1,1024]{2,1,0:T(1,128)S(1)}, u32[]{:S(2)}, u32[]{:S(2)}) collective-permute-start(s32[6,1,1024]{2,1,0:T(1,128)S(1)} %get-tuple-element.59), channel_id=1, source_target_pairs={{0,1},{1,2},{2,3},{3,4},{4,5},{5,6},{6,7},{7,8},{8,9},{9,10},{10,1... | collective-permute-start | bytes 73736 | tf_op jit(solution)/shard_map/ppermute | solution.py:28
  76.3 7.7 %collective-permute-start.27 = (s32[6,1,1024]{2,1,0:T(1,128)S(1)}, s32[6,1,1024]{2,1,0:T(1,128)S(1)}, u32[]{:S(2)}, u32[]{:S(2)}) collective-permute-start(s32[6,1,1024]{2,1,0:T(1,128)S(1)} %get-tuple-element.60), channel_id=1, source_target_pairs={{1,0},{2,1},{3,2},{4,3},{5,4},{6,5},{7,6},{8,7},{9,8},{10,9},{11,1... | collective-permute-start | bytes 73736 | tf_op jit(solution)/shard_map/ppermute | solution.py:30
  95.1 15.4 %collective-permute-start.22 = (f32[3,6,1,1024]{3,2,1,0:T(1,128)S(1)}, f32[3,6,1,1024]{3,2,1,0:T(1,128)S(1)}, u32[]{:S(2)}, u32[]{:S(2)}) collective-permute-start(f32[3,6,1,1024]{3,2,1,0:T(1,128)S(1)} %get-tuple-element.43), channel_id=1, source_target_pairs={{0,1},{1,2},{2,3},{3,4},{4,5},{5,6},{6,7},{7,8},{8,9},{9,10},{10,1... | collective-permute-start | bytes 221192 | tf_op jit(solution)/shard_map/ppermute | solution.py:28
  100.3 10.3 %collective-permute-start.23 = (f32[3,6,1,1024]{3,2,1,0:T(1,128)S(1)}, f32[3,6,1,1024]{3,2,1,0:T(1,128)S(1)}, u32[]{:S(2)}, u32[]{:S(2)}) collective-permute-start(f32[3,6,1,1024]{3,2,1,0:T(1,128)S(1)} %get-tuple-element.44), channel_id=1, source_target_pairs={{1,0},{2,1},{3,2},{4,3},{5,4},{6,5},{7,6},{8,7},{9,8},{10,9},{11,1... | collective-permute-start | bytes 221192 | tf_op jit(solution)/shard_map/ppermute | solution.py:30
  102.3 22.8 %collective-permute-start.29 = (f32[1,8,1024]{2,1,0:T(8,128)S(1)}, f32[1,8,1024]{2,1,0:T(8,128)S(1)}, u32[]{:S(2)}, u32[]{:S(2)}) collective-permute-start(f32[1,8,1024]{2,1,0:T(8,128)S(1)} %get-tuple-element.80), channel_id=1, source_target_pairs={{32,0},{64,32},{96,64},{128,96},{160,128},{192,160},{224,192},{256... | collective-permute-start | bytes 98312 | tf_op jit(solution)/shard_map/ppermute | solution.py:30
  103.6 21.5 %collective-permute-start.31 = (f32[1,8,1024]{2,1,0:T(8,128)S(1)}, f32[1,8,1024]{2,1,0:T(8,128)S(1)}, u32[]{:S(2)}, u32[]{:S(2)}) collective-permute-start(f32[1,8,1024]{2,1,0:T(8,128)S(1)} %get-tuple-element.79), channel_id=1, source_target_pairs={{0,32},{32,64},{64,96},{96,128},{128,160},{160,192},{192,224},{224... | collective-permute-start | bytes 98312 | tf_op jit(solution)/shard_map/ppermute | solution.py:28
  113.4 17.8 %collective-permute-start.28 = (f32[1,8,1024]{2,1,0:T(8,128)S(1)}, f32[1,8,1024]{2,1,0:T(8,128)S(1)}, u32[]{:S(2)}, u32[]{:S(2)}) collective-permute-start(f32[1,8,1024]{2,1,0:T(8,128)S(1)} %get-tuple-element.77), channel_id=1, source_target_pairs={{32,0},{64,32},{96,64},{128,96},{160,128},{192,160},{224,192},{256... | collective-permute-start | bytes 98312 | tf_op jit(solution)/shard_map/ppermute | solution.py:30
  114.7 16.5 %collective-permute-start.30 = (f32[1,8,1024]{2,1,0:T(8,128)S(1)}, f32[1,8,1024]{2,1,0:T(8,128)S(1)}, u32[]{:S(2)}, u32[]{:S(2)}) collective-permute-start(f32[1,8,1024]{2,1,0:T(8,128)S(1)} %get-tuple-element.78), channel_id=1, source_target_pairs={{0,32},{32,64},{64,96},{96,128},{128,160},{160,192},{192,224},{224... | collective-permute-start | bytes 98312 | tf_op jit(solution)/shard_map/ppermute | solution.py:28
  125.1 11.8 %collective-permute-start.33 = (f32[6,1,1024]{2,1,0:T(1,128)S(1)}, f32[6,1,1024]{2,1,0:T(1,128)S(1)}, u32[]{:S(2)}, u32[]{:S(2)}) collective-permute-start(f32[6,1,1024]{2,1,0:T(1,128)S(1)} %get-tuple-element.58), channel_id=1, source_target_pairs={{1,0},{2,1},{3,2},{4,3},{5,4},{6,5},{7,6},{8,7},{9,8},{10,9},{11,1... | collective-permute-start | bytes 73736 | tf_op jit(solution)/shard_map/ppermute | solution.py:30
  127.0 9.9 %collective-permute-start.35 = (f32[6,1,1024]{2,1,0:T(1,128)S(1)}, f32[6,1,1024]{2,1,0:T(1,128)S(1)}, u32[]{:S(2)}, u32[]{:S(2)}) collective-permute-start(f32[6,1,1024]{2,1,0:T(1,128)S(1)} %get-tuple-element.57), channel_id=1, source_target_pairs={{0,1},{1,2},{2,3},{3,4},{4,5},{5,6},{6,7},{7,8},{8,9},{9,10},{10,1... | collective-permute-start | bytes 73736 | tf_op jit(solution)/shard_map/ppermute | solution.py:28
  146.4 7.0 %collective-permute-start.38 = (f32[6,1,1024]{2,1,0:T(1,128)S(1)}, f32[6,1,1024]{2,1,0:T(1,128)S(1)}, u32[]{:S(2)}, u32[]{:S(2)}) collective-permute-start(f32[6,1,1024]{2,1,0:T(1,128)S(1)} %get-tuple-element.54), channel_id=1, source_target_pairs={{1,0},{2,1},{3,2},{4,3},{5,4},{6,5},{7,6},{8,7},{9,8},{10,9},{11,1... | collective-permute-start | bytes 73736 | tf_op jit(solution)/shard_map/ppermute | solution.py:30
  154.8 10.4 %collective-permute-start.40 = (f32[1,8,1024]{2,1,0:T(8,128)S(1)}, f32[1,8,1024]{2,1,0:T(8,128)S(1)}, u32[]{:S(2)}, u32[]{:S(2)}) collective-permute-start(f32[1,8,1024]{2,1,0:T(8,128)S(1)} %get-tuple-element.74), channel_id=1, source_target_pairs={{32,0},{64,32},{96,64},{128,96},{160,128},{192,160},{224,192},{256... | collective-permute-start | bytes 98312 | tf_op jit(solution)/shard_map/ppermute | solution.py:30
  156.1 10.1 %collective-permute-start.41 = (f32[1,8,1024]{2,1,0:T(8,128)S(1)}, f32[1,8,1024]{2,1,0:T(8,128)S(1)}, u32[]{:S(2)}, u32[]{:S(2)}) collective-permute-start(f32[1,8,1024]{2,1,0:T(8,128)S(1)} %get-tuple-element.73), channel_id=1, source_target_pairs={{0,32},{32,64},{64,96},{96,128},{128,160},{160,192},{192,224},{224... | collective-permute-start | bytes 98312 | tf_op jit(solution)/shard_map/ppermute | solution.py:28
  174.8 11.9 %collective-permute-start.44 = (f32[1,8,1024]{2,1,0:T(8,128)S(1)}, f32[1,8,1024]{2,1,0:T(8,128)S(1)}, u32[]{:S(2)}, u32[]{:S(2)}) collective-permute-start(f32[1,8,1024]{2,1,0:T(8,128)S(1)} %get-tuple-element.72), channel_id=1, source_target_pairs={{32,0},{64,32},{96,64},{128,96},{160,128},{192,160},{224,192},{256... | collective-permute-start | bytes 98312 | tf_op jit(solution)/shard_map/ppermute | solution.py:30
  176.1 11.6 %collective-permute-start.45 = (f32[1,8,1024]{2,1,0:T(8,128)S(1)}, f32[1,8,1024]{2,1,0:T(8,128)S(1)}, u32[]{:S(2)}, u32[]{:S(2)}) collective-permute-start(f32[1,8,1024]{2,1,0:T(8,128)S(1)} %get-tuple-element.71), channel_id=1, source_target_pairs={{0,32},{32,64},{64,96},{96,128},{128,160},{160,192},{192,224},{224... | collective-permute-start | bytes 98312 | tf_op jit(solution)/shard_map/ppermute | solution.py:28
  196.2 7.5 %collective-permute-start.48 = (f32[3,1,8,1024]{3,2,1,0:T(8,128)S(1)}, f32[3,1,8,1024]{3,2,1,0:T(8,128)S(1)}, u32[]{:S(2)}, u32[]{:S(2)}) collective-permute-start(f32[3,1,8,1024]{3,2,1,0:T(8,128)S(1)} %get-tuple-element.45), channel_id=1, source_target_pairs={{0,32},{32,64},{64,96},{96,128},{128,160},{160,192},{192,224},{224... | collective-permute-start | bytes 294920 | tf_op jit(solution)/shard_map/ppermute | solution.py:28
  202.1 12.1 %collective-permute-start.49 = (f32[3,1,8,1024]{3,2,1,0:T(8,128)S(1)}, f32[3,1,8,1024]{3,2,1,0:T(8,128)S(1)}, u32[]{:S(2)}, u32[]{:S(2)}) collective-permute-start(f32[3,1,8,1024]{3,2,1,0:T(8,128)S(1)} %get-tuple-element.46), channel_id=1, source_target_pairs={{32,0},{64,32},{96,64},{128,96},{160,128},{192,160},{224,192},{256... | collective-permute-start | bytes 294920 | tf_op jit(solution)/shard_map/ppermute | solution.py:30
  214.3 7.5 %collective-permute-start.50 = (f32[3,6,1,1024]{3,2,1,0:T(1,128)S(1)}, f32[3,6,1,1024]{3,2,1,0:T(1,128)S(1)}, u32[]{:S(2)}, u32[]{:S(2)}) collective-permute-start(f32[3,6,1,1024]{3,2,1,0:T(1,128)S(1)} %get-tuple-element.41), channel_id=1, source_target_pairs={{0,1},{1,2},{2,3},{3,4},{4,5},{5,6},{6,7},{7,8},{8,9},{9,10},{10,1... | collective-permute-start | bytes 221192 | tf_op jit(solution)/shard_map/ppermute | solution.py:28
  (28 other events, 448.5 us)
where the time goes:
time: 401 us; the launch traced here: 400 us
  starting transfers between devices  182 us (45%)
  blocking collectives  168 us (42%)
  waiting for transfers between devices  29.3 us (7%)
  other arithmetic  14.4 us (4%)
    psum x1, blocking collectives, per_device(): total = lax.psum(local_sum, ('ply', 'tile'))  168 us
    ppermute x26, starting transfers between devices, with_halo(): lax.ppermute(tail, axis, [(i, (i + 1) % count) for i in range(ends)])  135 us
    ppermute x26, starting transfers between devices, with_halo(): lax.ppermute(head, axis, [((i + 1) % count, i) for i in range(ends)])  47.7 us
    ppermute x26, waiting for transfers between devices, with_halo(): lax.ppermute(head, axis, [((i + 1) % count, i) for i in range(ends)])  18.2 us
    ppermute x26, waiting for transfers between devices, with_halo(): lax.ppermute(tail, axis, [(i, (i + 1) % count) for i in range(ends)])  11.1 us
  transfers between devices with their start and end apart: 52, of which 17 were waited for; matrix products, arithmetic and copies ran while one was open for 2% of the time, Pallas kernels for 0%

commit v1 on v0

--- a/solution.py
+++ b/solution.py
@@ -2,6 +2,7 @@
 import jax.numpy as jnp
 from jax import lax
 from jax.sharding import PartitionSpec as P
+
 
 STEPS = 2
 SWEEPS = 4
@@ -17,53 +18,60 @@
 epsilon = 1e-06
 
 
-def with_halo(cells, sides, width):
-    for axis, dim in sides:
-        count = lax.axis_size(axis)
-        ends = count - 1
-        head = lax.slice_in_dim(cells, 0, width, axis=dim)
-        tail = lax.slice_in_dim(cells, cells.shape[dim] - width, cells.shape[dim], axis=dim)
-        cells = jnp.concatenate(
-            [
-                lax.ppermute(tail, axis, [(i, (i + 1) % count) for i in range(ends)]),
-                cells,
-                lax.ppermute(head, axis, [((i + 1) % count, i) for i in range(ends)]),
-            ],
-            axis=dim,
-        )
-    return cells
-
-
-def interior(array):
-    return array[1:-1, 1:-1, 1:-1]
-
-
-def nearby_sites(array):
+def swap_pairs(count, parity):
+    pairs = []
+    for i in range(parity, count - 1, 2):
+        pairs += [(i, i + 1), (i + 1, i)]
+    return pairs
+
+
+def trade_faces(array):
+    ply_even = lax.axis_index("ply") % 2 == 0
+    tile_even = lax.axis_index("tile") % 2 == 0
+    first_ply, last_ply = array[:, :1], array[:, -1:]
+    first_row, last_row = array[:, :, :1], array[:, :, -1:]
+    sends = lax.optimization_barrier(
+        (
+            jnp.where(ply_even, first_ply, last_ply),
+            jnp.where(ply_even, last_ply, first_ply),
+            jnp.where(tile_even, first_row, last_row),
+            jnp.where(tile_even, last_row, first_row),
+        )
+    )
+    nply, ntile = lax.axis_size("ply"), lax.axis_size("tile")
+    ply_odd = lax.ppermute(sends[0], "ply", swap_pairs(nply, 1))
+    ply_pair = lax.ppermute(sends[1], "ply", swap_pairs(nply, 0))
+    tile_odd = lax.ppermute(sends[2], "tile", swap_pairs(ntile, 1))
+    tile_pair = lax.ppermute(sends[3], "tile", swap_pairs(ntile, 0))
+    return (
+        jnp.where(ply_even, ply_pair, ply_odd),
+        jnp.where(ply_even, ply_odd, ply_pair),
+        jnp.where(tile_even, tile_pair, tile_odd),
+        jnp.where(tile_even, tile_odd, tile_pair),
+    )
+
+
+def nearby_sites(array, faces):
+    edge = jnp.zeros_like(array[:, :, :1])
     return [
-        array[2:, 1:-1, 1:-1],
-        array[:-2, 1:-1, 1:-1],
-        array[1:-1, 2:, 1:-1],
-        array[1:-1, :-2, 1:-1],
-        array[1:-1, 1:-1, 2:],
-        array[1:-1, 1:-1, :-2],
+        jnp.concatenate([array[1:], faces[0]], axis=0),
+        jnp.concatenate([faces[1], array[:-1]], axis=0),
+        jnp.concatenate([array[:, 1:], faces[2]], axis=1),
+        jnp.concatenate([faces[3], array[:, :-1]], axis=1),
+        jnp.concatenate([array[:, :, 1:], edge], axis=2),
+        jnp.concatenate([edge, array[:, :, :-1]], axis=2),
     ]
 
 
-def pad_across(array, width):
-    return jnp.pad(array, [(0, 0)] * (array.ndim - 1) + [(width, width)])
-
-
-def face_mobility(mobility_pad):
-    centre = interior(mobility_pad)
+def face_mobility(centre, nearby):
     result = []
-    for beside in nearby_sites(mobility_pad):
+    for beside in nearby:
         denom = centre + beside
         result.append(2.0 * centre * beside / jnp.where(denom > 0, denom, 1.0))
     return result
 
 
-def jacobi_sweep(pressure_pad, boundary_sides, dry_site, fixed_value):
-    beside = nearby_sites(pressure_pad)
+def jacobi_sweep(beside, boundary_sides, dry_site, fixed_value):
     weighted = boundary_sides[0] * beside[0]
     diagonal_sum = boundary_sides[0]
     for iteration_counter in range(1, 6):
@@ -141,46 +149,50 @@
     wetted_status = wetted_flags.astype(jnp.float32)
     inlet_cell = injection_flags.astype(jnp.float32)
     dry_site = wetted_status * (1.0 - inlet_cell) * (1.0 - outlet_flags.astype(jnp.float32))
-    site_total = scaled_warmth.size * lax.axis_size("ply") * lax.axis_size("tile")
-    fill_pad = pad_across(with_halo(wetted_flags, (("ply", 0), ("tile", 1)), 1), 1).astype(
-        jnp.float32
-    )
-    nearby_wetted = nearby_sites(fill_pad)
-    gathered_magnitudes = []
-    for repeat in range(STEPS):
+    devices = lax.axis_size("ply") * lax.axis_size("tile")
+    site_total = scaled_warmth.size * devices
+    nearby_wetted = None
+    local_sums = []
+    for _ in range(STEPS):
         fluid_conductance = preform_porosity_coefficient * jnp.exp(
             -(
                 fluidity_barrier * (1.0 / scaled_warmth - 1.0)
                 + fluidity_gelation_coefficient * crosslink_fraction
             )
         )
-        mobility_pad = pad_across(with_halo(fluid_conductance, (("ply", 0), ("tile", 1)), 1), 1)
-        boundary_sides = face_mobility(mobility_pad)
-        for sweep_index in range(SWEEPS):
-            pressure_pad = pad_across(with_halo(fluid_stress, (("ply", 0), ("tile", 1)), 1), 1)
-            fluid_stress = jacobi_sweep(pressure_pad, boundary_sides, dry_site, inlet_cell)
-        state_pad = with_halo(
-            jnp.stack((fluid_stress, scaled_warmth, crosslink_fraction)),
-            (("ply", 1), ("tile", 2)),
-            1,
-        )
-        state_pad = pad_across(state_pad, 1)
+        fields = [fluid_stress, fluid_conductance, scaled_warmth, crosslink_fraction]
+        if nearby_wetted is None:
+            fields.append(wetted_status)
+        faces = trade_faces(jnp.stack(fields))
+        nearby = [
+            nearby_sites(field, [face[k] for face in faces]) for k, field in enumerate(fields)
+        ]
+        nearby_stress, nearby_mobility, nearby_warmth, nearby_crosslink = nearby[:4]
+        if nearby_wetted is None:
+            nearby_wetted = nearby[4]
+        boundary_sides = face_mobility(fluid_conductance, nearby_mobility)
+        for _ in range(SWEEPS):
+            fluid_stress = jacobi_sweep(nearby_stress, boundary_sides, dry_site, inlet_cell)
+            faces = trade_faces(fluid_stress[None])
+            nearby_stress = nearby_sites(fluid_stress, [face[0] for face in faces])
         darcy_imbalance, scaled_warmth, crosslink_fraction = donor_advection(
             fluid_stress,
             scaled_warmth,
             crosslink_fraction,
             boundary_sides,
-            nearby_sites(state_pad[0]),
-            nearby_sites(state_pad[1]),
-            nearby_sites(state_pad[2]),
+            nearby_stress,
+            nearby_warmth,
+            nearby_crosslink,
             wetted_status,
             nearby_wetted,
             dry_site,
         )
-        local_sum = jnp.sum(darcy_imbalance * darcy_imbalance)
-        total = lax.psum(local_sum, ("ply", "tile"))
-        gathered_magnitudes.append(jnp.sqrt(total / site_total + epsilon))
-    imbalance_record = jnp.stack(gathered_magnitudes)
+        local_sums.append(jnp.sum(darcy_imbalance * darcy_imbalance))
+    lane = lax.broadcasted_iota(jnp.int32, (devices, 1, 128), 2)
+    message = jnp.where(lane == 0, local_sums[0], jnp.where(lane == 1, local_sums[1], 0.0))
+    parts = lax.all_to_all(message, ("ply", "tile"), 0, 0)
+    totals = jnp.sum(parts, axis=(0, 1))[:STEPS]
+    imbalance_record = jnp.sqrt(totals / site_total + epsilon)
     return (scaled_warmth, crosslink_fraction, fluid_stress, imbalance_record)
 
 

time: 401 us -> 255 us (0.64)
  blocking collectives: 168 us -> 0 us
  starting transfers between devices: 182 us -> 206 us
  local copies, waits for them, and re-layouts: 2.1 us -> 12.5 us
  waiting for transfers between devices: 29.3 us -> 20.2 us
    psum x1 -> x0, blocking collectives: 168 us -> none  [per_device(): total = lax.psum(local_sum, ('ply', 'tile'))]
    all_to_all x0 -> x1, starting transfers between devices: none -> 43.1 us  [per_device(): parts = lax.all_to_all(message, ('ply', 'tile'), 0, 0)]
    ppermute x52 -> x40, waiting for transfers between devices: 29.3 us -> 8.33 us  [the longest x10 7.4 us: trade_faces(): ply_pair = lax.ppermute(sends[1], 'ply', swap_pairs(nply, 0))]
    ppermute x52 -> x40, starting transfers between devices: 182 us -> 163 us  [the longest x10 91.4 us: trade_faces(): ply_pair = lax.ppermute(sends[1], 'ply', swap_pairs(nply, 0))]
    all_to_all x0 -> x1, waiting for transfers between devices: none -> 11.9 us  [per_device(): parts = lax.all_to_all(message, ('ply', 'tile'), 0, 0)]
    concatenate x22 -> x0, other arithmetic: 4.87 us -> none  [with_halo(): jnp.concatenate([lax.ppermute(tail, axis, [(i, (i + 1) % count) for i in...]
    slice x13 -> x42, local copies, waits for them, and re-layouts: 0.92 us -> 5.26 us  [the longest x11 2.31 us: nearby_sites(): array[:, :, 1:]]
  transfers between devices with their start and end apart: 52 -> 41, of which waited for: 17 -> 12; matrix products, arithmetic and copies ran while one was open for 2% -> 3% of each run, Pallas kernels for 0% -> 0%
where the time goes in v1:
time: 255 us; the launch traced here: 254 us
  starting transfers between devices  206 us (81%)
  waiting for transfers between devices  20.2 us (8%)
  other arithmetic  12.9 us (5%)
  local copies, waits for them, and re-layouts  12.5 us (5%)
    ppermute x10, starting transfers between devices, trade_faces(): ply_pair = lax.ppermute(sends[1], 'ply', swap_pairs(nply, 0))  91.4 us
    all_to_all x1, starting transfers between devices, per_device(): parts = lax.all_to_all(message, ('ply', 'tile'), 0, 0)  43.1 us
    ppermute x10, starting transfers between devices, trade_faces(): tile_odd = lax.ppermute(sends[2], 'tile', swap_pairs(ntile, 1))  38.5 us
    ppermute x10, starting transfers between devices, trade_faces(): tile_pair = lax.ppermute(sends[3], 'tile', swap_pairs(ntile, 0))  26.2 us
    all_to_all x1, waiting for transfers between devices, per_device(): parts = lax.all_to_all(message, ('ply', 'tile'), 0, 0)  11.9 us
    ppermute x10, waiting for transfers between devices, trade_faces(): ply_pair = lax.ppermute(sends[1], 'ply', swap_pairs(nply, 0))  7.4 us
    ppermute x10, starting transfers between devices, trade_faces(): ply_odd = lax.ppermute(sends[0], 'ply', swap_pairs(nply, 1))  6.65 us
  transfers between devices with their start and end apart: 41, of which 12 were waited for; matrix products, arithmetic and copies ran while one was open for 3% of the time, Pallas kernels for 0%

profile of v1, /device:TPU:1, one launch (start us, length us, event | category | flops | bytes accessed | tf_op | source)
XLA Modules:
  0.0 253.5 jit_solution(11905749375855315369)
XLA Ops:
  3.7 8.9 %collective-permute-start.2 = (f32[5,4,1,1024]{3,2,1,0:T(1,128)S(1)}, f32[5,4,1,1024]{3,2,1,0:T(1,128)S(1)}, u32[]{:S(2)}, u32[]{:S(2)}) collective-permute-start(f32[5,4,1,1024]{3,2,1,0:T(1,128)S(1)} %get-tuple-element.46), channel_id=1, source_target_pairs={{0,1},{1,0},{2,3},{3,2},{4,5},{5,4},{6,7},{7,6},{8,9},{9,8},{10,11... | collective-permute-start | bytes 245768 | tf_op jit(solution)/shard_map/ppermute | solution.py:45
  12.6 1.9 collective-permute-start.3
  14.6 1.9 collective-permute-start
  18.8 2.8 %collective-permute-done = f32[5,1,8,1024]{3,2,1,0:T(8,128)S(1)} collective-permute-done((f32[5,1,8,1024]{3,2,1,0:T(8,128)S(1)}, f32[5,1,8,1024]{3,2,1,0:T(8,128)S(1)}, u32[]{:S(2)}, u32[]{:S(2)}) %collective-permute-start) | collective-permute-done | bytes 163872 | tf_op jit(solution)/shard_map/ppermute | solution.py:43
  23.2 1.9 collective-permute-start.6
  25.2 3.8 %collective-permute-start.7 = (f32[1,4,1,1024]{3,2,1,0:T(1,128)S(1)}, f32[1,4,1,1024]{3,2,1,0:T(1,128)S(1)}, u32[]{:S(2)}, u32[]{:S(2)}) collective-permute-start(f32[1,4,1,1024]{3,2,1,0:T(1,128)S(1)} %get-tuple-element.51), channel_id=1, source_target_pairs={{1,2},{2,1},{3,4},{4,3},{5,6},{6,5},{7,8},{8,7},{9,10},{10,9},{11,... | collective-permute-start | bytes 49160 | tf_op jit(solution)/shard_map/ppermute | solution.py:44
  29.0 5.6 %collective-permute-start.4 = (f32[1,1,8,1024]{3,2,1,0:T(8,128)S(1)}, f32[1,1,8,1024]{3,2,1,0:T(8,128)S(1)}, u32[]{:S(2)}, u32[]{:S(2)}) collective-permute-start(f32[1,1,8,1024]{3,2,1,0:T(8,128)S(1)} %get-tuple-element.48), channel_id=1, source_target_pairs={{0,32},{32,0},{64,96},{96,64},{128,160},{160,128},{192,224},{224,1... | collective-permute-start | bytes 98312 | tf_op jit(solution)/shard_map/ppermute | solution.py:43
  36.3 1.9 collective-permute-start.10
  38.2 2.9 %collective-permute-start.11 = (f32[1,4,1,1024]{3,2,1,0:T(1,128)S(1)}, f32[1,4,1,1024]{3,2,1,0:T(1,128)S(1)}, u32[]{:S(2)}, u32[]{:S(2)}) collective-permute-start(f32[1,4,1,1024]{3,2,1,0:T(1,128)S(1)} %get-tuple-element.55), channel_id=1, source_target_pairs={{1,2},{2,1},{3,4},{4,3},{5,6},{6,5},{7,8},{8,7},{9,10},{10,9},{11,... | collective-permute-start | bytes 49160 | tf_op jit(solution)/shard_map/ppermute | solution.py:44
  41.2 5.4 %collective-permute-start.8 = (f32[1,1,8,1024]{3,2,1,0:T(8,128)S(1)}, f32[1,1,8,1024]{3,2,1,0:T(8,128)S(1)}, u32[]{:S(2)}, u32[]{:S(2)}) collective-permute-start(f32[1,1,8,1024]{3,2,1,0:T(8,128)S(1)} %get-tuple-element.52), channel_id=1, source_target_pairs={{0,32},{32,0},{64,96},{96,64},{128,160},{160,128},{192,224},{224,1... | collective-permute-start | bytes 98312 | tf_op jit(solution)/shard_map/ppermute | solution.py:43
  48.3 1.9 collective-permute-start.14
  50.2 4.1 %collective-permute-start.15 = (f32[1,4,1,1024]{3,2,1,0:T(1,128)S(1)}, f32[1,4,1,1024]{3,2,1,0:T(1,128)S(1)}, u32[]{:S(2)}, u32[]{:S(2)}) collective-permute-start(f32[1,4,1,1024]{3,2,1,0:T(1,128)S(1)} %get-tuple-element.59), channel_id=1, source_target_pairs={{1,2},{2,1},{3,4},{4,3},{5,6},{6,5},{7,8},{8,7},{9,10},{10,9},{11,... | collective-permute-start | bytes 49160 | tf_op jit(solution)/shard_map/ppermute | solution.py:44
  54.4 6.5 %collective-permute-start.12 = (f32[1,1,8,1024]{3,2,1,0:T(8,128)S(1)}, f32[1,1,8,1024]{3,2,1,0:T(8,128)S(1)}, u32[]{:S(2)}, u32[]{:S(2)}) collective-permute-start(f32[1,1,8,1024]{3,2,1,0:T(8,128)S(1)} %get-tuple-element.56), channel_id=1, source_target_pairs={{0,32},{32,0},{64,96},{96,64},{128,160},{160,128},{192,224},{224,1... | collective-permute-start | bytes 98312 | tf_op jit(solution)/shard_map/ppermute | solution.py:43
  64.5 3.1 %collective-permute-start.19 = (f32[1,4,1,1024]{3,2,1,0:T(1,128)S(1)}, f32[1,4,1,1024]{3,2,1,0:T(1,128)S(1)}, u32[]{:S(2)}, u32[]{:S(2)}) collective-permute-start(f32[1,4,1,1024]{3,2,1,0:T(1,128)S(1)} %get-tuple-element.63), channel_id=1, source_target_pairs={{1,2},{2,1},{3,4},{4,3},{5,6},{6,5},{7,8},{8,7},{9,10},{10,9},{11,... | collective-permute-start | bytes 49160 | tf_op jit(solution)/shard_map/ppermute | solution.py:44
  67.6 12.6 %collective-permute-start.16 = (f32[1,1,8,1024]{3,2,1,0:T(8,128)S(1)}, f32[1,1,8,1024]{3,2,1,0:T(8,128)S(1)}, u32[]{:S(2)}, u32[]{:S(2)}) collective-permute-start(f32[1,1,8,1024]{3,2,1,0:T(8,128)S(1)} %get-tuple-element.60), channel_id=1, source_target_pairs={{0,32},{32,0},{64,96},{96,64},{128,160},{160,128},{192,224},{224,1... | collective-permute-start | bytes 98312 | tf_op jit(solution)/shard_map/ppermute | solution.py:43
  86.6 1.9 collective-permute-start.22
  88.6 5.3 %collective-permute-start.23 = (f32[4,4,1,1024]{3,2,1,0:T(1,128)S(1)}, f32[4,4,1,1024]{3,2,1,0:T(1,128)S(1)}, u32[]{:S(2)}, u32[]{:S(2)}) collective-permute-start(f32[4,4,1,1024]{3,2,1,0:T(1,128)S(1)} %broadcast_select_fusion.8), channel_id=1, source_target_pairs={{1,2},{2,1},{3,4},{4,3},{5,6},{6,5},{7,8},{8,7},{9,10},{10,9},{11,... | collective-permute-start | bytes 196616 | tf_op jit(solution)/shard_map/ppermute | solution.py:44
  94.7 11.7 %collective-permute-start.20 = (f32[4,1,8,1024]{3,2,1,0:T(8,128)S(1)}, f32[4,1,8,1024]{3,2,1,0:T(8,128)S(1)}, u32[]{:S(2)}, u32[]{:S(2)}) collective-permute-start(f32[4,1,8,1024]{3,2,1,0:T(8,128)S(1)} %get-tuple-element.64), channel_id=1, source_target_pairs={{0,32},{32,0},{64,96},{96,64},{128,160},{160,128},{192,224},{224,1... | collective-permute-start | bytes 393224 | tf_op jit(solution)/shard_map/ppermute | solution.py:43
  110.6 1.9 collective-permute-start.26
  112.5 4.0 %collective-permute-start.27 = (f32[1,4,1,1024]{3,2,1,0:T(1,128)S(1)}, f32[1,4,1,1024]{3,2,1,0:T(1,128)S(1)}, u32[]{:S(2)}, u32[]{:S(2)}) collective-permute-start(f32[1,4,1,1024]{3,2,1,0:T(1,128)S(1)} %get-tuple-element.71), channel_id=1, source_target_pairs={{1,2},{2,1},{3,4},{4,3},{5,6},{6,5},{7,8},{8,7},{9,10},{10,9},{11,... | collective-permute-start | bytes 49160 | tf_op jit(solution)/shard_map/ppermute | solution.py:44
  116.6 12.2 %collective-permute-start.24 = (f32[1,1,8,1024]{3,2,1,0:T(8,128)S(1)}, f32[1,1,8,1024]{3,2,1,0:T(8,128)S(1)}, u32[]{:S(2)}, u32[]{:S(2)}) collective-permute-start(f32[1,1,8,1024]{3,2,1,0:T(8,128)S(1)} %get-tuple-element.68), channel_id=1, source_target_pairs={{0,32},{32,0},{64,96},{96,64},{128,160},{160,128},{192,224},{224,1... | collective-permute-start | bytes 98312 | tf_op jit(solution)/shard_map/ppermute | solution.py:43
  130.4 1.9 collective-permute-start.30
  132.4 4.5 %collective-permute-start.31 = (f32[1,4,1,1024]{3,2,1,0:T(1,128)S(1)}, f32[1,4,1,1024]{3,2,1,0:T(1,128)S(1)}, u32[]{:S(2)}, u32[]{:S(2)}) collective-permute-start(f32[1,4,1,1024]{3,2,1,0:T(1,128)S(1)} %get-tuple-element.75), channel_id=1, source_target_pairs={{1,2},{2,1},{3,4},{4,3},{5,6},{6,5},{7,8},{8,7},{9,10},{10,9},{11,... | collective-permute-start | bytes 49160 | tf_op jit(solution)/shard_map/ppermute | solution.py:44
  136.9 11.6 %collective-permute-start.28 = (f32[1,1,8,1024]{3,2,1,0:T(8,128)S(1)}, f32[1,1,8,1024]{3,2,1,0:T(8,128)S(1)}, u32[]{:S(2)}, u32[]{:S(2)}) collective-permute-start(f32[1,1,8,1024]{3,2,1,0:T(8,128)S(1)} %get-tuple-element.72), channel_id=1, source_target_pairs={{0,32},{32,0},{64,96},{96,64},{128,160},{160,128},{192,224},{224,1... | collective-permute-start | bytes 98312 | tf_op jit(solution)/shard_map/ppermute | solution.py:43
  152.2 4.3 %collective-permute-start.35 = (f32[1,4,1,1024]{3,2,1,0:T(1,128)S(1)}, f32[1,4,1,1024]{3,2,1,0:T(1,128)S(1)}, u32[]{:S(2)}, u32[]{:S(2)}) collective-permute-start(f32[1,4,1,1024]{3,2,1,0:T(1,128)S(1)} %get-tuple-element.79), channel_id=1, source_target_pairs={{1,2},{2,1},{3,4},{4,3},{5,6},{6,5},{7,8},{8,7},{9,10},{10,9},{11,... | collective-permute-start | bytes 49160 | tf_op jit(solution)/shard_map/ppermute | solution.py:44
  156.5 11.3 %collective-permute-start.32 = (f32[1,1,8,1024]{3,2,1,0:T(8,128)S(1)}, f32[1,1,8,1024]{3,2,1,0:T(8,128)S(1)}, u32[]{:S(2)}, u32[]{:S(2)}) collective-permute-start(f32[1,1,8,1024]{3,2,1,0:T(8,128)S(1)} %get-tuple-element.76), channel_id=1, source_target_pairs={{0,32},{32,0},{64,96},{96,64},{128,160},{160,128},{192,224},{224,1... | collective-permute-start | bytes 98312 | tf_op jit(solution)/shard_map/ppermute | solution.py:43
  169.5 1.9 collective-permute-start.38
  171.4 4.5 %collective-permute-start.39 = (f32[1,4,1,1024]{3,2,1,0:T(1,128)S(1)}, f32[1,4,1,1024]{3,2,1,0:T(1,128)S(1)}, u32[]{:S(2)}, u32[]{:S(2)}) collective-permute-start(f32[1,4,1,1024]{3,2,1,0:T(1,128)S(1)} %get-tuple-element.83), channel_id=1, source_target_pairs={{1,2},{2,1},{3,4},{4,3},{5,6},{6,5},{7,8},{8,7},{9,10},{10,9},{11,... | collective-permute-start | bytes 49160 | tf_op jit(solution)/shard_map/ppermute | solution.py:44
  176.0 12.6 %collective-permute-start.36 = (f32[1,1,8,1024]{3,2,1,0:T(8,128)S(1)}, f32[1,1,8,1024]{3,2,1,0:T(8,128)S(1)}, u32[]{:S(2)}, u32[]{:S(2)}) collective-permute-start(f32[1,1,8,1024]{3,2,1,0:T(8,128)S(1)} %get-tuple-element.80), channel_id=1, source_target_pairs={{0,32},{32,0},{64,96},{96,64},{128,160},{160,128},{192,224},{224,1... | collective-permute-start | bytes 98312 | tf_op jit(solution)/shard_map/ppermute | solution.py:43
  192.8 43.1 %all-to-all-start = ((f32[512,1,128]{2,1,0:T(1,128)}), f32[512,1,128]{2,1,0:T(1,128)S(1)}, u32[]{:S(2)}, u32[]{:S(2)}) async-start(f32[512,1,128]{2,1,0:T(1,128)} %broadcast_select_fusion), calls=%async_computation | async-start | bytes 524288 | tf_op jit(solution)/shard_map/all_to_all | solution.py:193
  236.7 2.5 fusion.90
  241.0 11.9 %all-to-all-done = f32[512,1,128]{2,1,0:T(1,128)S(1)} async-done(((f32[512,1,128]{2,1,0:T(1,128)}), f32[512,1,128]{2,1,0:T(1,128)S(1)}, u32[]{:S(2)}, u32[]{:S(2)}) %all-to-all-start) | async-done | bytes 262176 | tf_op jit(solution)/shard_map/all_to_all | solution.py:193
  (203 shorter events, 39.1 us)
Async XLA Ops:
  3.7 14.1 %collective-permute-start.2 = (f32[5,4,1,1024]{3,2,1,0:T(1,128)S(1)}, f32[5,4,1,1024]{3,2,1,0:T(1,128)S(1)}, u32[]{:S(2)}, u32[]{:S(2)}) collective-permute-start(f32[5,4,1,1024]{3,2,1,0:T(1,128)S(1)} %get-tuple-element.46), channel_id=1, source_target_pairs={{0,1},{1,0},{2,3},{3,2},{4,5},{5,4},{6,7},{7,6},{8,9},{9,8},{10,11... | collective-permute-start | bytes 245768 | tf_op jit(solution)/shard_map/ppermute | solution.py:45
  12.6 6.1 %collective-permute-start.3 = (f32[5,4,1,1024]{3,2,1,0:T(1,128)S(1)}, f32[5,4,1,1024]{3,2,1,0:T(1,128)S(1)}, u32[]{:S(2)}, u32[]{:S(2)}) collective-permute-start(f32[5,4,1,1024]{3,2,1,0:T(1,128)S(1)} %get-tuple-element.47), channel_id=1, source_target_pairs={{1,2},{2,1},{3,4},{4,3},{5,6},{6,5},{7,8},{8,7},{9,10},{10,9},{11,... | collective-permute-start | bytes 245768 | tf_op jit(solution)/shard_map/ppermute | solution.py:44
  14.6 7.0 %collective-permute-start = (f32[5,1,8,1024]{3,2,1,0:T(8,128)S(1)}, f32[5,1,8,1024]{3,2,1,0:T(8,128)S(1)}, u32[]{:S(2)}, u32[]{:S(2)}) collective-permute-start(f32[5,1,8,1024]{3,2,1,0:T(8,128)S(1)} %get-tuple-element.44), channel_id=1, source_target_pairs={{0,32},{32,0},{64,96},{96,64},{128,160},{160,128},{192,224},{224,1... | collective-permute-start | bytes 491528 | tf_op jit(solution)/shard_map/ppermute | solution.py:43
  16.5 5.1 %collective-permute-start.1 = (f32[5,1,8,1024]{3,2,1,0:T(8,128)S(1)}, f32[5,1,8,1024]{3,2,1,0:T(8,128)S(1)}, u32[]{:S(2)}, u32[]{:S(2)}) collective-permute-start(f32[5,1,8,1024]{3,2,1,0:T(8,128)S(1)} %get-tuple-element.45), channel_id=1, source_target_pairs={{32,64},{64,32},{96,128},{128,96},{160,192},{192,160},{224,256},{2... | collective-permute-start | bytes 491528 | tf_op jit(solution)/shard_map/ppermute | solution.py:42
  23.2 12.0 %collective-permute-start.6 = (f32[1,4,1,1024]{3,2,1,0:T(1,128)S(1)}, f32[1,4,1,1024]{3,2,1,0:T(1,128)S(1)}, u32[]{:S(2)}, u32[]{:S(2)}) collective-permute-start(f32[1,4,1,1024]{3,2,1,0:T(1,128)S(1)} %get-tuple-element.50), channel_id=1, source_target_pairs={{0,1},{1,0},{2,3},{3,2},{4,5},{5,4},{6,7},{7,6},{8,9},{9,8},{10,11... | collective-permute-start | bytes 49160 | tf_op jit(solution)/shard_map/ppermute | solution.py:45
  25.2 10.1 %collective-permute-start.7 = (f32[1,4,1,1024]{3,2,1,0:T(1,128)S(1)}, f32[1,4,1,1024]{3,2,1,0:T(1,128)S(1)}, u32[]{:S(2)}, u32[]{:S(2)}) collective-permute-start(f32[1,4,1,1024]{3,2,1,0:T(1,128)S(1)} %get-tuple-element.51), channel_id=1, source_target_pairs={{1,2},{2,1},{3,4},{4,3},{5,6},{6,5},{7,8},{8,7},{9,10},{10,9},{11,... | collective-permute-start | bytes 49160 | tf_op jit(solution)/shard_map/ppermute | solution.py:44
  29.0 6.9 %collective-permute-start.4 = (f32[1,1,8,1024]{3,2,1,0:T(8,128)S(1)}, f32[1,1,8,1024]{3,2,1,0:T(8,128)S(1)}, u32[]{:S(2)}, u32[]{:S(2)}) collective-permute-start(f32[1,1,8,1024]{3,2,1,0:T(8,128)S(1)} %get-tuple-element.48), channel_id=1, source_target_pairs={{0,32},{32,0},{64,96},{96,64},{128,160},{160,128},{192,224},{224,1... | collective-permute-start | bytes 98312 | tf_op jit(solution)/shard_map/ppermute | solution.py:43
  36.3 11.0 %collective-permute-start.10 = (f32[1,4,1,1024]{3,2,1,0:T(1,128)S(1)}, f32[1,4,1,1024]{3,2,1,0:T(1,128)S(1)}, u32[]{:S(2)}, u32[]{:S(2)}) collective-permute-start(f32[1,4,1,1024]{3,2,1,0:T(1,128)S(1)} %get-tuple-element.54), channel_id=1, source_target_pairs={{0,1},{1,0},{2,3},{3,2},{4,5},{5,4},{6,7},{7,6},{8,9},{9,8},{10,11... | collective-permute-start | bytes 49160 | tf_op jit(solution)/shard_map/ppermute | solution.py:45
  38.2 9.1 %collective-permute-start.11 = (f32[1,4,1,1024]{3,2,1,0:T(1,128)S(1)}, f32[1,4,1,1024]{3,2,1,0:T(1,128)S(1)}, u32[]{:S(2)}, u32[]{:S(2)}) collective-permute-start(f32[1,4,1,1024]{3,2,1,0:T(1,128)S(1)} %get-tuple-element.55), channel_id=1, source_target_pairs={{1,2},{2,1},{3,4},{4,3},{5,6},{6,5},{7,8},{8,7},{9,10},{10,9},{11,... | collective-permute-start | bytes 49160 | tf_op jit(solution)/shard_map/ppermute | solution.py:44
  41.2 6.7 %collective-permute-start.8 = (f32[1,1,8,1024]{3,2,1,0:T(8,128)S(1)}, f32[1,1,8,1024]{3,2,1,0:T(8,128)S(1)}, u32[]{:S(2)}, u32[]{:S(2)}) collective-permute-start(f32[1,1,8,1024]{3,2,1,0:T(8,128)S(1)} %get-tuple-element.52), channel_id=1, source_target_pairs={{0,32},{32,0},{64,96},{96,64},{128,160},{160,128},{192,224},{224,1... | collective-permute-start | bytes 98312 | tf_op jit(solution)/shard_map/ppermute | solution.py:43
  48.3 13.3 %collective-permute-start.14 = (f32[1,4,1,1024]{3,2,1,0:T(1,128)S(1)}, f32[1,4,1,1024]{3,2,1,0:T(1,128)S(1)}, u32[]{:S(2)}, u32[]{:S(2)}) collective-permute-start(f32[1,4,1,1024]{3,2,1,0:T(1,128)S(1)} %get-tuple-element.58), channel_id=1, source_target_pairs={{0,1},{1,0},{2,3},{3,2},{4,5},{5,4},{6,7},{7,6},{8,9},{9,8},{10,11... | collective-permute-start | bytes 49160 | tf_op jit(solution)/shard_map/ppermute | solution.py:45
  50.2 11.3 %collective-permute-start.15 = (f32[1,4,1,1024]{3,2,1,0:T(1,128)S(1)}, f32[1,4,1,1024]{3,2,1,0:T(1,128)S(1)}, u32[]{:S(2)}, u32[]{:S(2)}) collective-permute-start(f32[1,4,1,1024]{3,2,1,0:T(1,128)S(1)} %get-tuple-element.59), channel_id=1, source_target_pairs={{1,2},{2,1},{3,4},{4,3},{5,6},{6,5},{7,8},{8,7},{9,10},{10,9},{11,... | collective-permute-start | bytes 49160 | tf_op jit(solution)/shard_map/ppermute | solution.py:44
  54.4 7.8 %collective-permute-start.12 = (f32[1,1,8,1024]{3,2,1,0:T(8,128)S(1)}, f32[1,1,8,1024]{3,2,1,0:T(8,128)S(1)}, u32[]{:S(2)}, u32[]{:S(2)}) collective-permute-start(f32[1,1,8,1024]{3,2,1,0:T(8,128)S(1)} %get-tuple-element.56), channel_id=1, source_target_pairs={{0,32},{32,0},{64,96},{96,64},{128,160},{160,128},{192,224},{224,1... | collective-permute-start | bytes 98312 | tf_op jit(solution)/shard_map/ppermute | solution.py:43
  62.6 18.3 %collective-permute-start.18 = (f32[1,4,1,1024]{3,2,1,0:T(1,128)S(1)}, f32[1,4,1,1024]{3,2,1,0:T(1,128)S(1)}, u32[]{:S(2)}, u32[]{:S(2)}) collective-permute-start(f32[1,4,1,1024]{3,2,1,0:T(1,128)S(1)} %get-tuple-element.62), channel_id=1, source_target_pairs={{0,1},{1,0},{2,3},{3,2},{4,5},{5,4},{6,7},{7,6},{8,9},{9,8},{10,11... | collective-permute-start | bytes 49160 | tf_op jit(solution)/shard_map/ppermute | solution.py:45
  64.5 16.4 %collective-permute-start.19 = (f32[1,4,1,1024]{3,2,1,0:T(1,128)S(1)}, f32[1,4,1,1024]{3,2,1,0:T(1,128)S(1)}, u32[]{:S(2)}, u32[]{:S(2)}) collective-permute-start(f32[1,4,1,1024]{3,2,1,0:T(1,128)S(1)} %get-tuple-element.63), channel_id=1, source_target_pairs={{1,2},{2,1},{3,4},{4,3},{5,6},{6,5},{7,8},{8,7},{9,10},{10,9},{11,... | collective-permute-start | bytes 49160 | tf_op jit(solution)/shard_map/ppermute | solution.py:44
  67.6 13.9 %collective-permute-start.16 = (f32[1,1,8,1024]{3,2,1,0:T(8,128)S(1)}, f32[1,1,8,1024]{3,2,1,0:T(8,128)S(1)}, u32[]{:S(2)}, u32[]{:S(2)}) collective-permute-start(f32[1,1,8,1024]{3,2,1,0:T(8,128)S(1)} %get-tuple-element.60), channel_id=1, source_target_pairs={{0,32},{32,0},{64,96},{96,64},{128,160},{160,128},{192,224},{224,1... | collective-permute-start | bytes 98312 | tf_op jit(solution)/shard_map/ppermute | solution.py:43
  86.6 20.4 %collective-permute-start.22 = (f32[4,4,1,1024]{3,2,1,0:T(1,128)S(1)}, f32[4,4,1,1024]{3,2,1,0:T(1,128)S(1)}, u32[]{:S(2)}, u32[]{:S(2)}) collective-permute-start(f32[4,4,1,1024]{3,2,1,0:T(1,128)S(1)} %get-tuple-element.66), channel_id=1, source_target_pairs={{0,1},{1,0},{2,3},{3,2},{4,5},{5,4},{6,7},{7,6},{8,9},{9,8},{10,11... | collective-permute-start | bytes 196616 | tf_op jit(solution)/shard_map/ppermute | solution.py:45
  88.6 18.5 %collective-permute-start.23 = (f32[4,4,1,1024]{3,2,1,0:T(1,128)S(1)}, f32[4,4,1,1024]{3,2,1,0:T(1,128)S(1)}, u32[]{:S(2)}, u32[]{:S(2)}) collective-permute-start(f32[4,4,1,1024]{3,2,1,0:T(1,128)S(1)} %broadcast_select_fusion.8), channel_id=1, source_target_pairs={{1,2},{2,1},{3,4},{4,3},{5,6},{6,5},{7,8},{8,7},{9,10},{10,9},{11,... | collective-permute-start | bytes 196616 | tf_op jit(solution)/shard_map/ppermute | solution.py:44
  94.7 14.0 %collective-permute-start.20 = (f32[4,1,8,1024]{3,2,1,0:T(8,128)S(1)}, f32[4,1,8,1024]{3,2,1,0:T(8,128)S(1)}, u32[]{:S(2)}, u32[]{:S(2)}) collective-permute-start(f32[4,1,8,1024]{3,2,1,0:T(8,128)S(1)} %get-tuple-element.64), channel_id=1, source_target_pairs={{0,32},{32,0},{64,96},{96,64},{128,160},{160,128},{192,224},{224,1... | collective-permute-start | bytes 393224 | tf_op jit(solution)/shard_map/ppermute | solution.py:43
  110.6 18.8 %collective-permute-start.26 = (f32[1,4,1,1024]{3,2,1,0:T(1,128)S(1)}, f32[1,4,1,1024]{3,2,1,0:T(1,128)S(1)}, u32[]{:S(2)}, u32[]{:S(2)}) collective-permute-start(f32[1,4,1,1024]{3,2,1,0:T(1,128)S(1)} %get-tuple-element.70), channel_id=1, source_target_pairs={{0,1},{1,0},{2,3},{3,2},{4,5},{5,4},{6,7},{7,6},{8,9},{9,8},{10,11... | collective-permute-start | bytes 49160 | tf_op jit(solution)/shard_map/ppermute | solution.py:45
  112.5 16.9 %collective-permute-start.27 = (f32[1,4,1,1024]{3,2,1,0:T(1,128)S(1)}, f32[1,4,1,1024]{3,2,1,0:T(1,128)S(1)}, u32[]{:S(2)}, u32[]{:S(2)}) collective-permute-start(f32[1,4,1,1024]{3,2,1,0:T(1,128)S(1)} %get-tuple-element.71), channel_id=1, source_target_pairs={{1,2},{2,1},{3,4},{4,3},{5,6},{6,5},{7,8},{8,7},{9,10},{10,9},{11,... | collective-permute-start | bytes 49160 | tf_op jit(solution)/shard_map/ppermute | solution.py:44
  116.6 13.5 %collective-permute-start.24 = (f32[1,1,8,1024]{3,2,1,0:T(8,128)S(1)}, f32[1,1,8,1024]{3,2,1,0:T(8,128)S(1)}, u32[]{:S(2)}, u32[]{:S(2)}) collective-permute-start(f32[1,1,8,1024]{3,2,1,0:T(8,128)S(1)} %get-tuple-element.68), channel_id=1, source_target_pairs={{0,32},{32,0},{64,96},{96,64},{128,160},{160,128},{192,224},{224,1... | collective-permute-start | bytes 98312 | tf_op jit(solution)/shard_map/ppermute | solution.py:43
  130.4 18.8 %collective-permute-start.30 = (f32[1,4,1,1024]{3,2,1,0:T(1,128)S(1)}, f32[1,4,1,1024]{3,2,1,0:T(1,128)S(1)}, u32[]{:S(2)}, u32[]{:S(2)}) collective-permute-start(f32[1,4,1,1024]{3,2,1,0:T(1,128)S(1)} %get-tuple-element.74), channel_id=1, source_target_pairs={{0,1},{1,0},{2,3},{3,2},{4,5},{5,4},{6,7},{7,6},{8,9},{9,8},{10,11... | collective-permute-start | bytes 49160 | tf_op jit(solution)/shard_map/ppermute | solution.py:45
  132.4 16.9 %collective-permute-start.31 = (f32[1,4,1,1024]{3,2,1,0:T(1,128)S(1)}, f32[1,4,1,1024]{3,2,1,0:T(1,128)S(1)}, u32[]{:S(2)}, u32[]{:S(2)}) collective-permute-start(f32[1,4,1,1024]{3,2,1,0:T(1,128)S(1)} %get-tuple-element.75), channel_id=1, source_target_pairs={{1,2},{2,1},{3,4},{4,3},{5,6},{6,5},{7,8},{8,7},{9,10},{10,9},{11,... | collective-permute-start | bytes 49160 | tf_op jit(solution)/shard_map/ppermute | solution.py:44
  136.9 12.9 %collective-permute-start.28 = (f32[1,1,8,1024]{3,2,1,0:T(8,128)S(1)}, f32[1,1,8,1024]{3,2,1,0:T(8,128)S(1)}, u32[]{:S(2)}, u32[]{:S(2)}) collective-permute-start(f32[1,1,8,1024]{3,2,1,0:T(8,128)S(1)} %get-tuple-element.72), channel_id=1, source_target_pairs={{0,32},{32,0},{64,96},{96,64},{128,160},{160,128},{192,224},{224,1... | collective-permute-start | bytes 98312 | tf_op jit(solution)/shard_map/ppermute | solution.py:43
  150.2 18.2 %collective-permute-start.34 = (f32[1,4,1,1024]{3,2,1,0:T(1,128)S(1)}, f32[1,4,1,1024]{3,2,1,0:T(1,128)S(1)}, u32[]{:S(2)}, u32[]{:S(2)}) collective-permute-start(f32[1,4,1,1024]{3,2,1,0:T(1,128)S(1)} %get-tuple-element.78), channel_id=1, source_target_pairs={{0,1},{1,0},{2,3},{3,2},{4,5},{5,4},{6,7},{7,6},{8,9},{9,8},{10,11... | collective-permute-start | bytes 49160 | tf_op jit(solution)/shard_map/ppermute | solution.py:45
  152.2 16.3 %collective-permute-start.35 = (f32[1,4,1,1024]{3,2,1,0:T(1,128)S(1)}, f32[1,4,1,1024]{3,2,1,0:T(1,128)S(1)}, u32[]{:S(2)}, u32[]{:S(2)}) collective-permute-start(f32[1,4,1,1024]{3,2,1,0:T(1,128)S(1)} %get-tuple-element.79), channel_id=1, source_target_pairs={{1,2},{2,1},{3,4},{4,3},{5,6},{6,5},{7,8},{8,7},{9,10},{10,9},{11,... | collective-permute-start | bytes 49160 | tf_op jit(solution)/shard_map/ppermute | solution.py:44
  156.5 12.6 %collective-permute-start.32 = (f32[1,1,8,1024]{3,2,1,0:T(8,128)S(1)}, f32[1,1,8,1024]{3,2,1,0:T(8,128)S(1)}, u32[]{:S(2)}, u32[]{:S(2)}) collective-permute-start(f32[1,1,8,1024]{3,2,1,0:T(8,128)S(1)} %get-tuple-element.76), channel_id=1, source_target_pairs={{0,32},{32,0},{64,96},{96,64},{128,160},{160,128},{192,224},{224,1... | collective-permute-start | bytes 98312 | tf_op jit(solution)/shard_map/ppermute | solution.py:43
  169.5 19.8 %collective-permute-start.38 = (f32[1,4,1,1024]{3,2,1,0:T(1,128)S(1)}, f32[1,4,1,1024]{3,2,1,0:T(1,128)S(1)}, u32[]{:S(2)}, u32[]{:S(2)}) collective-permute-start(f32[1,4,1,1024]{3,2,1,0:T(1,128)S(1)} %get-tuple-element.82), channel_id=1, source_target_pairs={{0,1},{1,0},{2,3},{3,2},{4,5},{5,4},{6,7},{7,6},{8,9},{9,8},{10,11... | collective-permute-start | bytes 49160 | tf_op jit(solution)/shard_map/ppermute | solution.py:45
  171.4 17.9 %collective-permute-start.39 = (f32[1,4,1,1024]{3,2,1,0:T(1,128)S(1)}, f32[1,4,1,1024]{3,2,1,0:T(1,128)S(1)}, u32[]{:S(2)}, u32[]{:S(2)}) collective-permute-start(f32[1,4,1,1024]{3,2,1,0:T(1,128)S(1)} %get-tuple-element.83), channel_id=1, source_target_pairs={{1,2},{2,1},{3,4},{4,3},{5,6},{6,5},{7,8},{8,7},{9,10},{10,9},{11,... | collective-permute-start | bytes 49160 | tf_op jit(solution)/shard_map/ppermute | solution.py:44
  176.0 13.9 %collective-permute-start.36 = (f32[1,1,8,1024]{3,2,1,0:T(8,128)S(1)}, f32[1,1,8,1024]{3,2,1,0:T(8,128)S(1)}, u32[]{:S(2)}, u32[]{:S(2)}) collective-permute-start(f32[1,1,8,1024]{3,2,1,0:T(8,128)S(1)} %get-tuple-element.80), channel_id=1, source_target_pairs={{0,32},{32,0},{64,96},{96,64},{128,160},{160,128},{192,224},{224,1... | collective-permute-start | bytes 98312 | tf_op jit(solution)/shard_map/ppermute | solution.py:43
  192.8 60.1 %all-to-all-start = ((f32[512,1,128]{2,1,0:T(1,128)}), f32[512,1,128]{2,1,0:T(1,128)S(1)}, u32[]{:S(2)}, u32[]{:S(2)}) async-start(f32[512,1,128]{2,1,0:T(1,128)} %broadcast_select_fusion), calls=%async_computation | async-start | bytes 524288 | tf_op jit(solution)/shard_map/all_to_all | solution.py:193
  (28 other events, 182.3 us)

commit v2 on v1

--- a/solution.py
+++ b/solution.py
@@ -61,6 +61,11 @@
         jnp.concatenate([array[:, :, 1:], edge], axis=2),
         jnp.concatenate([edge, array[:, :, :-1]], axis=2),
     ]
+
+
+def trade(*fields):
+    faces = trade_faces(jnp.stack(fields))
+    return [nearby_sites(field, [face[k] for face in faces]) for k, field in enumerate(fields)]
 
 
 def face_mobility(centre, nearby):
@@ -151,7 +156,7 @@
     dry_site = wetted_status * (1.0 - inlet_cell) * (1.0 - outlet_flags.astype(jnp.float32))
     devices = lax.axis_size("ply") * lax.axis_size("tile")
     site_total = scaled_warmth.size * devices
-    nearby_wetted = None
+    nearby_wetted = nearby_stress = None
     local_sums = []
     for _ in range(STEPS):
         fluid_conductance = preform_porosity_coefficient * jnp.exp(
@@ -160,21 +165,23 @@
                 + fluidity_gelation_coefficient * crosslink_fraction
             )
         )
-        fields = [fluid_stress, fluid_conductance, scaled_warmth, crosslink_fraction]
+        if nearby_stress is None:
+            nearby_mobility, nearby_stress = trade(fluid_conductance, fluid_stress)
+            riders = [scaled_warmth, crosslink_fraction, wetted_status]
+            arrived = []
+        else:
+            nearby_mobility, nearby_warmth = trade(fluid_conductance, scaled_warmth)
+            riders = [crosslink_fraction]
+            arrived = [nearby_warmth]
+        boundary_sides = face_mobility(fluid_conductance, nearby_mobility)
+        for sweep_index in range(SWEEPS):
+            fluid_stress = jacobi_sweep(nearby_stress, boundary_sides, dry_site, inlet_cell)
+            rider = riders[sweep_index : sweep_index + 1]
+            nearby_stress, *rest = trade(fluid_stress, *rider)
+            arrived += rest
+        nearby_warmth, nearby_crosslink = arrived[:2]
         if nearby_wetted is None:
-            fields.append(wetted_status)
-        faces = trade_faces(jnp.stack(fields))
-        nearby = [
-            nearby_sites(field, [face[k] for face in faces]) for k, field in enumerate(fields)
-        ]
-        nearby_stress, nearby_mobility, nearby_warmth, nearby_crosslink = nearby[:4]
-        if nearby_wetted is None:
-            nearby_wetted = nearby[4]
-        boundary_sides = face_mobility(fluid_conductance, nearby_mobility)
-        for _ in range(SWEEPS):
-            fluid_stress = jacobi_sweep(nearby_stress, boundary_sides, dry_site, inlet_cell)
-            faces = trade_faces(fluid_stress[None])
-            nearby_stress = nearby_sites(fluid_stress, [face[0] for face in faces])
+            nearby_wetted = arrived[2]
         darcy_imbalance, scaled_warmth, crosslink_fraction = donor_advection(
             fluid_stress,
             scaled_warmth,

time: 255 us -> 252 us (0.988)
  waiting for transfers between devices: 20.2 us -> 16.7 us
  local copies, waits for them, and re-layouts: 12.5 us -> 15.6 us
  starting transfers between devices: 206 us -> 203 us
    ppermute x10, waiting for transfers between devices: 7.4 us -> 4.67 us  [trade_faces(): ply_pair = lax.ppermute(sends[1], 'ply', swap_pairs(nply, 0))]
    unnamed x41 -> x38, local copies, waits for them, and re-layouts: 4.74 us -> 5.44 us
  transfers between devices with their start and end apart: 41 -> 41, of which waited for: 12 -> 8; matrix products, arithmetic and copies ran while one was open for 3% -> 3% of each run, Pallas kernels for 0% -> 0%
where the time goes in v2:
time: 252 us; the launch traced here: 250 us
  starting transfers between devices  203 us (81%)
  waiting for transfers between devices  16.7 us (7%)
  local copies, waits for them, and re-layouts  15.6 us (6%)
  other arithmetic  13.2 us (5%)
    ppermute x10, starting transfers between devices, trade_faces(): ply_pair = lax.ppermute(sends[1], 'ply', swap_pairs(nply, 0))  89.1 us
    all_to_all x1, starting transfers between devices, per_device(): parts = lax.all_to_all(message, ('ply', 'tile'), 0, 0)  42.4 us
    ppermute x10, starting transfers between devices, trade_faces(): tile_odd = lax.ppermute(sends[2], 'tile', swap_pairs(ntile, 1))  38.4 us
    ppermute x10, starting transfers between devices, trade_faces(): tile_pair = lax.ppermute(sends[3], 'tile', swap_pairs(ntile, 0))  26 us
    all_to_all x1, waiting for transfers between devices, per_device(): parts = lax.all_to_all(message, ('ply', 'tile'), 0, 0)  11.9 us
    ppermute x10, starting transfers between devices, trade_faces(): ply_odd = lax.ppermute(sends[0], 'ply', swap_pairs(nply, 1))  6.64 us
    unnamed x38, local copies, waits for them, and re-layouts  5.44 us
  transfers between devices with their start and end apart: 41, of which 8 were waited for; matrix products, arithmetic and copies ran while one was open for 3% of the time, Pallas kernels for 0%

profile of v2, /device:TPU:1, one launch (start us, length us, event | category | flops | bytes accessed | tf_op | source)
XLA Modules:
  0.0 250.2 jit_solution(7804273917349253142)
XLA Ops:
  1.9 8.7 %collective-permute-start.2 = (f32[2,4,1,1024]{3,2,1,0:T(1,128)S(1)}, f32[2,4,1,1024]{3,2,1,0:T(1,128)S(1)}, u32[]{:S(2)}, u32[]{:S(2)}) collective-permute-start(f32[2,4,1,1024]{3,2,1,0:T(1,128)S(1)} %get-tuple-element.46), channel_id=1, source_target_pairs={{0,1},{1,0},{2,3},{3,2},{4,5},{5,4},{6,7},{7,6},{8,9},{9,8},{10,11... | collective-permute-start | bytes 98312 | tf_op jit(solution)/shard_map/ppermute | solution.py:45
  10.7 1.9 collective-permute-start.3
  12.6 1.9 collective-permute-start
  20.3 1.9 collective-permute-start.6
  22.2 3.8 %collective-permute-start.7 = (f32[2,4,1,1024]{3,2,1,0:T(1,128)S(1)}, f32[2,4,1,1024]{3,2,1,0:T(1,128)S(1)}, u32[]{:S(2)}, u32[]{:S(2)}) collective-permute-start(f32[2,4,1,1024]{3,2,1,0:T(1,128)S(1)} %broadcast_select_fusion.20), channel_id=1, source_target_pairs={{1,2},{2,1},{3,4},{4,3},{5,6},{6,5},{7,8},{8,7},{9,10},{10,9},{11,... | collective-permute-start | bytes 98312 | tf_op jit(solution)/shard_map/ppermute | solution.py:44
  26.1 5.6 %collective-permute-start.4 = (f32[2,1,8,1024]{3,2,1,0:T(8,128)S(1)}, f32[2,1,8,1024]{3,2,1,0:T(8,128)S(1)}, u32[]{:S(2)}, u32[]{:S(2)}) collective-permute-start(f32[2,1,8,1024]{3,2,1,0:T(8,128)S(1)} %get-tuple-element.48), channel_id=1, source_target_pairs={{0,32},{32,0},{64,96},{96,64},{128,160},{160,128},{192,224},{224,1... | collective-permute-start | bytes 196616 | tf_op jit(solution)/shard_map/ppermute | solution.py:43
  33.8 1.9 collective-permute-start.10
  35.7 3.3 %collective-permute-start.11 = (f32[2,4,1,1024]{3,2,1,0:T(1,128)S(1)}, f32[2,4,1,1024]{3,2,1,0:T(1,128)S(1)}, u32[]{:S(2)}, u32[]{:S(2)}) collective-permute-start(f32[2,4,1,1024]{3,2,1,0:T(1,128)S(1)} %broadcast_select_fusion.16), channel_id=1, source_target_pairs={{1,2},{2,1},{3,4},{4,3},{5,6},{6,5},{7,8},{8,7},{9,10},{10,9},{11,... | collective-permute-start | bytes 98312 | tf_op jit(solution)/shard_map/ppermute | solution.py:44
  39.1 5.3 %collective-permute-start.8 = (f32[2,1,8,1024]{3,2,1,0:T(8,128)S(1)}, f32[2,1,8,1024]{3,2,1,0:T(8,128)S(1)}, u32[]{:S(2)}, u32[]{:S(2)}) collective-permute-start(f32[2,1,8,1024]{3,2,1,0:T(8,128)S(1)} %get-tuple-element.52), channel_id=1, source_target_pairs={{0,32},{32,0},{64,96},{96,64},{128,160},{160,128},{192,224},{224,1... | collective-permute-start | bytes 196616 | tf_op jit(solution)/shard_map/ppermute | solution.py:43
  46.5 1.9 collective-permute-start.14
  48.4 3.9 %collective-permute-start.15 = (f32[2,4,1,1024]{3,2,1,0:T(1,128)S(1)}, f32[2,4,1,1024]{3,2,1,0:T(1,128)S(1)}, u32[]{:S(2)}, u32[]{:S(2)}) collective-permute-start(f32[2,4,1,1024]{3,2,1,0:T(1,128)S(1)} %broadcast_select_fusion.12), channel_id=1, source_target_pairs={{1,2},{2,1},{3,4},{4,3},{5,6},{6,5},{7,8},{8,7},{9,10},{10,9},{11,... | collective-permute-start | bytes 98312 | tf_op jit(solution)/shard_map/ppermute | solution.py:44
  52.4 7.6 %collective-permute-start.12 = (f32[2,1,8,1024]{3,2,1,0:T(8,128)S(1)}, f32[2,1,8,1024]{3,2,1,0:T(8,128)S(1)}, u32[]{:S(2)}, u32[]{:S(2)}) collective-permute-start(f32[2,1,8,1024]{3,2,1,0:T(8,128)S(1)} %get-tuple-element.56), channel_id=1, source_target_pairs={{0,32},{32,0},{64,96},{96,64},{128,160},{160,128},{192,224},{224,1... | collective-permute-start | bytes 196616 | tf_op jit(solution)/shard_map/ppermute | solution.py:43
  62.1 1.9 collective-permute-start.18
  64.0 3.3 %collective-permute-start.19 = (f32[1,4,1,1024]{3,2,1,0:T(1,128)S(1)}, f32[1,4,1,1024]{3,2,1,0:T(1,128)S(1)}, u32[]{:S(2)}, u32[]{:S(2)}) collective-permute-start(f32[1,4,1,1024]{3,2,1,0:T(1,128)S(1)} %get-tuple-element.63), channel_id=1, source_target_pairs={{1,2},{2,1},{3,4},{4,3},{5,6},{6,5},{7,8},{8,7},{9,10},{10,9},{11,... | collective-permute-start | bytes 49160 | tf_op jit(solution)/shard_map/ppermute | solution.py:44
  67.3 9.8 %collective-permute-start.16 = (f32[1,1,8,1024]{3,2,1,0:T(8,128)S(1)}, f32[1,1,8,1024]{3,2,1,0:T(8,128)S(1)}, u32[]{:S(2)}, u32[]{:S(2)}) collective-permute-start(f32[1,1,8,1024]{3,2,1,0:T(8,128)S(1)} %get-tuple-element.60), channel_id=1, source_target_pairs={{0,32},{32,0},{64,96},{96,64},{128,160},{160,128},{192,224},{224,1... | collective-permute-start | bytes 98312 | tf_op jit(solution)/shard_map/ppermute | solution.py:43
  83.4 1.9 collective-permute-start.22
  85.4 4.0 %collective-permute-start.23 = (f32[2,4,1,1024]{3,2,1,0:T(1,128)S(1)}, f32[2,4,1,1024]{3,2,1,0:T(1,128)S(1)}, u32[]{:S(2)}, u32[]{:S(2)}) collective-permute-start(f32[2,4,1,1024]{3,2,1,0:T(1,128)S(1)} %broadcast_select_fusion.8), channel_id=1, source_target_pairs={{1,2},{2,1},{3,4},{4,3},{5,6},{6,5},{7,8},{8,7},{9,10},{10,9},{11,... | collective-permute-start | bytes 98312 | tf_op jit(solution)/shard_map/ppermute | solution.py:44
  90.2 12.5 %collective-permute-start.20 = (f32[2,1,8,1024]{3,2,1,0:T(8,128)S(1)}, f32[2,1,8,1024]{3,2,1,0:T(8,128)S(1)}, u32[]{:S(2)}, u32[]{:S(2)}) collective-permute-start(f32[2,1,8,1024]{3,2,1,0:T(8,128)S(1)} %get-tuple-element.64), channel_id=1, source_target_pairs={{0,32},{32,0},{64,96},{96,64},{128,160},{160,128},{192,224},{224,1... | collective-permute-start | bytes 196616 | tf_op jit(solution)/shard_map/ppermute | solution.py:43
  106.5 1.9 collective-permute-start.26
  108.5 3.7 %collective-permute-start.27 = (f32[2,4,1,1024]{3,2,1,0:T(1,128)S(1)}, f32[2,4,1,1024]{3,2,1,0:T(1,128)S(1)}, u32[]{:S(2)}, u32[]{:S(2)}) collective-permute-start(f32[2,4,1,1024]{3,2,1,0:T(1,128)S(1)} %broadcast_select_fusion.4), channel_id=1, source_target_pairs={{1,2},{2,1},{3,4},{4,3},{5,6},{6,5},{7,8},{8,7},{9,10},{10,9},{11,... | collective-permute-start | bytes 98312 | tf_op jit(solution)/shard_map/ppermute | solution.py:44
  112.2 12.1 %collective-permute-start.24 = (f32[2,1,8,1024]{3,2,1,0:T(8,128)S(1)}, f32[2,1,8,1024]{3,2,1,0:T(8,128)S(1)}, u32[]{:S(2)}, u32[]{:S(2)}) collective-permute-start(f32[2,1,8,1024]{3,2,1,0:T(8,128)S(1)} %get-tuple-element.68), channel_id=1, source_target_pairs={{0,32},{32,0},{64,96},{96,64},{128,160},{160,128},{192,224},{224,1... | collective-permute-start | bytes 196616 | tf_op jit(solution)/shard_map/ppermute | solution.py:43
  127.9 1.9 collective-permute-start.30
  129.8 5.7 %collective-permute-start.31 = (f32[1,4,1,1024]{3,2,1,0:T(1,128)S(1)}, f32[1,4,1,1024]{3,2,1,0:T(1,128)S(1)}, u32[]{:S(2)}, u32[]{:S(2)}) collective-permute-start(f32[1,4,1,1024]{3,2,1,0:T(1,128)S(1)} %get-tuple-element.75), channel_id=1, source_target_pairs={{1,2},{2,1},{3,4},{4,3},{5,6},{6,5},{7,8},{8,7},{9,10},{10,9},{11,... | collective-permute-start | bytes 49160 | tf_op jit(solution)/shard_map/ppermute | solution.py:44
  135.6 11.0 %collective-permute-start.28 = (f32[1,1,8,1024]{3,2,1,0:T(8,128)S(1)}, f32[1,1,8,1024]{3,2,1,0:T(8,128)S(1)}, u32[]{:S(2)}, u32[]{:S(2)}) collective-permute-start(f32[1,1,8,1024]{3,2,1,0:T(8,128)S(1)} %get-tuple-element.72), channel_id=1, source_target_pairs={{0,32},{32,0},{64,96},{96,64},{128,160},{160,128},{192,224},{224,1... | collective-permute-start | bytes 98312 | tf_op jit(solution)/shard_map/ppermute | solution.py:43
  148.2 1.9 collective-permute-start.34
  150.2 4.4 %collective-permute-start.35 = (f32[1,4,1,1024]{3,2,1,0:T(1,128)S(1)}, f32[1,4,1,1024]{3,2,1,0:T(1,128)S(1)}, u32[]{:S(2)}, u32[]{:S(2)}) collective-permute-start(f32[1,4,1,1024]{3,2,1,0:T(1,128)S(1)} %get-tuple-element.79), channel_id=1, source_target_pairs={{1,2},{2,1},{3,4},{4,3},{5,6},{6,5},{7,8},{8,7},{9,10},{10,9},{11,... | collective-permute-start | bytes 49160 | tf_op jit(solution)/shard_map/ppermute | solution.py:44
  154.6 11.5 %collective-permute-start.32 = (f32[1,1,8,1024]{3,2,1,0:T(8,128)S(1)}, f32[1,1,8,1024]{3,2,1,0:T(8,128)S(1)}, u32[]{:S(2)}, u32[]{:S(2)}) collective-permute-start(f32[1,1,8,1024]{3,2,1,0:T(8,128)S(1)} %get-tuple-element.76), channel_id=1, source_target_pairs={{0,32},{32,0},{64,96},{96,64},{128,160},{160,128},{192,224},{224,1... | collective-permute-start | bytes 98312 | tf_op jit(solution)/shard_map/ppermute | solution.py:43
  169.7 4.4 %collective-permute-start.39 = (f32[1,4,1,1024]{3,2,1,0:T(1,128)S(1)}, f32[1,4,1,1024]{3,2,1,0:T(1,128)S(1)}, u32[]{:S(2)}, u32[]{:S(2)}) collective-permute-start(f32[1,4,1,1024]{3,2,1,0:T(1,128)S(1)} %get-tuple-element.83), channel_id=1, source_target_pairs={{1,2},{2,1},{3,4},{4,3},{5,6},{6,5},{7,8},{8,7},{9,10},{10,9},{11,... | collective-permute-start | bytes 49160 | tf_op jit(solution)/shard_map/ppermute | solution.py:44
  174.2 11.8 %collective-permute-start.36 = (f32[1,1,8,1024]{3,2,1,0:T(8,128)S(1)}, f32[1,1,8,1024]{3,2,1,0:T(8,128)S(1)}, u32[]{:S(2)}, u32[]{:S(2)}) collective-permute-start(f32[1,1,8,1024]{3,2,1,0:T(8,128)S(1)} %get-tuple-element.80), channel_id=1, source_target_pairs={{0,32},{32,0},{64,96},{96,64},{128,160},{160,128},{192,224},{224,1... | collective-permute-start | bytes 98312 | tf_op jit(solution)/shard_map/ppermute | solution.py:43
  190.2 42.4 %all-to-all-start = ((f32[512,1,128]{2,1,0:T(1,128)}), f32[512,1,128]{2,1,0:T(1,128)S(1)}, u32[]{:S(2)}, u32[]{:S(2)}) async-start(f32[512,1,128]{2,1,0:T(1,128)} %broadcast_select_fusion), calls=%async_computation | async-start | bytes 524288 | tf_op jit(solution)/shard_map/all_to_all | solution.py:200
  233.4 2.5 fusion.81
  237.7 11.9 %all-to-all-done = f32[512,1,128]{2,1,0:T(1,128)S(1)} async-done(((f32[512,1,128]{2,1,0:T(1,128)}), f32[512,1,128]{2,1,0:T(1,128)S(1)}, u32[]{:S(2)}, u32[]{:S(2)}) %all-to-all-start) | async-done | bytes 262176 | tf_op jit(solution)/shard_map/all_to_all | solution.py:200
  (219 shorter events, 39.7 us)
Async XLA Ops:
  1.9 16.5 %collective-permute-start.2 = (f32[2,4,1,1024]{3,2,1,0:T(1,128)S(1)}, f32[2,4,1,1024]{3,2,1,0:T(1,128)S(1)}, u32[]{:S(2)}, u32[]{:S(2)}) collective-permute-start(f32[2,4,1,1024]{3,2,1,0:T(1,128)S(1)} %get-tuple-element.46), channel_id=1, source_target_pairs={{0,1},{1,0},{2,3},{3,2},{4,5},{5,4},{6,7},{7,6},{8,9},{9,8},{10,11... | collective-permute-start | bytes 98312 | tf_op jit(solution)/shard_map/ppermute | solution.py:45
  10.7 7.8 %collective-permute-start.3 = (f32[2,4,1,1024]{3,2,1,0:T(1,128)S(1)}, f32[2,4,1,1024]{3,2,1,0:T(1,128)S(1)}, u32[]{:S(2)}, u32[]{:S(2)}) collective-permute-start(f32[2,4,1,1024]{3,2,1,0:T(1,128)S(1)} %broadcast_select_fusion.24), channel_id=1, source_target_pairs={{1,2},{2,1},{3,4},{4,3},{5,6},{6,5},{7,8},{8,7},{9,10},{10,9},{11,... | collective-permute-start | bytes 98312 | tf_op jit(solution)/shard_map/ppermute | solution.py:44
  12.6 5.9 %collective-permute-start = (f32[2,1,8,1024]{3,2,1,0:T(8,128)S(1)}, f32[2,1,8,1024]{3,2,1,0:T(8,128)S(1)}, u32[]{:S(2)}, u32[]{:S(2)}) collective-permute-start(f32[2,1,8,1024]{3,2,1,0:T(8,128)S(1)} %get-tuple-element.44), channel_id=1, source_target_pairs={{0,32},{32,0},{64,96},{96,64},{128,160},{160,128},{192,224},{224,1... | collective-permute-start | bytes 196616 | tf_op jit(solution)/shard_map/ppermute | solution.py:43
  14.5 4.0 %collective-permute-start.1 = (f32[2,1,8,1024]{3,2,1,0:T(8,128)S(1)}, f32[2,1,8,1024]{3,2,1,0:T(8,128)S(1)}, u32[]{:S(2)}, u32[]{:S(2)}) collective-permute-start(f32[2,1,8,1024]{3,2,1,0:T(8,128)S(1)} %get-tuple-element.45), channel_id=1, source_target_pairs={{32,64},{64,32},{96,128},{128,96},{160,192},{192,160},{224,256},{2... | collective-permute-start | bytes 196616 | tf_op jit(solution)/shard_map/ppermute | solution.py:42
  20.3 12.0 %collective-permute-start.6 = (f32[2,4,1,1024]{3,2,1,0:T(1,128)S(1)}, f32[2,4,1,1024]{3,2,1,0:T(1,128)S(1)}, u32[]{:S(2)}, u32[]{:S(2)}) collective-permute-start(f32[2,4,1,1024]{3,2,1,0:T(1,128)S(1)} %get-tuple-element.50), channel_id=1, source_target_pairs={{0,1},{1,0},{2,3},{3,2},{4,5},{5,4},{6,7},{7,6},{8,9},{9,8},{10,11... | collective-permute-start | bytes 98312 | tf_op jit(solution)/shard_map/ppermute | solution.py:45
  22.2 10.1 %collective-permute-start.7 = (f32[2,4,1,1024]{3,2,1,0:T(1,128)S(1)}, f32[2,4,1,1024]{3,2,1,0:T(1,128)S(1)}, u32[]{:S(2)}, u32[]{:S(2)}) collective-permute-start(f32[2,4,1,1024]{3,2,1,0:T(1,128)S(1)} %broadcast_select_fusion.20), channel_id=1, source_target_pairs={{1,2},{2,1},{3,4},{4,3},{5,6},{6,5},{7,8},{8,7},{9,10},{10,9},{11,... | collective-permute-start | bytes 98312 | tf_op jit(solution)/shard_map/ppermute | solution.py:44
  26.1 7.2 %collective-permute-start.4 = (f32[2,1,8,1024]{3,2,1,0:T(8,128)S(1)}, f32[2,1,8,1024]{3,2,1,0:T(8,128)S(1)}, u32[]{:S(2)}, u32[]{:S(2)}) collective-permute-start(f32[2,1,8,1024]{3,2,1,0:T(8,128)S(1)} %get-tuple-element.48), channel_id=1, source_target_pairs={{0,32},{32,0},{64,96},{96,64},{128,160},{160,128},{192,224},{224,1... | collective-permute-start | bytes 196616 | tf_op jit(solution)/shard_map/ppermute | solution.py:43
  33.8 11.2 %collective-permute-start.10 = (f32[2,4,1,1024]{3,2,1,0:T(1,128)S(1)}, f32[2,4,1,1024]{3,2,1,0:T(1,128)S(1)}, u32[]{:S(2)}, u32[]{:S(2)}) collective-permute-start(f32[2,4,1,1024]{3,2,1,0:T(1,128)S(1)} %get-tuple-element.54), channel_id=1, source_target_pairs={{0,1},{1,0},{2,3},{3,2},{4,5},{5,4},{6,7},{7,6},{8,9},{9,8},{10,11... | collective-permute-start | bytes 98312 | tf_op jit(solution)/shard_map/ppermute | solution.py:45
  35.7 9.3 %collective-permute-start.11 = (f32[2,4,1,1024]{3,2,1,0:T(1,128)S(1)}, f32[2,4,1,1024]{3,2,1,0:T(1,128)S(1)}, u32[]{:S(2)}, u32[]{:S(2)}) collective-permute-start(f32[2,4,1,1024]{3,2,1,0:T(1,128)S(1)} %broadcast_select_fusion.16), channel_id=1, source_target_pairs={{1,2},{2,1},{3,4},{4,3},{5,6},{6,5},{7,8},{8,7},{9,10},{10,9},{11,... | collective-permute-start | bytes 98312 | tf_op jit(solution)/shard_map/ppermute | solution.py:44
  39.1 6.9 %collective-permute-start.8 = (f32[2,1,8,1024]{3,2,1,0:T(8,128)S(1)}, f32[2,1,8,1024]{3,2,1,0:T(8,128)S(1)}, u32[]{:S(2)}, u32[]{:S(2)}) collective-permute-start(f32[2,1,8,1024]{3,2,1,0:T(8,128)S(1)} %get-tuple-element.52), channel_id=1, source_target_pairs={{0,32},{32,0},{64,96},{96,64},{128,160},{160,128},{192,224},{224,1... | collective-permute-start | bytes 196616 | tf_op jit(solution)/shard_map/ppermute | solution.py:43
  46.5 14.2 %collective-permute-start.14 = (f32[2,4,1,1024]{3,2,1,0:T(1,128)S(1)}, f32[2,4,1,1024]{3,2,1,0:T(1,128)S(1)}, u32[]{:S(2)}, u32[]{:S(2)}) collective-permute-start(f32[2,4,1,1024]{3,2,1,0:T(1,128)S(1)} %get-tuple-element.58), channel_id=1, source_target_pairs={{0,1},{1,0},{2,3},{3,2},{4,5},{5,4},{6,7},{7,6},{8,9},{9,8},{10,11... | collective-permute-start | bytes 98312 | tf_op jit(solution)/shard_map/ppermute | solution.py:45
  48.4 12.3 %collective-permute-start.15 = (f32[2,4,1,1024]{3,2,1,0:T(1,128)S(1)}, f32[2,4,1,1024]{3,2,1,0:T(1,128)S(1)}, u32[]{:S(2)}, u32[]{:S(2)}) collective-permute-start(f32[2,4,1,1024]{3,2,1,0:T(1,128)S(1)} %broadcast_select_fusion.12), channel_id=1, source_target_pairs={{1,2},{2,1},{3,4},{4,3},{5,6},{6,5},{7,8},{8,7},{9,10},{10,9},{11,... | collective-permute-start | bytes 98312 | tf_op jit(solution)/shard_map/ppermute | solution.py:44
  52.4 9.3 %collective-permute-start.12 = (f32[2,1,8,1024]{3,2,1,0:T(8,128)S(1)}, f32[2,1,8,1024]{3,2,1,0:T(8,128)S(1)}, u32[]{:S(2)}, u32[]{:S(2)}) collective-permute-start(f32[2,1,8,1024]{3,2,1,0:T(8,128)S(1)} %get-tuple-element.56), channel_id=1, source_target_pairs={{0,32},{32,0},{64,96},{96,64},{128,160},{160,128},{192,224},{224,1... | collective-permute-start | bytes 196616 | tf_op jit(solution)/shard_map/ppermute | solution.py:43
  62.1 15.7 %collective-permute-start.18 = (f32[1,4,1,1024]{3,2,1,0:T(1,128)S(1)}, f32[1,4,1,1024]{3,2,1,0:T(1,128)S(1)}, u32[]{:S(2)}, u32[]{:S(2)}) collective-permute-start(f32[1,4,1,1024]{3,2,1,0:T(1,128)S(1)} %get-tuple-element.62), channel_id=1, source_target_pairs={{0,1},{1,0},{2,3},{3,2},{4,5},{5,4},{6,7},{7,6},{8,9},{9,8},{10,11... | collective-permute-start | bytes 49160 | tf_op jit(solution)/shard_map/ppermute | solution.py:45
  64.0 13.8 %collective-permute-start.19 = (f32[1,4,1,1024]{3,2,1,0:T(1,128)S(1)}, f32[1,4,1,1024]{3,2,1,0:T(1,128)S(1)}, u32[]{:S(2)}, u32[]{:S(2)}) collective-permute-start(f32[1,4,1,1024]{3,2,1,0:T(1,128)S(1)} %get-tuple-element.63), channel_id=1, source_target_pairs={{1,2},{2,1},{3,4},{4,3},{5,6},{6,5},{7,8},{8,7},{9,10},{10,9},{11,... | collective-permute-start | bytes 49160 | tf_op jit(solution)/shard_map/ppermute | solution.py:44
  67.3 11.1 %collective-permute-start.16 = (f32[1,1,8,1024]{3,2,1,0:T(8,128)S(1)}, f32[1,1,8,1024]{3,2,1,0:T(8,128)S(1)}, u32[]{:S(2)}, u32[]{:S(2)}) collective-permute-start(f32[1,1,8,1024]{3,2,1,0:T(8,128)S(1)} %get-tuple-element.60), channel_id=1, source_target_pairs={{0,32},{32,0},{64,96},{96,64},{128,160},{160,128},{192,224},{224,1... | collective-permute-start | bytes 98312 | tf_op jit(solution)/shard_map/ppermute | solution.py:43
  83.4 19.9 %collective-permute-start.22 = (f32[2,4,1,1024]{3,2,1,0:T(1,128)S(1)}, f32[2,4,1,1024]{3,2,1,0:T(1,128)S(1)}, u32[]{:S(2)}, u32[]{:S(2)}) collective-permute-start(f32[2,4,1,1024]{3,2,1,0:T(1,128)S(1)} %get-tuple-element.66), channel_id=1, source_target_pairs={{0,1},{1,0},{2,3},{3,2},{4,5},{5,4},{6,7},{7,6},{8,9},{9,8},{10,11... | collective-permute-start | bytes 98312 | tf_op jit(solution)/shard_map/ppermute | solution.py:45
  85.4 18.0 %collective-permute-start.23 = (f32[2,4,1,1024]{3,2,1,0:T(1,128)S(1)}, f32[2,4,1,1024]{3,2,1,0:T(1,128)S(1)}, u32[]{:S(2)}, u32[]{:S(2)}) collective-permute-start(f32[2,4,1,1024]{3,2,1,0:T(1,128)S(1)} %broadcast_select_fusion.8), channel_id=1, source_target_pairs={{1,2},{2,1},{3,4},{4,3},{5,6},{6,5},{7,8},{8,7},{9,10},{10,9},{11,... | collective-permute-start | bytes 98312 | tf_op jit(solution)/shard_map/ppermute | solution.py:44
  90.2 14.4 %collective-permute-start.20 = (f32[2,1,8,1024]{3,2,1,0:T(8,128)S(1)}, f32[2,1,8,1024]{3,2,1,0:T(8,128)S(1)}, u32[]{:S(2)}, u32[]{:S(2)}) collective-permute-start(f32[2,1,8,1024]{3,2,1,0:T(8,128)S(1)} %get-tuple-element.64), channel_id=1, source_target_pairs={{0,32},{32,0},{64,96},{96,64},{128,160},{160,128},{192,224},{224,1... | collective-permute-start | bytes 196616 | tf_op jit(solution)/shard_map/ppermute | solution.py:43
  106.5 18.4 %collective-permute-start.26 = (f32[2,4,1,1024]{3,2,1,0:T(1,128)S(1)}, f32[2,4,1,1024]{3,2,1,0:T(1,128)S(1)}, u32[]{:S(2)}, u32[]{:S(2)}) collective-permute-start(f32[2,4,1,1024]{3,2,1,0:T(1,128)S(1)} %get-tuple-element.70), channel_id=1, source_target_pairs={{0,1},{1,0},{2,3},{3,2},{4,5},{5,4},{6,7},{7,6},{8,9},{9,8},{10,11... | collective-permute-start | bytes 98312 | tf_op jit(solution)/shard_map/ppermute | solution.py:45
  108.5 16.5 %collective-permute-start.27 = (f32[2,4,1,1024]{3,2,1,0:T(1,128)S(1)}, f32[2,4,1,1024]{3,2,1,0:T(1,128)S(1)}, u32[]{:S(2)}, u32[]{:S(2)}) collective-permute-start(f32[2,4,1,1024]{3,2,1,0:T(1,128)S(1)} %broadcast_select_fusion.4), channel_id=1, source_target_pairs={{1,2},{2,1},{3,4},{4,3},{5,6},{6,5},{7,8},{8,7},{9,10},{10,9},{11,... | collective-permute-start | bytes 98312 | tf_op jit(solution)/shard_map/ppermute | solution.py:44
  112.2 14.1 %collective-permute-start.24 = (f32[2,1,8,1024]{3,2,1,0:T(8,128)S(1)}, f32[2,1,8,1024]{3,2,1,0:T(8,128)S(1)}, u32[]{:S(2)}, u32[]{:S(2)}) collective-permute-start(f32[2,1,8,1024]{3,2,1,0:T(8,128)S(1)} %get-tuple-element.68), channel_id=1, source_target_pairs={{0,32},{32,0},{64,96},{96,64},{128,160},{160,128},{192,224},{224,1... | collective-permute-start | bytes 196616 | tf_op jit(solution)/shard_map/ppermute | solution.py:43
  127.9 19.3 %collective-permute-start.30 = (f32[1,4,1,1024]{3,2,1,0:T(1,128)S(1)}, f32[1,4,1,1024]{3,2,1,0:T(1,128)S(1)}, u32[]{:S(2)}, u32[]{:S(2)}) collective-permute-start(f32[1,4,1,1024]{3,2,1,0:T(1,128)S(1)} %get-tuple-element.74), channel_id=1, source_target_pairs={{0,1},{1,0},{2,3},{3,2},{4,5},{5,4},{6,7},{7,6},{8,9},{9,8},{10,11... | collective-permute-start | bytes 49160 | tf_op jit(solution)/shard_map/ppermute | solution.py:45
  129.8 17.4 %collective-permute-start.31 = (f32[1,4,1,1024]{3,2,1,0:T(1,128)S(1)}, f32[1,4,1,1024]{3,2,1,0:T(1,128)S(1)}, u32[]{:S(2)}, u32[]{:S(2)}) collective-permute-start(f32[1,4,1,1024]{3,2,1,0:T(1,128)S(1)} %get-tuple-element.75), channel_id=1, source_target_pairs={{1,2},{2,1},{3,4},{4,3},{5,6},{6,5},{7,8},{8,7},{9,10},{10,9},{11,... | collective-permute-start | bytes 49160 | tf_op jit(solution)/shard_map/ppermute | solution.py:44
  135.6 12.3 %collective-permute-start.28 = (f32[1,1,8,1024]{3,2,1,0:T(8,128)S(1)}, f32[1,1,8,1024]{3,2,1,0:T(8,128)S(1)}, u32[]{:S(2)}, u32[]{:S(2)}) collective-permute-start(f32[1,1,8,1024]{3,2,1,0:T(8,128)S(1)} %get-tuple-element.72), channel_id=1, source_target_pairs={{0,32},{32,0},{64,96},{96,64},{128,160},{160,128},{192,224},{224,1... | collective-permute-start | bytes 98312 | tf_op jit(solution)/shard_map/ppermute | solution.py:43
  148.2 18.5 %collective-permute-start.34 = (f32[1,4,1,1024]{3,2,1,0:T(1,128)S(1)}, f32[1,4,1,1024]{3,2,1,0:T(1,128)S(1)}, u32[]{:S(2)}, u32[]{:S(2)}) collective-permute-start(f32[1,4,1,1024]{3,2,1,0:T(1,128)S(1)} %get-tuple-element.78), channel_id=1, source_target_pairs={{0,1},{1,0},{2,3},{3,2},{4,5},{5,4},{6,7},{7,6},{8,9},{9,8},{10,11... | collective-permute-start | bytes 49160 | tf_op jit(solution)/shard_map/ppermute | solution.py:45
  150.2 16.6 %collective-permute-start.35 = (f32[1,4,1,1024]{3,2,1,0:T(1,128)S(1)}, f32[1,4,1,1024]{3,2,1,0:T(1,128)S(1)}, u32[]{:S(2)}, u32[]{:S(2)}) collective-permute-start(f32[1,4,1,1024]{3,2,1,0:T(1,128)S(1)} %get-tuple-element.79), channel_id=1, source_target_pairs={{1,2},{2,1},{3,4},{4,3},{5,6},{6,5},{7,8},{8,7},{9,10},{10,9},{11,... | collective-permute-start | bytes 49160 | tf_op jit(solution)/shard_map/ppermute | solution.py:44
  154.6 12.8 %collective-permute-start.32 = (f32[1,1,8,1024]{3,2,1,0:T(8,128)S(1)}, f32[1,1,8,1024]{3,2,1,0:T(8,128)S(1)}, u32[]{:S(2)}, u32[]{:S(2)}) collective-permute-start(f32[1,1,8,1024]{3,2,1,0:T(8,128)S(1)} %get-tuple-element.76), channel_id=1, source_target_pairs={{0,32},{32,0},{64,96},{96,64},{128,160},{160,128},{192,224},{224,1... | collective-permute-start | bytes 98312 | tf_op jit(solution)/shard_map/ppermute | solution.py:43
  167.8 18.9 %collective-permute-start.38 = (f32[1,4,1,1024]{3,2,1,0:T(1,128)S(1)}, f32[1,4,1,1024]{3,2,1,0:T(1,128)S(1)}, u32[]{:S(2)}, u32[]{:S(2)}) collective-permute-start(f32[1,4,1,1024]{3,2,1,0:T(1,128)S(1)} %get-tuple-element.82), channel_id=1, source_target_pairs={{0,1},{1,0},{2,3},{3,2},{4,5},{5,4},{6,7},{7,6},{8,9},{9,8},{10,11... | collective-permute-start | bytes 49160 | tf_op jit(solution)/shard_map/ppermute | solution.py:45
  169.7 16.9 %collective-permute-start.39 = (f32[1,4,1,1024]{3,2,1,0:T(1,128)S(1)}, f32[1,4,1,1024]{3,2,1,0:T(1,128)S(1)}, u32[]{:S(2)}, u32[]{:S(2)}) collective-permute-start(f32[1,4,1,1024]{3,2,1,0:T(1,128)S(1)} %get-tuple-element.83), channel_id=1, source_target_pairs={{1,2},{2,1},{3,4},{4,3},{5,6},{6,5},{7,8},{8,7},{9,10},{10,9},{11,... | collective-permute-start | bytes 49160 | tf_op jit(solution)/shard_map/ppermute | solution.py:44
  174.2 13.1 %collective-permute-start.36 = (f32[1,1,8,1024]{3,2,1,0:T(8,128)S(1)}, f32[1,1,8,1024]{3,2,1,0:T(8,128)S(1)}, u32[]{:S(2)}, u32[]{:S(2)}) collective-permute-start(f32[1,1,8,1024]{3,2,1,0:T(8,128)S(1)} %get-tuple-element.80), channel_id=1, source_target_pairs={{0,32},{32,0},{64,96},{96,64},{128,160},{160,128},{192,224},{224,1... | collective-permute-start | bytes 98312 | tf_op jit(solution)/shard_map/ppermute | solution.py:43
  190.2 59.4 %all-to-all-start = ((f32[512,1,128]{2,1,0:T(1,128)}), f32[512,1,128]{2,1,0:T(1,128)S(1)}, u32[]{:S(2)}, u32[]{:S(2)}) async-start(f32[512,1,128]{2,1,0:T(1,128)} %broadcast_select_fusion), calls=%async_computation | async-start | bytes 524288 | tf_op jit(solution)/shard_map/all_to_all | solution.py:200
  (28 other events, 124.4 us)

commit v3 on v1

v3 whole, which is shorter than its diff:
```python
import functools

import jax
import jax.numpy as jnp
from jax import lax
from jax.experimental import pallas as pl
from jax.experimental.pallas import tpu as pltpu
from jax.sharding import PartitionSpec as P


STEPS = 2


fluidity_barrier = 4.0
fluidity_gelation_coefficient = 2.0
arrhenius_prefactor = 0.2
arrhenius_barrier = 8.0
released_enthalpy = 0.3
diffusion_coefficient = 0.1
clock_step_size = 0.5
epsilon = 1e-06

PLIES, ROWS, SUB, LANE = 4, 8, 8, 128
OFF = 3
DEEP = (PLIES + 2 * OFF, ROWS + 2 * OFF, SUB, LANE)
RIM = (PLIES + 2, ROWS + 2, SUB, LANE)
BLOCK = (PLIES, ROWS, SUB, LANE)


def swap_pairs(count, parity):
    pairs = []
    for i in range(parity, count - 1, 2):
        pairs += [(i, i + 1), (i + 1, i)]
    return pairs


def swap(axis, odd_send, even_send):
    count = lax.axis_size(axis)
    odd = lax.ppermute(odd_send, axis, swap_pairs(count, 1))
    even = lax.ppermute(even_send, axis, swap_pairs(count, 0))
    return odd, even


def cell_index(shape):
    return LANE * lax.broadcasted_iota(jnp.int32, shape, 1) + lax.broadcasted_iota(
        jnp.int32, shape, 2
    )


def next_cell(x):
    moved = pltpu.roll(x, LANE - 1, 2)
    lane = lax.broadcasted_iota(jnp.int32, x.shape, 2)
    return jnp.where(lane == LANE - 1, pltpu.roll(moved, SUB - 1, 1), moved)


def previous_cell(x):
    moved = pltpu.roll(x, 1, 2)
    lane = lax.broadcasted_iota(jnp.int32, x.shape, 2)
    return jnp.where(lane == 0, pltpu.roll(moved, 1, 1), moved)


def beside(ref, i, top, end, walled=False):
    centre = ref[i, top:end]
    after, before = next_cell(centre), previous_cell(centre)
    if walled:
        cell = cell_index(centre.shape)
        after = jnp.where(cell == SUB * LANE - 1, 0.0, after)
        before = jnp.where(cell == 0, 0.0, before)
    return centre, [
        ref[i + 1, top:end],
        ref[i - 1, top:end],
        ref[i, top + 1 : end + 1],
        ref[i, top - 1 : end - 1],
        after,
        before,
    ]


def face_list(mobility, i, top, end):
    centre, around = beside(mobility, i, top, end, walled=True)
    result = []
    for other in around:
        denom = centre + other
        result.append(2.0 * centre * other / jnp.where(denom > 0, denom, 1.0))
    return result


def mobility_of(preform, warmth, crosslink):
    return preform * jnp.exp(
        -(
            fluidity_barrier * (1.0 / warmth - 1.0)
            + fluidity_gelation_coefficient * crosslink
        )
    )


def loop(count, body):
    def step(i, carry):
        body(i)
        return carry

    lax.fori_loop(0, count, step, 0)


def pack_plies(par, local, depth, odd_out, even_out, unit):
    last = PLIES - depth
    odd_out[unit : unit + depth] = local[pl.ds(par[0] * last, depth)]
    even_out[unit : unit + depth] = local[pl.ds((1 - par[0]) * last, depth)]


def pack_rows(par, local, odd_in, even_in, unit, depth, odd_out, even_out, base, corners=True):
    last = ROWS - depth
    for out, start in ((odd_out, par[1] * last), (even_out, (1 - par[1]) * last)):
        skip = depth if corners else 0
        for i in range(PLIES):
            at = base + (skip + i) * depth
            out[at : at + depth] = local[i, pl.ds(start, depth)]
        if corners:
            for came, first in (
                (odd_in, par[0] * (PLIES + depth)),
                (even_in, (1 - par[0]) * (PLIES + depth)),
            ):
                for i in range(depth):
                    out[pl.ds(base + (first + i) * depth, depth)] = came[
                        unit + i, pl.ds(start, depth)
                    ]


def assemble(par, dst, off, local, ply_in, unit, row_in, base, depth, corners=True):
    for i in range(PLIES):
        dst[off + i, off : off + ROWS] = local[i]
    for came, side in zip(ply_in, (par[0], 1 - par[0]), strict=True):
        first = off - depth + side * (PLIES + depth)
        for i in range(depth):
            dst[first + i, off : off + ROWS] = came[unit + i]
    skip = 0 if corners else depth
    for came, side in zip(row_in, (par[1], 1 - par[1]), strict=True):
        first = off - depth + side * (ROWS + depth)
        for i in range(PLIES + 2 * (depth - skip)):
            at = base + i * depth
            dst[off - depth + skip + i, pl.ds(first, depth)] = came[at : at + depth]


def to_lines(flat, lines, i):
    for j in range(SUB):
        part = flat[i, :, j * LANE : (j + 1) * LANE].astype(jnp.float32)
        lines[pl.ds(j, ROWS, stride=SUB), :] = part
    return lines[...].reshape(ROWS, SUB, LANE)


def from_lines(value, lines, flat, i):
    lines[...] = value.reshape(ROWS * SUB, LANE)
    for j in range(SUB):
        flat[i, :, j * LANE : (j + 1) * LANE] = lines[pl.ds(j, ROWS, stride=SUB), :]


def prepare_kernel(
    par, warmth, crosslink, stress, preform, wetted, inlet, outlet,
    warmth_out, crosslink_out, stress_out, preform_out, mobility, free, fixed, fill,
    odd_out, even_out, *lines,
):
    for i in range(PLIES):
        t = to_lines(warmth, lines[0], i)
        c = to_lines(crosslink, lines[1], i)
        k = to_lines(preform, lines[2], i)
        warmth_out[i] = t
        crosslink_out[i] = c
        preform_out[i] = k
        mobility[i] = mobility_of(k, t, c)
        stress_out[i] = to_lines(stress, lines[3], i)
        w = to_lines(wetted, lines[4], i)
        n = to_lines(inlet, lines[5], i)
        o = to_lines(outlet, lines[6], i)
        fill[i] = w
        fixed[i] = n
        free[i] = w * (1.0 - n) * (1.0 - o)
    pack_plies(par, stress_out, 3, odd_out, even_out, 0)
    pack_plies(par, mobility, 3, odd_out, even_out, 3)
    pack_plies(par, free, 2, odd_out, even_out, 6)
    pack_plies(par, fixed, 2, odd_out, even_out, 8)


FIRST = ((0, 0, 3), (3, 30, 3), (6, 60, 2), (8, 76, 2))


def rows_kernel(layout, corners, par, *refs):
    n = len(layout)
    odd_in, even_in, odd_out, even_out = refs[n:]
    for local, (unit, base, depth), corner in zip(refs[:n], layout, corners, strict=True):
        pack_rows(par, local, odd_in, even_in, unit, depth, odd_out, even_out, base, corner)


def sweep(source, target, weights, shift, depth):
    top, end = OFF - depth, OFF + ROWS + depth

    def ply(k):
        i = OFF - depth + k
        _, around = beside(source, i, top, end)
        rows = slice(top - shift, end - shift)
        total = weights[6, i - shift, rows]
        for f in range(6):
            total = total + weights[f, i - shift, rows] * around[f]
        target[i, top:end] = total

    loop(PLIES + 2 * depth, ply)


def sweeps_kernel(first, par, *refs):
    if first:
        (stress, mobility, free, fixed, warmth, crosslink, fill,
         odd_in, even_in, odd_rows, even_rows,
         stress_out, weights_out, mobility_out, free_deep, fixed_deep, odd_out, even_out,
         p0, p1, m, weights) = refs
    else:
        (stress, mobility, free_deep, fixed_deep, warmth, crosslink,
         odd_in, even_in, odd_rows, even_rows,
         stress_out, weights_out, mobility_out, odd_out, even_out,
         p0, p1, m, weights) = refs
    fields = [(p0, stress), (m, mobility)]
    if first:
        fields += [(free_deep, free), (fixed_deep, fixed)]
    for (dst, local), (unit, base, depth) in zip(fields, FIRST, strict=False):
        assemble(par, dst, OFF, local, (odd_in, even_in), unit, (odd_rows, even_rows), base, depth)
    top, end = 1, OFF + ROWS + 2

    def weigh(k):
        i = 1 + k
        faces = face_list(m, i, top, end)
        is_free = free_deep[i, top:end] > 0
        total = faces[0]
        for f in range(1, 6):
            total = total + faces[f]
        scale = jnp.where(is_free, 1.0 / jnp.where(is_free, total, 1.0), 0.0)
        for f in range(6):
            weights[f, k] = faces[f] * scale
        weights[6, k] = jnp.where(is_free, 0.0, fixed_deep[i, top:end])

    loop(PLIES + 4, weigh)
    sweep(p0, p1, weights, 1, 2)
    sweep(p1, p0, weights, 1, 1)
    sweep(p0, p1, weights, 1, 0)
    for i in range(PLIES):
        stress_out[i] = p1[OFF + i, OFF : OFF + ROWS]

    def keep(k):
        mobility_out[k] = m[k + OFF - 1, OFF - 1 : OFF + ROWS + 1]
        for f in range(7):
            weights_out[f, k] = weights[f, k + 1, 1 : 1 + ROWS + 2]

    loop(PLIES + 2, keep)
    pack_plies(par, stress_out, 2, odd_out, even_out, 0)
    pack_plies(par, warmth, 1, odd_out, even_out, 2)
    pack_plies(par, crosslink, 1, odd_out, even_out, 3)
    if first:
        pack_plies(par, fill, 1, odd_out, even_out, 4)


SECOND = ((0, 0, 2), (2, 16, 1), (3, 20, 1), (4, 24, 1))


def residual_kernel(
    par, stress, weights, mobility, free, odd_in, even_in, odd_rows, even_rows,
    stress_rim, squares, p0, p1,
):
    assemble(par, p0, OFF, stress, (odd_in, even_in), 0, (odd_rows, even_rows), 0, 2)
    sweep(p0, p1, weights, OFF - 1, 1)
    squares[...] = jnp.zeros((SUB, LANE), jnp.float32)

    def ply(k):
        centre, around = beside(p1, OFF + k, OFF, OFF + ROWS)
        faces = face_list(mobility, 1 + k, 1, 1 + ROWS)
        weighted = faces[0] * around[0]
        total = faces[0]
        for f in range(1, 6):
            weighted = weighted + faces[f] * around[f]
            total = total + faces[f]
        imbalance = free[k] * (weighted - total * centre)
        squares[...] += jnp.sum(imbalance * imbalance, axis=0)

    loop(PLIES, ply)

    def keep(k):
        stress_rim[k] = p1[k + OFF - 1, OFF - 1 : OFF + ROWS + 1]

    loop(PLIES + 2, keep)


def transport_kernel(first, last, par, *refs):
    stress_rim, mobility, warmth, crosslink, preform = refs[:5]
    if first:
        fill, refs = refs[5], refs[6:]
    else:
        fill_rim, refs = refs[5], refs[6:]
    odd_in, even_in, odd_rows, even_rows = refs[:4]
    refs = refs[4:]
    if last:
        warmth_out, crosslink_out, stress_out = refs[:3]
        refs = refs[3:]
    else:
        warmth_out, crosslink_out, stress_out, mobility_out, odd_out, even_out = refs[:6]
        refs = refs[6:]
    if first:
        fill_rim, refs = refs[0], refs[1:]
    t_rim, c_rim = refs[:2]
    lines = refs[2:]
    fields = [(t_rim, warmth), (c_rim, crosslink)]
    if first:
        fields.append((fill_rim, fill))
    for (dst, local), (unit, base, depth) in zip(fields, SECOND[1:], strict=False):
        assemble(
            par, dst, 1, local, (odd_in, even_in), unit, (odd_rows, even_rows), base, depth, False
        )

    def ply(k):
        i, top, end = 1 + k, 1, 1 + ROWS
        stress, near_stress = beside(stress_rim, i, top, end)
        t, near_t = beside(t_rim, i, top, end)
        c, near_c = beside(c_rim, i, top, end)
        full, near_full = beside(fill_rim, i, top, end, walled=True)
        faces = face_list(mobility, i, top, end)
        t_gain = jnp.zeros_like(t)
        c_gain = jnp.zeros_like(t)
        spread = jnp.zeros_like(t)
        for f in range(6):
            inward = jnp.maximum(faces[f] * (near_stress[f] - stress), 0.0) * near_full[f]
            t_step = near_t[f] - t
            t_gain = t_gain + inward * t_step
            c_gain = c_gain + inward * (near_c[f] - c)
            spread = spread + near_full[f] * t_step
        speed = (
            arrhenius_prefactor * jnp.exp(arrhenius_barrier * (1.0 - 1.0 / t)) * (1.0 - c)
        )
        t_new = t + full * clock_step_size * (
            t_gain + diffusion_coefficient * spread + released_enthalpy * speed
        )
        c_new = c + full * clock_step_size * (c_gain + speed)
        if last:
            from_lines(t_new, lines[0], warmth_out, k)
            from_lines(c_new, lines[1], crosslink_out, k)
            from_lines(stress, lines[2], stress_out, k)
        else:
            warmth_out[k] = t_new
            crosslink_out[k] = c_new
            stress_out[k] = stress
            mobility_out[k] = mobility_of(preform[k], t_new, c_new)

    if last:
        for k in range(PLIES):
            ply(k)
    else:
        loop(PLIES, ply)
        pack_plies(par, stress_out, 3, odd_out, even_out, 0)
        pack_plies(par, mobility_out, 3, odd_out, even_out, 3)


def call(kernel, args, outs, scratch=()):
    vmem = pl.BlockSpec(memory_space=pltpu.VMEM)
    return pl.pallas_call(
        kernel,
        out_shape=[jax.ShapeDtypeStruct(shape, jnp.float32) for shape in outs],
        in_specs=[pl.BlockSpec(memory_space=pltpu.SMEM)] + [vmem] * (len(args) - 1),
        out_specs=[vmem] * len(outs),
        scratch_shapes=[pltpu.VMEM(shape, jnp.float32) for shape in scratch],
    )(*args)


def exchange(par, fields, layout, corners, sends):
    came = swap("ply", *sends)
    lines = sum(
        (PLIES + (2 * depth if corner else 0)) * depth
        for (_, _, depth), corner in zip(layout, corners, strict=True)
    )
    rows = call(
        functools.partial(rows_kernel, layout, corners),
        [par, *fields, *came],
        [(lines, SUB, LANE)] * 2,
    )
    return (*came, *swap("tile", *rows))


def per_device(
    scaled_warmth,
    crosslink_fraction,
    fluid_stress,
    preform_porosity_coefficient,
    wetted_flags,
    injection_flags,
    outlet_flags,
):
    devices = lax.axis_size("ply") * lax.axis_size("tile")
    site_total = scaled_warmth.size * devices
    shape = scaled_warmth.shape
    assert shape == (PLIES, ROWS, SUB * LANE)
    pair = lax.broadcasted_iota(jnp.int32, (2,), 0)
    par = jnp.where(pair == 0, lax.axis_index("ply") % 2, lax.axis_index("tile") % 2)
    line = (ROWS * SUB, LANE)
    (warmth, crosslink, stress, preform, mobility, free, fixed, fill, *sends) = call(
        prepare_kernel,
        [
            par,
            scaled_warmth,
            crosslink_fraction,
            fluid_stress,
            preform_porosity_coefficient,
            wetted_flags,
            injection_flags,
            outlet_flags,
        ],
        [BLOCK] * 8 + [(10, ROWS, SUB, LANE)] * 2,
        [line] * 7,
    )
    local_sums = []
    for repeat in range(STEPS):
        first, last = repeat == 0, repeat == STEPS - 1
        fields = [stress, mobility] + ([free, fixed] if first else [])
        count = len(fields)
        came = exchange(par, fields, FIRST[:count], (True,) * count, sends)
        units = 5 if first else 4
        args = fields if first else fields + [free_deep, fixed_deep]
        result = call(
            functools.partial(sweeps_kernel, first),
            [par, *args, warmth, crosslink, *([fill] if first else []), *came],
            [BLOCK, (7, *RIM), RIM]
            + ([DEEP] * 2 if first else [])
            + [(units, ROWS, SUB, LANE)] * 2,
            [DEEP, DEEP, DEEP, (7, PLIES + 4, ROWS + 4, SUB, LANE)],
        )
        stress, weights, mobility_rim, *rest = result
        if first:
            free_deep, fixed_deep, *rest = rest
        fields = [stress, warmth, crosslink] + ([fill] if first else [])
        came = exchange(
            par, fields, SECOND[: len(fields)], (True, False, False, False)[: len(fields)], rest
        )
        stress_rim, squares = call(
            residual_kernel,
            [par, stress, weights, mobility_rim, free, *came],
            [RIM, (SUB, LANE)],
            [DEEP, DEEP],
        )
        local_sums.append(jnp.sum(squares))
        outs = [shape] * 3 if last else [BLOCK] * 4 + [(6, ROWS, SUB, LANE)] * 2
        warmth, crosslink, stress, *rest = call(
            functools.partial(transport_kernel, first, last),
            [
                par,
                stress_rim,
                mobility_rim,
                warmth,
                crosslink,
                preform,
                fill if first else fill_rim,
                *came,
            ],
            outs + ([RIM] if first else []),
            [RIM, RIM] + ([line] * 3 if last else []),
        )
        if first:
            fill_rim = rest.pop()
        if not last:
            mobility, *sends = rest
    lane = lax.broadcasted_iota(jnp.int32, (devices, 1, LANE), 2)
    message = jnp.where(lane == 0, local_sums[0], jnp.where(lane == 1, local_sums[1], 0.0))
    parts = lax.all_to_all(message, ("ply", "tile"), 0, 0)
    totals = jnp.sum(parts, axis=(0, 1))[:STEPS]
    imbalance_record = jnp.sqrt(totals / site_total + epsilon)
    return (warmth, crosslink, stress, imbalance_record)


def solution(mesh):
    return jax.shard_map(
        per_device,
        mesh=mesh,
        in_specs=(P("ply", "tile", None),) * 7,
        out_specs=(P("ply", "tile", None), P("ply", "tile", None), P("ply", "tile", None), P()),
        check_vma=False,
    )
```

time: 255 us -> 187 us (0.73)
  starting transfers between devices: 206 us -> 97.7 us
  Pallas kernels: 0 us -> 36.5 us
  waiting for transfers between devices: 20.2 us -> 40.1 us
  other arithmetic: 12.9 us -> 5.07 us
  local copies, waits for them, and re-layouts: 12.5 us -> 5.71 us
    ppermute x40 -> x16, starting transfers between devices: 163 us -> 58.8 us  [the longest x8 36.6 us: swap(): even = lax.ppermute(even_send, axis, swap_pairs(count, 0))]
    pallas_call x0 -> x11, Pallas kernels: none -> 36.5 us  [call(): pl.pallas_call(kernel, out_shape=[jax.ShapeDtypeStruct(shape, jnp.float32...]
    ppermute x40 -> x16, waiting for transfers between devices: 8.33 us -> 26.1 us  [the longest x8 19.7 us: swap(): even = lax.ppermute(even_send, axis, swap_pairs(count, 0))]
    slice x42 -> x0, local copies, waits for them, and re-layouts: 5.26 us -> none  [the longest x11 2.31 us: nearby_sites(): array[:, :, 1:]]
    all_to_all x1, starting transfers between devices: 43.1 us -> 38.9 us  [per_device(): parts = lax.all_to_all(message, ('ply', 'tile'), 0, 0)]
    add x2 -> x0, other arithmetic: 3.59 us -> none  [the longest x1 2.48 us: donor_advection(): crosslink_fraction + wetted_status * clock_step_size * (donor_crosslink_a...]
    unnamed x41 -> x34, local copies, waits for them, and re-layouts: 4.74 us -> 5.71 us
  transfers between devices with their start and end apart: 41 -> 17, of which waited for: 12 -> 10; matrix products, arithmetic and copies ran while one was open for 3% -> 0% of each run, Pallas kernels for 0% -> 2%
where the time goes in v3:
time: 187 us; the launch traced here: 186 us
  starting transfers between devices  97.7 us (52%)
  waiting for transfers between devices  40.1 us (21%)
  Pallas kernels  36.5 us (20%)
  local copies, waits for them, and re-layouts  5.71 us (3%)
  other arithmetic  5.07 us (3%)
    all_to_all x1, starting transfers between devices, per_device(): parts = lax.all_to_all(message, ('ply', 'tile'), 0, 0)  38.9 us
    ppermute x8, starting transfers between devices, swap(): even = lax.ppermute(even_send, axis, swap_pairs(count, 0))  36.6 us
    pallas_call x11, Pallas kernels, call(): pl.pallas_call(kernel, out_shape=[jax.ShapeDtypeStruct(shape, jnp.float32...  36.5 us
    ppermute x8, starting transfers between devices, swap(): odd = lax.ppermute(odd_send, axis, swap_pairs(count, 1))  22.2 us
    ppermute x8, waiting for transfers between devices, swap(): even = lax.ppermute(even_send, axis, swap_pairs(count, 0))  19.7 us
    all_to_all x1, waiting for transfers between devices, per_device(): parts = lax.all_to_all(message, ('ply', 'tile'), 0, 0)  14 us
    ppermute x8, waiting for transfers between devices, swap(): odd = lax.ppermute(odd_send, axis, swap_pairs(count, 1))  6.46 us
    unnamed x34, local copies, waits for them, and re-layouts  5.71 us
  transfers between devices with their start and end apart: 17, of which 10 were waited for; matrix products, arithmetic and copies ran while one was open for 0% of the time, Pallas kernels for 2%

profile of v3, /device:TPU:1, one launch (start us, length us, event | category | flops | bytes accessed | tf_op | source)
XLA Modules:
  0.0 186.0 jit_solution(4330396698606646947)
XLA Ops:
  1.2 2.5 %shard_map.102 = (f32[4,8,8,128]{3,2,1,0:T(8,128)}, f32[4,8,8,128]{3,2,1,0:T(8,128)}, f32[4,8,8,128]{3,2,1,0:T(8,128)}, f32[4,8,8,128]{3,2,1,0:T(8,128)}, f32[4,...) custom-call(s32[2]{0:T(128)} %compare_select_fusion.1.par, ...), custom_call_target="tpu_custom_call" | custom-call | tf_op jit(solution)/shard_map/pallas_call | solution.py:358
  4.3 6.5 %collective-permute-start.1 = (f32[10,8,8,128]{3,2,1,0:T(8,128)}, f32[10,8,8,128]{3,2,1,0:T(8,128)S(1)}, u32[]{:S(2)}, u32[]{:S(2)}) collective-permute-start(f32[10,8,8,128]{3,2,1,0:T(8,128)} %get-tuple-element.56), channel_id=1, source_target_pairs={{0,32},{32,0},{64,96},{96,64},{128,160},{160,128},{192,224},{224,1... | collective-permute-start | bytes 983048 | tf_op jit(solution)/shard_map/ppermute | solution.py:40
  10.9 5.4 %collective-permute-done.1.refs_5_.refs_8_ = f32[10,8,8,128]{3,2,1,0:T(8,128)S(1)} collective-permute-done((f32[10,8,8,128]{3,2,1,0:T(8,128)}, f32[10,8,8,128]{3,2,1,0:T(8,128)S(1)}, u32[]{:S(2)}, u32[]{:S(2)}) %collective-permute-start.1) | collective-permute-done | bytes 327712 | tf_op jit(solution)/shard_map/ppermute | solution.py:40
  17.1 2.3 %shard_map.103 = (f32[92,8,128]{2,1,0:T(8,128)}, f32[92,8,128]{2,1,0:T(8,128)}) custom-call(s32[2]{0:T(128)} %compare_select_fusion.1.par, f32[4,8,8,128]{3,2,1,0:T(8,128)} %get-tuple-element.48.refs_0_, f32[4,8,8,128]{3,2,1,0:T(8,128)} %get-tuple-element.49.refs_1_, f32[4,8,8,128]{3,2,1,0:T(8,128)} %get-tuple-element.50.refs_2_.free, ...), custom_call_target="tpu_custom_call" | custom-call | tf_op jit(solution)/shard_map/pallas_call | solution.py:358
  19.3 6.4 %collective-permute-start.2 = (f32[92,8,128]{2,1,0:T(8,128)}, f32[92,8,128]{2,1,0:T(8,128)S(1)}, u32[]{:S(2)}, u32[]{:S(2)}) collective-permute-start(f32[92,8,128]{2,1,0:T(8,128)} %get-tuple-element.57), channel_id=1, source_target_pairs={{1,2},{2,1},{3,4},{4,3},{5,6},{6,5},{7,8},{8,7},{9,10},{10,9},{11,... | collective-permute-start | bytes 1130504 | tf_op jit(solution)/shard_map/ppermute | solution.py:39
  25.8 1.9 %collective-permute-start.3 = (f32[92,8,128]{2,1,0:T(8,128)}, f32[92,8,128]{2,1,0:T(8,128)S(1)}, u32[]{:S(2)}, u32[]{:S(2)}) collective-permute-start(f32[92,8,128]{2,1,0:T(8,128)} %get-tuple-element.58), channel_id=1, source_target_pairs={{0,1},{1,0},{2,3},{3,2},{4,5},{5,4},{6,7},{7,6},{8,9},{9,8},{10,11... | collective-permute-start | bytes 1130504 | tf_op jit(solution)/shard_map/ppermute | solution.py:40
  27.7 3.6 %collective-permute-done.2.refs_9_ = f32[92,8,128]{2,1,0:T(8,128)S(1)} collective-permute-done((f32[92,8,128]{2,1,0:T(8,128)}, f32[92,8,128]{2,1,0:T(8,128)S(1)}, u32[]{:S(2)}, u32[]{:S(2)}) %collective-permute-start.2) | collective-permute-done | bytes 376864 | tf_op jit(solution)/shard_map/ppermute | solution.py:39
  32.1 6.5 %shard_map.104 = (f32[4,8,8,128]{3,2,1,0:T(8,128)}, f32[7,6,10,8,128]{4,3,2,1,0:T(8,128)}, f32[6,10,8,128]{3,2,1,0:T(8,128)}, f32[10,14,8,128]{3,2,1,0:T(8,128)}...) custom-call(s32[2]{0:T(128)} %compare_select_fusion.1.par, ...), custom_call_target="tpu_custom_call" | custom-call | tf_op jit(solution)/shard_map/pallas_call | solution.py:358
  39.3 6.9 %collective-permute-start.5 = (f32[5,8,8,128]{3,2,1,0:T(8,128)}, f32[5,8,8,128]{3,2,1,0:T(8,128)S(1)}, u32[]{:S(2)}, u32[]{:S(2)}) collective-permute-start(f32[5,8,8,128]{3,2,1,0:T(8,128)} %get-tuple-element.63), channel_id=1, source_target_pairs={{0,32},{32,0},{64,96},{96,64},{128,160},{160,128},{192,224},{224,1... | collective-permute-start | bytes 491528 | tf_op jit(solution)/shard_map/ppermute | solution.py:40
  46.3 3.4 %collective-permute-done.5.refs_5_.even_in.refs_7_ = f32[5,8,8,128]{3,2,1,0:T(8,128)S(1)} collective-permute-done((f32[5,8,8,128]{3,2,1,0:T(8,128)}, f32[5,8,8,128]{3,2,1,0:T(8,128)S(1)}, u32[]{:S(2)}, u32[]{:S(2)}) %collective-permute-start.5) | collective-permute-done | bytes 163872 | tf_op jit(solution)/shard_map/ppermute | solution.py:40
  50.4 2.0 %shard_map.105 = (f32[28,8,128]{2,1,0:T(8,128)}, f32[28,8,128]{2,1,0:T(8,128)}) custom-call(s32[2]{0:T(128)} %compare_select_fusion.1.par, f32[4,8,8,128]{3,2,1,0:T(8,128)} %get-tuple-element.59.refs_0_.stress, f32[4,8,8,128]{3,2,1,0:T(8,128)} %get-tuple-element.52.refs_4_.refs_1_.refs_2_, f32[4,8,8,128]{3,2,1,0:T(8,128)} %get-tuple-element.53.refs_5_.refs_2_.refs_3_, ...), custom_call_target="tpu_custom_call" | custom-call | tf_op jit(solution)/shard_map/pallas_call | solution.py:358
  52.3 5.1 %collective-permute-start.6 = (f32[28,8,128]{2,1,0:T(8,128)}, f32[28,8,128]{2,1,0:T(8,128)S(1)}, u32[]{:S(2)}, u32[]{:S(2)}) collective-permute-start(f32[28,8,128]{2,1,0:T(8,128)} %get-tuple-element.64), channel_id=1, source_target_pairs={{1,2},{2,1},{3,4},{4,3},{5,6},{6,5},{7,8},{8,7},{9,10},{10,9},{11,... | collective-permute-start | bytes 344072 | tf_op jit(solution)/shard_map/ppermute | solution.py:39
  57.5 1.9 %collective-permute-start.7 = (f32[28,8,128]{2,1,0:T(8,128)}, f32[28,8,128]{2,1,0:T(8,128)S(1)}, u32[]{:S(2)}, u32[]{:S(2)}) collective-permute-start(f32[28,8,128]{2,1,0:T(8,128)} %get-tuple-element.65), channel_id=1, source_target_pairs={{0,1},{1,0},{2,3},{3,2},{4,5},{5,4},{6,7},{7,6},{8,9},{9,8},{10,11... | collective-permute-start | bytes 344072 | tf_op jit(solution)/shard_map/ppermute | solution.py:40
  61.5 3.5 %shard_map.106 = (f32[6,10,8,128]{3,2,1,0:T(8,128)}, f32[8,128]{1,0:T(8,128)}) custom-call(s32[2]{0:T(128)} %compare_select_fusion.1.par, f32[4,8,8,128]{3,2,1,0:T(8,128)} %get-tuple-element.59.refs_0_.stress, f32[7,6,10,8,128]{4,3,2,1,0:T(8,128)} %get-tuple-element.60.weights, f32[6,10,8,128]{3,2,1,0:T(8,128)} %get-tuple-element.61.mobility.refs_1_, ...), custom_call_target="tpu_custom_call" | custom-call | tf_op jit(solution)/shard_map/pallas_call | solution.py:358
  65.0 3.4 %shard_map.107 = (f32[4,8,8,128]{3,2,1,0:T(8,128)}, f32[4,8,8,128]{3,2,1,0:T(8,128)}, f32[4,8,8,128]{3,2,1,0:T(8,128)}, f32[4,8,8,128]{3,2,1,0:T(8,128)}, f32[6,...) custom-call(s32[2]{0:T(128)} %compare_select_fusion.1.par, ...), custom_call_target="tpu_custom_call" | custom-call | tf_op jit(solution)/shard_map/pallas_call | solution.py:358
  69.1 4.8 %collective-permute-start.9 = (f32[6,8,8,128]{3,2,1,0:T(8,128)}, f32[6,8,8,128]{3,2,1,0:T(8,128)S(1)}, u32[]{:S(2)}, u32[]{:S(2)}) collective-permute-start(f32[6,8,8,128]{3,2,1,0:T(8,128)} %get-tuple-element.75), channel_id=1, source_target_pairs={{0,32},{32,0},{64,96},{96,64},{128,160},{160,128},{192,224},{224,1... | collective-permute-start | bytes 589832 | tf_op jit(solution)/shard_map/ppermute | solution.py:40
  73.9 5.0 %collective-permute-done.9.refs_3_.refs_7_ = f32[6,8,8,128]{3,2,1,0:T(8,128)S(1)} collective-permute-done((f32[6,8,8,128]{3,2,1,0:T(8,128)}, f32[6,8,8,128]{3,2,1,0:T(8,128)S(1)}, u32[]{:S(2)}, u32[]{:S(2)}) %collective-permute-start.9) | collective-permute-done | bytes 196640 | tf_op jit(solution)/shard_map/ppermute | solution.py:40
  79.6 2.0 %shard_map.108 = (f32[60,8,128]{2,1,0:T(8,128)}, f32[60,8,128]{2,1,0:T(8,128)}) custom-call(s32[2]{0:T(128)} %compare_select_fusion.1.par, f32[4,8,8,128]{3,2,1,0:T(8,128)} %get-tuple-element.68.refs_0_, f32[4,8,8,128]{3,2,1,0:T(8,128)} %get-tuple-element.69.refs_1_, f32[6,8,8,128]{3,2,1,0:T(8,128)} %copy-done.6, f32[6,8,8,128]{3,2,1,0:T(8,128)} %copy-done.7), custom_call_target="tpu_custom_call" | custom-call | tf_op jit(solution)/shard_map/pallas_call | solution.py:358
  81.6 3.9 %collective-permute-start.10 = (f32[60,8,128]{2,1,0:T(8,128)}, f32[60,8,128]{2,1,0:T(8,128)S(1)}, u32[]{:S(2)}, u32[]{:S(2)}) collective-permute-start(f32[60,8,128]{2,1,0:T(8,128)} %get-tuple-element.76), channel_id=1, source_target_pairs={{1,2},{2,1},{3,4},{4,3},{5,6},{6,5},{7,8},{8,7},{9,10},{10,9},{11,... | collective-permute-start | bytes 737288 | tf_op jit(solution)/shard_map/ppermute | solution.py:39
  85.5 1.9 %collective-permute-start.11 = (f32[60,8,128]{2,1,0:T(8,128)}, f32[60,8,128]{2,1,0:T(8,128)S(1)}, u32[]{:S(2)}, u32[]{:S(2)}) collective-permute-start(f32[60,8,128]{2,1,0:T(8,128)} %get-tuple-element.77), channel_id=1, source_target_pairs={{0,1},{1,0},{2,3},{3,2},{4,5},{5,4},{6,7},{7,6},{8,9},{9,8},{10,11... | collective-permute-start | bytes 737288 | tf_op jit(solution)/shard_map/ppermute | solution.py:40
  87.4 2.1 %collective-permute-done.10.refs_8_ = f32[60,8,128]{2,1,0:T(8,128)S(1)} collective-permute-done((f32[60,8,128]{2,1,0:T(8,128)}, f32[60,8,128]{2,1,0:T(8,128)S(1)}, u32[]{:S(2)}, u32[]{:S(2)}) %collective-permute-start.10) | collective-permute-done | bytes 245792 | tf_op jit(solution)/shard_map/ppermute | solution.py:39
  90.4 6.1 %shard_map.109 = (f32[4,8,8,128]{3,2,1,0:T(8,128)}, f32[7,6,10,8,128]{4,3,2,1,0:T(8,128)}, f32[6,10,8,128]{3,2,1,0:T(8,128)}, f32[4,8,8,128]{3,2,1,0:T(8,128)}, f32[4,8,8,128]{3,2,1,0:T(8,128)}) custom-call(s32[2]{0:T(128)} %compare_select_fusion.1.par, f32[4,8,8,128]{3,2,1,0:T(8,128)} %get-tuple-element.68.refs_0_, ...), custom_call_target="tpu_custom_call" | custom-call | tf_op jit(solution)/shard_map/pallas_call | solution.py:358
  97.1 10.6 %collective-permute-start.13 = (f32[4,8,8,128]{3,2,1,0:T(8,128)}, f32[4,8,8,128]{3,2,1,0:T(8,128)S(1)}, u32[]{:S(2)}, u32[]{:S(2)}) collective-permute-start(f32[4,8,8,128]{3,2,1,0:T(8,128)} %get-tuple-element.82), channel_id=1, source_target_pairs={{0,32},{32,0},{64,96},{96,64},{128,160},{160,128},{192,224},{224,1... | collective-permute-start | bytes 393224 | tf_op jit(solution)/shard_map/ppermute | solution.py:40
  107.8 4.2 %collective-permute-done.13.refs_4_.even_in.refs_7_ = f32[4,8,8,128]{3,2,1,0:T(8,128)S(1)} collective-permute-done((f32[4,8,8,128]{3,2,1,0:T(8,128)}, f32[4,8,8,128]{3,2,1,0:T(8,128)S(1)}, u32[]{:S(2)}, u32[]{:S(2)}) %collective-permute-start.13) | collective-permute-done | bytes 131104 | tf_op jit(solution)/shard_map/ppermute | solution.py:40
  112.7 1.9 %shard_map.110 = (f32[24,8,128]{2,1,0:T(8,128)}, f32[24,8,128]{2,1,0:T(8,128)}) custom-call(s32[2]{0:T(128)} %compare_select_fusion.1.par, f32[4,8,8,128]{3,2,1,0:T(8,128)} %get-tuple-element.78.refs_0_.stress, f32[4,8,8,128]{3,2,1,0:T(8,128)} %get-tuple-element.72.refs_4_.refs_1_.refs_2_, f32[4,8,8,128]{3,2,1,0:T(8,128)} %get-tuple-element.73.refs_5_.refs_2_.refs_3_, ...), custom_call_target="tpu_custom_call" | custom-call | tf_op jit(solution)/shard_map/pallas_call | solution.py:358
  114.5 4.1 %collective-permute-start.14 = (f32[24,8,128]{2,1,0:T(8,128)}, f32[24,8,128]{2,1,0:T(8,128)S(1)}, u32[]{:S(2)}, u32[]{:S(2)}) collective-permute-start(f32[24,8,128]{2,1,0:T(8,128)} %get-tuple-element.83), channel_id=1, source_target_pairs={{1,2},{2,1},{3,4},{4,3},{5,6},{6,5},{7,8},{8,7},{9,10},{10,9},{11,... | collective-permute-start | bytes 294920 | tf_op jit(solution)/shard_map/ppermute | solution.py:39
  118.6 1.9 %collective-permute-start.15 = (f32[24,8,128]{2,1,0:T(8,128)}, f32[24,8,128]{2,1,0:T(8,128)S(1)}, u32[]{:S(2)}, u32[]{:S(2)}) collective-permute-start(f32[24,8,128]{2,1,0:T(8,128)} %get-tuple-element.84), channel_id=1, source_target_pairs={{0,1},{1,0},{2,3},{3,2},{4,5},{5,4},{6,7},{7,6},{8,9},{9,8},{10,11... | collective-permute-start | bytes 294920 | tf_op jit(solution)/shard_map/ppermute | solution.py:40
  122.7 3.4 %shard_map.111 = (f32[6,10,8,128]{3,2,1,0:T(8,128)}, f32[8,128]{1,0:T(8,128)}) custom-call(s32[2]{0:T(128)} %compare_select_fusion.1.par, f32[4,8,8,128]{3,2,1,0:T(8,128)} %get-tuple-element.78.refs_0_.stress, f32[7,6,10,8,128]{4,3,2,1,0:T(8,128)} %get-tuple-element.79.weights, f32[6,10,8,128]{3,2,1,0:T(8,128)} %get-tuple-element.80.mobility.refs_1_, ...), custom_call_target="tpu_custom_call" | custom-call | tf_op jit(solution)/shard_map/pallas_call | solution.py:358
  128.1 1.4 broadcast_select_fusion
  129.5 38.9 %all-to-all-start = ((f32[512,1,128]{2,1,0:T(1,128)}), f32[512,1,128]{2,1,0:T(1,128)S(1)}, u32[]{:S(2)}, u32[]{:S(2)}) async-start(f32[512,1,128]{2,1,0:T(1,128)} %broadcast_select_fusion), calls=%async_computation | async-start | bytes 524288 | tf_op jit(solution)/shard_map/all_to_all | solution.py:464
  168.4 3.0 %shard_map.112 = (f32[4,8,1024]{2,1,0:T(8,128)}, f32[4,8,1024]{2,1,0:T(8,128)}, f32[4,8,1024]{2,1,0:T(8,128)}) custom-call(s32[2]{0:T(128)} %compare_select_fusion.1.par, f32[6,10,8,128]{3,2,1,0:T(8,128)} %get-tuple-element.85.refs_0_, f32[6,10,8,128]{3,2,1,0:T(8,128)} %get-tuple-element.80.mobility.refs_1_, ...), custom_call_target="tpu_custom_call" | custom-call | tf_op jit(solution)/shard_map/pallas_call | solution.py:358
  171.4 14.0 %all-to-all-done = f32[512,1,128]{2,1,0:T(1,128)S(1)} async-done(((f32[512,1,128]{2,1,0:T(1,128)}), f32[512,1,128]{2,1,0:T(1,128)S(1)}, u32[]{:S(2)}, u32[]{:S(2)}) %all-to-all-start) | async-done | bytes 262176 | tf_op jit(solution)/shard_map/all_to_all | solution.py:464
  (55 shorter events, 14.4 us)
Async XLA Ops:
  3.7 7.2 %collective-permute-start = (f32[10,8,8,128]{3,2,1,0:T(8,128)}, f32[10,8,8,128]{3,2,1,0:T(8,128)S(1)}, u32[]{:S(2)}, u32[]{:S(2)}) collective-permute-start(f32[10,8,8,128]{3,2,1,0:T(8,128)} %get-tuple-element.55), channel_id=1, source_target_pairs={{32,64},{64,32},{96,128},{128,96},{160,192},{192,160},{224,256},{2... | collective-permute-start | bytes 983048 | tf_op jit(solution)/shard_map/ppermute | solution.py:39
  4.3 12.0 %collective-permute-start.1 = (f32[10,8,8,128]{3,2,1,0:T(8,128)}, f32[10,8,8,128]{3,2,1,0:T(8,128)S(1)}, u32[]{:S(2)}, u32[]{:S(2)}) collective-permute-start(f32[10,8,8,128]{3,2,1,0:T(8,128)} %get-tuple-element.56), channel_id=1, source_target_pairs={{0,32},{32,0},{64,96},{96,64},{128,160},{160,128},{192,224},{224,1... | collective-permute-start | bytes 983048 | tf_op jit(solution)/shard_map/ppermute | solution.py:40
  10.9 5.4 %copy-start.2 = (f32[10,8,8,128]{3,2,1,0:T(8,128)}, f32[10,8,8,128]{3,2,1,0:T(8,128)S(1)}, u32[]{:S(2)}) copy-start(f32[10,8,8,128]{3,2,1,0:T(8,128)S(1)} %collective-permute-done.refs_4_.refs_7_) | copy-start | bytes 983044
  16.3 0.7 copy-start.3
  19.3 11.9 %collective-permute-start.2 = (f32[92,8,128]{2,1,0:T(8,128)}, f32[92,8,128]{2,1,0:T(8,128)S(1)}, u32[]{:S(2)}, u32[]{:S(2)}) collective-permute-start(f32[92,8,128]{2,1,0:T(8,128)} %get-tuple-element.57), channel_id=1, source_target_pairs={{1,2},{2,1},{3,4},{4,3},{5,6},{6,5},{7,8},{8,7},{9,10},{10,9},{11,... | collective-permute-start | bytes 1130504 | tf_op jit(solution)/shard_map/ppermute | solution.py:39
  25.8 5.5 %collective-permute-start.3 = (f32[92,8,128]{2,1,0:T(8,128)}, f32[92,8,128]{2,1,0:T(8,128)S(1)}, u32[]{:S(2)}, u32[]{:S(2)}) collective-permute-start(f32[92,8,128]{2,1,0:T(8,128)} %get-tuple-element.58), channel_id=1, source_target_pairs={{0,1},{1,0},{2,3},{3,2},{4,5},{5,4},{6,7},{7,6},{8,9},{9,8},{10,11... | collective-permute-start | bytes 1130504 | tf_op jit(solution)/shard_map/ppermute | solution.py:40
  31.2 0.8 copy-start.12
  31.3 0.9 copy-start.13
  38.6 7.6 %collective-permute-start.4 = (f32[5,8,8,128]{3,2,1,0:T(8,128)}, f32[5,8,8,128]{3,2,1,0:T(8,128)S(1)}, u32[]{:S(2)}, u32[]{:S(2)}) collective-permute-start(f32[5,8,8,128]{3,2,1,0:T(8,128)} %get-tuple-element.62), channel_id=1, source_target_pairs={{32,64},{64,32},{96,128},{128,96},{160,192},{192,160},{224,256},{2... | collective-permute-start | bytes 491528 | tf_op jit(solution)/shard_map/ppermute | solution.py:39
  39.3 10.4 %collective-permute-start.5 = (f32[5,8,8,128]{3,2,1,0:T(8,128)}, f32[5,8,8,128]{3,2,1,0:T(8,128)S(1)}, u32[]{:S(2)}, u32[]{:S(2)}) collective-permute-start(f32[5,8,8,128]{3,2,1,0:T(8,128)} %get-tuple-element.63), channel_id=1, source_target_pairs={{0,32},{32,0},{64,96},{96,64},{128,160},{160,128},{192,224},{224,1... | collective-permute-start | bytes 491528 | tf_op jit(solution)/shard_map/ppermute | solution.py:40
  46.3 3.4 %copy-start = (f32[5,8,8,128]{3,2,1,0:T(8,128)}, f32[5,8,8,128]{3,2,1,0:T(8,128)S(1)}, u32[]{:S(2)}) copy-start(f32[5,8,8,128]{3,2,1,0:T(8,128)S(1)} %collective-permute-done.4.refs_4_.odd_in.refs_6_) | copy-start | bytes 491524
  49.7 0.7 copy-start.1
  52.3 7.8 %collective-permute-start.6 = (f32[28,8,128]{2,1,0:T(8,128)}, f32[28,8,128]{2,1,0:T(8,128)S(1)}, u32[]{:S(2)}, u32[]{:S(2)}) collective-permute-start(f32[28,8,128]{2,1,0:T(8,128)} %get-tuple-element.64), channel_id=1, source_target_pairs={{1,2},{2,1},{3,4},{4,3},{5,6},{6,5},{7,8},{8,7},{9,10},{10,9},{11,... | collective-permute-start | bytes 344072 | tf_op jit(solution)/shard_map/ppermute | solution.py:39
  57.5 3.4 %collective-permute-start.7 = (f32[28,8,128]{2,1,0:T(8,128)}, f32[28,8,128]{2,1,0:T(8,128)S(1)}, u32[]{:S(2)}, u32[]{:S(2)}) collective-permute-start(f32[28,8,128]{2,1,0:T(8,128)} %get-tuple-element.65), channel_id=1, source_target_pairs={{0,1},{1,0},{2,3},{3,2},{4,5},{5,4},{6,7},{7,6},{8,9},{9,8},{10,11... | collective-permute-start | bytes 344072 | tf_op jit(solution)/shard_map/ppermute | solution.py:40
  60.1 0.8 copy-start.8
  68.4 5.4 %collective-permute-start.8 = (f32[6,8,8,128]{3,2,1,0:T(8,128)}, f32[6,8,8,128]{3,2,1,0:T(8,128)S(1)}, u32[]{:S(2)}, u32[]{:S(2)}) collective-permute-start(f32[6,8,8,128]{3,2,1,0:T(8,128)} %get-tuple-element.74), channel_id=1, source_target_pairs={{32,64},{64,32},{96,128},{128,96},{160,192},{192,160},{224,256},{2... | collective-permute-start | bytes 589832 | tf_op jit(solution)/shard_map/ppermute | solution.py:39
  69.1 9.8 %collective-permute-start.9 = (f32[6,8,8,128]{3,2,1,0:T(8,128)}, f32[6,8,8,128]{3,2,1,0:T(8,128)S(1)}, u32[]{:S(2)}, u32[]{:S(2)}) collective-permute-start(f32[6,8,8,128]{3,2,1,0:T(8,128)} %get-tuple-element.75), channel_id=1, source_target_pairs={{0,32},{32,0},{64,96},{96,64},{128,160},{160,128},{192,224},{224,1... | collective-permute-start | bytes 589832 | tf_op jit(solution)/shard_map/ppermute | solution.py:40
  73.9 5.0 %copy-start.6 = (f32[6,8,8,128]{3,2,1,0:T(8,128)}, f32[6,8,8,128]{3,2,1,0:T(8,128)S(1)}, u32[]{:S(2)}) copy-start(f32[6,8,8,128]{3,2,1,0:T(8,128)S(1)} %collective-permute-done.8.refs_2_.refs_6_) | copy-start | bytes 589828
  78.9 0.7 copy-start.7
  81.6 39.0 %copy-start.16 = (f32[8,128]{1,0:T(8,128)S(1)}, f32[8,128]{1,0:T(8,128)}, u32[]{:S(2)}) copy-start(f32[8,128]{1,0:T(8,128)} %get-tuple-element.90) | copy-start | bytes 12292
  81.6 8.0 %collective-permute-start.10 = (f32[60,8,128]{2,1,0:T(8,128)}, f32[60,8,128]{2,1,0:T(8,128)S(1)}, u32[]{:S(2)}, u32[]{:S(2)}) collective-permute-start(f32[60,8,128]{2,1,0:T(8,128)} %get-tuple-element.76), channel_id=1, source_target_pairs={{1,2},{2,1},{3,4},{4,3},{5,6},{6,5},{7,8},{8,7},{9,10},{10,9},{11,... | collective-permute-start | bytes 737288 | tf_op jit(solution)/shard_map/ppermute | solution.py:39
  85.5 4.1 %collective-permute-start.11 = (f32[60,8,128]{2,1,0:T(8,128)}, f32[60,8,128]{2,1,0:T(8,128)S(1)}, u32[]{:S(2)}, u32[]{:S(2)}) collective-permute-start(f32[60,8,128]{2,1,0:T(8,128)} %get-tuple-element.77), channel_id=1, source_target_pairs={{0,1},{1,0},{2,3},{3,2},{4,5},{5,4},{6,7},{7,6},{8,9},{9,8},{10,11... | collective-permute-start | bytes 737288 | tf_op jit(solution)/shard_map/ppermute | solution.py:40
  89.6 0.7 copy-start.14
  89.6 0.8 copy-start.15
  96.5 11.3 %collective-permute-start.12 = (f32[4,8,8,128]{3,2,1,0:T(8,128)}, f32[4,8,8,128]{3,2,1,0:T(8,128)S(1)}, u32[]{:S(2)}, u32[]{:S(2)}) collective-permute-start(f32[4,8,8,128]{3,2,1,0:T(8,128)} %get-tuple-element.81), channel_id=1, source_target_pairs={{32,64},{64,32},{96,128},{128,96},{160,192},{192,160},{224,256},{2... | collective-permute-start | bytes 393224 | tf_op jit(solution)/shard_map/ppermute | solution.py:39
  97.1 14.9 %collective-permute-start.13 = (f32[4,8,8,128]{3,2,1,0:T(8,128)}, f32[4,8,8,128]{3,2,1,0:T(8,128)S(1)}, u32[]{:S(2)}, u32[]{:S(2)}) collective-permute-start(f32[4,8,8,128]{3,2,1,0:T(8,128)} %get-tuple-element.82), channel_id=1, source_target_pairs={{0,32},{32,0},{64,96},{96,64},{128,160},{160,128},{192,224},{224,1... | collective-permute-start | bytes 393224 | tf_op jit(solution)/shard_map/ppermute | solution.py:40
  107.8 4.2 %copy-start.4 = (f32[4,8,8,128]{3,2,1,0:T(8,128)}, f32[4,8,8,128]{3,2,1,0:T(8,128)S(1)}, u32[]{:S(2)}) copy-start(f32[4,8,8,128]{3,2,1,0:T(8,128)S(1)} %collective-permute-done.12.refs_3_.odd_in.refs_6_) | copy-start | bytes 393220
  112.0 0.6 copy-start.5
  114.5 6.7 %collective-permute-start.14 = (f32[24,8,128]{2,1,0:T(8,128)}, f32[24,8,128]{2,1,0:T(8,128)S(1)}, u32[]{:S(2)}, u32[]{:S(2)}) collective-permute-start(f32[24,8,128]{2,1,0:T(8,128)} %get-tuple-element.83), channel_id=1, source_target_pairs={{1,2},{2,1},{3,4},{4,3},{5,6},{6,5},{7,8},{8,7},{9,10},{10,9},{11,... | collective-permute-start | bytes 294920 | tf_op jit(solution)/shard_map/ppermute | solution.py:39
  118.6 3.4 %collective-permute-start.15 = (f32[24,8,128]{2,1,0:T(8,128)}, f32[24,8,128]{2,1,0:T(8,128)S(1)}, u32[]{:S(2)}, u32[]{:S(2)}) collective-permute-start(f32[24,8,128]{2,1,0:T(8,128)} %get-tuple-element.84), channel_id=1, source_target_pairs={{0,1},{1,0},{2,3},{3,2},{4,5},{5,4},{6,7},{7,6},{8,9},{9,8},{10,11... | collective-permute-start | bytes 294920 | tf_op jit(solution)/shard_map/ppermute | solution.py:40
  121.2 0.9 copy-start.10
  129.5 55.9 %all-to-all-start = ((f32[512,1,128]{2,1,0:T(1,128)}), f32[512,1,128]{2,1,0:T(1,128)S(1)}, u32[]{:S(2)}, u32[]{:S(2)}) async-start(f32[512,1,128]{2,1,0:T(1,128)} %broadcast_select_fusion), calls=%async_computation | async-start | bytes 524288 | tf_op jit(solution)/shard_map/all_to_all | solution.py:464
  (2 other events, 1.3 us)

commit v4 on v3

--- a/solution.py
+++ b/solution.py
@@ -283,6 +283,40 @@
         stress_rim[k] = p1[k + OFF - 1, OFF - 1 : OFF + ROWS + 1]
 
     loop(PLIES + 2, keep)
+
+
+def last_residual_kernel(
+    par, stress, weights, mobility, free, odd_in, even_in, odd_rows, even_rows, earlier,
+    stress_rim, message, p0, p1, squares,
+):
+    residual_kernel(
+        par, stress, weights, mobility, free, odd_in, even_in, odd_rows, even_rows,
+        stress_rim, squares, p0, p1,
+    )
+    lane = lax.broadcasted_iota(jnp.int32, message.shape, 1)
+    message[...] = jnp.where(
+        lane == 0,
+        jnp.sum(earlier[...]),
+        jnp.where(lane == 1, jnp.sum(squares[...]), 0.0),
+    )
+
+
+def step_end_kernel(
+    par, stress, weights, mobility, free, warmth, crosslink, preform, fill,
+    odd_in, even_in, odd_rows, even_rows,
+    warmth_out, crosslink_out, stress_out, mobility_out, odd_out, even_out, fill_rim, squares,
+    stress_rim, p0, p1, t_rim, c_rim,
+):
+    residual_kernel(
+        par, stress, weights, mobility, free, odd_in, even_in, odd_rows, even_rows,
+        stress_rim, squares, p0, p1,
+    )
+    transport_kernel(
+        True, False, par, stress_rim, mobility, warmth, crosslink, preform, fill,
+        odd_in, even_in, odd_rows, even_rows,
+        warmth_out, crosslink_out, stress_out, mobility_out, odd_out, even_out, fill_rim,
+        t_rim, c_rim,
+    )
 
 
 def transport_kernel(first, last, par, *refs):
@@ -361,6 +395,7 @@
         in_specs=[pl.BlockSpec(memory_space=pltpu.SMEM)] + [vmem] * (len(args) - 1),
         out_specs=[vmem] * len(outs),
         scratch_shapes=[pltpu.VMEM(shape, jnp.float32) for shape in scratch],
+        compiler_params=pltpu.CompilerParams(vmem_limit_bytes=16 << 20),
     )(*args)
 
 
@@ -409,9 +444,8 @@
         [BLOCK] * 8 + [(10, ROWS, SUB, LANE)] * 2,
         [line] * 7,
     )
-    local_sums = []
     for repeat in range(STEPS):
-        first, last = repeat == 0, repeat == STEPS - 1
+        first = repeat == 0
         fields = [stress, mobility] + ([free, fixed] if first else [])
         count = len(fields)
         came = exchange(par, fields, FIRST[:count], (True,) * count, sends)
@@ -432,35 +466,29 @@
         came = exchange(
             par, fields, SECOND[: len(fields)], (True, False, False, False)[: len(fields)], rest
         )
-        stress_rim, squares = call(
-            residual_kernel,
-            [par, stress, weights, mobility_rim, free, *came],
-            [RIM, (SUB, LANE)],
-            [DEEP, DEEP],
-        )
-        local_sums.append(jnp.sum(squares))
-        outs = [shape] * 3 if last else [BLOCK] * 4 + [(6, ROWS, SUB, LANE)] * 2
-        warmth, crosslink, stress, *rest = call(
-            functools.partial(transport_kernel, first, last),
-            [
-                par,
-                stress_rim,
-                mobility_rim,
-                warmth,
-                crosslink,
-                preform,
-                fill if first else fill_rim,
-                *came,
-            ],
-            outs + ([RIM] if first else []),
-            [RIM, RIM] + ([line] * 3 if last else []),
-        )
         if first:
-            fill_rim = rest.pop()
-        if not last:
-            mobility, *sends = rest
-    lane = lax.broadcasted_iota(jnp.int32, (devices, 1, LANE), 2)
-    message = jnp.where(lane == 0, local_sums[0], jnp.where(lane == 1, local_sums[1], 0.0))
+            warmth, crosslink, stress, mobility, *sends, fill_rim, squares = call(
+                step_end_kernel,
+                [
+                    par, stress, weights, mobility_rim, free,
+                    warmth, crosslink, preform, fill, *came,
+                ],
+                [BLOCK] * 4 + [(6, ROWS, SUB, LANE)] * 2 + [RIM, (SUB, LANE)],
+                [RIM, DEEP, DEEP, RIM, RIM],
+            )
+    stress_rim, message = call(
+        last_residual_kernel,
+        [par, stress, weights, mobility_rim, free, *came, squares],
+        [RIM, (devices, LANE)],
+        [DEEP, DEEP, (SUB, LANE)],
+    )
+    message = message.reshape(devices, 1, LANE)
+    warmth, crosslink, stress = call(
+        functools.partial(transport_kernel, False, True),
+        [par, stress_rim, mobility_rim, warmth, crosslink, preform, fill_rim, *came],
+        [shape] * 3,
+        [RIM, RIM] + [line] * 3,
+    )
     parts = lax.all_to_all(message, ("ply", "tile"), 0, 0)
     totals = jnp.sum(parts, axis=(0, 1))[:STEPS]
     imbalance_record = jnp.sqrt(totals / site_total + epsilon)

time: 187 us -> 164 us (0.88)
  Pallas kernels: 36.5 us -> 17.4 us
  other arithmetic: 5.07 us -> 1.08 us
    pallas_call x11 -> x10, Pallas kernels: 36.5 us -> 17.4 us  [call(): pl.pallas_call(kernel, out_shape=[jax.ShapeDtypeStruct(shape, jnp.float32...]
    select_n x2 -> x0, other arithmetic: 2.05 us -> none  [the longest x1 1.4 us: per_device(): jnp.where(lane == 0, local_sums[0], jnp.where(lane == 1, local_sums[1], 0...]
    reduce_sum x2 -> x0, other arithmetic: 1.9 us -> none  [per_device(): local_sums.append(jnp.sum(squares))]
    unnamed x34 -> x14, local copies, waits for them, and re-layouts: 5.71 us -> 6.32 us
  transfers between devices with their start and end apart: 17 -> 17, of which waited for: 10 -> 11; matrix products, arithmetic and copies ran while one was open for 0% -> 0% of each run, Pallas kernels for 2% -> 1%
where the time goes in v4:
time: 164 us; the launch traced here: 163 us
  starting transfers between devices  97.4 us (59%)
  waiting for transfers between devices  39.9 us (24%)
  Pallas kernels  17.4 us (11%)
  local copies, waits for them, and re-layouts  6.32 us (4%)
    all_to_all x1, starting transfers between devices, per_device(): parts = lax.all_to_all(message, ('ply', 'tile'), 0, 0)  38.6 us
    ppermute x8, starting transfers between devices, swap(): even = lax.ppermute(even_send, axis, swap_pairs(count, 0))  36.6 us
    ppermute x8, starting transfers between devices, swap(): odd = lax.ppermute(odd_send, axis, swap_pairs(count, 1))  22.3 us
    ppermute x8, waiting for transfers between devices, swap(): even = lax.ppermute(even_send, axis, swap_pairs(count, 0))  18.8 us
    pallas_call x10, Pallas kernels, call(): pl.pallas_call(kernel, out_shape=[jax.ShapeDtypeStruct(shape, jnp.float32...  17.4 us
    all_to_all x1, waiting for transfers between devices, per_device(): parts = lax.all_to_all(message, ('ply', 'tile'), 0, 0)  14.9 us
    unnamed x14, local copies, waits for them, and re-layouts  6.32 us
    ppermute x8, waiting for transfers between devices, swap(): odd = lax.ppermute(odd_send, axis, swap_pairs(count, 1))  6.18 us
  transfers between devices with their start and end apart: 17, of which 11 were waited for; matrix products, arithmetic and copies ran while one was open for 0% of the time, Pallas kernels for 1%

profile of v4, /device:TPU:1, one launch (start us, length us, event | category | flops | bytes accessed | tf_op | source)
XLA Modules:
  0.0 163.0 jit_solution(10266863673558019831)
XLA Ops:
  1.6 0.9 copy-done.1
  2.5 0.9 copy-done.2
  3.4 0.9 copy-done.3
  4.3 0.9 copy-done.4
  5.2 0.9 copy-done.5
  6.1 0.9 copy-done.6
  8.5 6.5 %collective-permute-start.1 = (f32[10,8,8,128]{3,2,1,0:T(8,128)S(1)}, f32[10,8,8,128]{3,2,1,0:T(8,128)S(1)}, u32[]{:S(2)}, u32[]{:S(2)}) collective-permute-start(f32[10,8,8,128]{3,2,1,0:T(8,128)S(1)} %get-tuple-element.55), channel_id=1, source_target_pairs={{0,32},{32,0},{64,96},{96,64},{128,160},{160,128},{192,224},{224,1... | collective-permute-start | bytes 983048 | tf_op jit(solution)/shard_map/ppermute | solution.py:40
  15.0 5.1 %collective-permute-done.1.refs_5_.refs_8_ = f32[10,8,8,128]{3,2,1,0:T(8,128)S(1)} collective-permute-done((f32[10,8,8,128]{3,2,1,0:T(8,128)S(1)}, f32[10,8,8,128]{3,2,1,0:T(8,128)S(1)}, u32[]{:S(2)}, u32[]{:S(2)}) %collective-permute-start.1) | collective-permute-done | bytes 327712 | tf_op jit(solution)/shard_map/ppermute | solution.py:40
  20.8 6.5 %collective-permute-start.2 = (f32[92,8,128]{2,1,0:T(8,128)S(1)}, f32[92,8,128]{2,1,0:T(8,128)S(1)}, u32[]{:S(2)}, u32[]{:S(2)}) collective-permute-start(f32[92,8,128]{2,1,0:T(8,128)S(1)} %get-tuple-element.56), channel_id=1, source_target_pairs={{1,2},{2,1},{3,4},{4,3},{5,6},{6,5},{7,8},{8,7},{9,10},{10,9},{11,... | collective-permute-start | bytes 1130504 | tf_op jit(solution)/shard_map/ppermute | solution.py:39
  27.3 1.9 %collective-permute-start.3 = (f32[92,8,128]{2,1,0:T(8,128)S(1)}, f32[92,8,128]{2,1,0:T(8,128)S(1)}, u32[]{:S(2)}, u32[]{:S(2)}) collective-permute-start(f32[92,8,128]{2,1,0:T(8,128)S(1)} %get-tuple-element.57), channel_id=1, source_target_pairs={{0,1},{1,0},{2,3},{3,2},{4,5},{5,4},{6,7},{7,6},{8,9},{9,8},{10,11... | collective-permute-start | bytes 1130504 | tf_op jit(solution)/shard_map/ppermute | solution.py:40
  29.2 3.3 %collective-permute-done.2.refs_9_ = f32[92,8,128]{2,1,0:T(8,128)S(1)} collective-permute-done((f32[92,8,128]{2,1,0:T(8,128)S(1)}, f32[92,8,128]{2,1,0:T(8,128)S(1)}, u32[]{:S(2)}, u32[]{:S(2)}) %collective-permute-start.2) | collective-permute-done | bytes 376864 | tf_op jit(solution)/shard_map/ppermute | solution.py:39
  32.6 3.6 %shard_map.104 = (f32[4,8,8,128]{3,2,1,0:T(8,128)S(1)}, f32[7,6,10,8,128]{4,3,2,1,0:T(8,128)S(1)}, f32[6,10,8,128]{3,2,1,0:T(8,128)S(1)}, f32[10,14,8,128]{3,2,1...) custom-call(s32[2]{0:T(128)S(1)} %compare_select_fusion.par, ...), custom_call_target="tpu_custom_call" | custom-call | tf_op jit(solution)/shard_map/pallas_call | solution.py:392
  36.9 6.9 %collective-permute-start.5 = (f32[5,8,8,128]{3,2,1,0:T(8,128)S(1)}, f32[5,8,8,128]{3,2,1,0:T(8,128)S(1)}, u32[]{:S(2)}, u32[]{:S(2)}) collective-permute-start(f32[5,8,8,128]{3,2,1,0:T(8,128)S(1)} %get-tuple-element.63), channel_id=1, source_target_pairs={{0,32},{32,0},{64,96},{96,64},{128,160},{160,128},{192,224},{224,1... | collective-permute-start | bytes 491528 | tf_op jit(solution)/shard_map/ppermute | solution.py:40
  43.9 3.4 %collective-permute-done.5.refs_5_.even_in = f32[5,8,8,128]{3,2,1,0:T(8,128)S(1)} collective-permute-done((f32[5,8,8,128]{3,2,1,0:T(8,128)S(1)}, f32[5,8,8,128]{3,2,1,0:T(8,128)S(1)}, u32[]{:S(2)}, u32[]{:S(2)}) %collective-permute-start.5) | collective-permute-done | bytes 163872 | tf_op jit(solution)/shard_map/ppermute | solution.py:40
  47.8 5.0 %collective-permute-start.6 = (f32[28,8,128]{2,1,0:T(8,128)S(1)}, f32[28,8,128]{2,1,0:T(8,128)S(1)}, u32[]{:S(2)}, u32[]{:S(2)}) collective-permute-start(f32[28,8,128]{2,1,0:T(8,128)S(1)} %get-tuple-element.64), channel_id=1, source_target_pairs={{1,2},{2,1},{3,4},{4,3},{5,6},{6,5},{7,8},{8,7},{9,10},{10,9},{11,... | collective-permute-start | bytes 344072 | tf_op jit(solution)/shard_map/ppermute | solution.py:39
  52.8 1.9 %collective-permute-start.7 = (f32[28,8,128]{2,1,0:T(8,128)S(1)}, f32[28,8,128]{2,1,0:T(8,128)S(1)}, u32[]{:S(2)}, u32[]{:S(2)}) collective-permute-start(f32[28,8,128]{2,1,0:T(8,128)S(1)} %get-tuple-element.65), channel_id=1, source_target_pairs={{0,1},{1,0},{2,3},{3,2},{4,5},{5,4},{6,7},{7,6},{8,9},{9,8},{10,11... | collective-permute-start | bytes 344072 | tf_op jit(solution)/shard_map/ppermute | solution.py:40
  56.0 2.6 %shard_map.106 = (f32[4,8,8,128]{3,2,1,0:T(8,128)S(1)}, f32[4,8,8,128]{3,2,1,0:T(8,128)S(1)}, f32[4,8,8,128]{3,2,1,0:T(8,128)S(1)}, f32[4,8,8,128]{3,2,1,0:T(8,1...) custom-call(s32[2]{0:T(128)S(1)} %compare_select_fusion.par, ...), custom_call_target="tpu_custom_call" | custom-call | tf_op jit(solution)/shard_map/pallas_call | solution.py:392
  59.3 4.8 %collective-permute-start.9 = (f32[6,8,8,128]{3,2,1,0:T(8,128)S(1)}, f32[6,8,8,128]{3,2,1,0:T(8,128)S(1)}, u32[]{:S(2)}, u32[]{:S(2)}) collective-permute-start(f32[6,8,8,128]{3,2,1,0:T(8,128)S(1)} %get-tuple-element.73), channel_id=1, source_target_pairs={{0,32},{32,0},{64,96},{96,64},{128,160},{160,128},{192,224},{224,1... | collective-permute-start | bytes 589832 | tf_op jit(solution)/shard_map/ppermute | solution.py:40
  64.1 4.8 %collective-permute-done.9.refs_3_.refs_7_ = f32[6,8,8,128]{3,2,1,0:T(8,128)S(1)} collective-permute-done((f32[6,8,8,128]{3,2,1,0:T(8,128)S(1)}, f32[6,8,8,128]{3,2,1,0:T(8,128)S(1)}, u32[]{:S(2)}, u32[]{:S(2)}) %collective-permute-start.9) | collective-permute-done | bytes 196640 | tf_op jit(solution)/shard_map/ppermute | solution.py:40
  69.5 3.8 %collective-permute-start.10 = (f32[60,8,128]{2,1,0:T(8,128)S(1)}, f32[60,8,128]{2,1,0:T(8,128)S(1)}, u32[]{:S(2)}, u32[]{:S(2)}) collective-permute-start(f32[60,8,128]{2,1,0:T(8,128)S(1)} %get-tuple-element.74), channel_id=1, source_target_pairs={{1,2},{2,1},{3,4},{4,3},{5,6},{6,5},{7,8},{8,7},{9,10},{10,9},{11,... | collective-permute-start | bytes 737288 | tf_op jit(solution)/shard_map/ppermute | solution.py:39
  73.3 1.9 %collective-permute-start.11 = (f32[60,8,128]{2,1,0:T(8,128)S(1)}, f32[60,8,128]{2,1,0:T(8,128)S(1)}, u32[]{:S(2)}, u32[]{:S(2)}) collective-permute-start(f32[60,8,128]{2,1,0:T(8,128)S(1)} %get-tuple-element.75), channel_id=1, source_target_pairs={{0,1},{1,0},{2,3},{3,2},{4,5},{5,4},{6,7},{7,6},{8,9},{9,8},{10,11... | collective-permute-start | bytes 737288 | tf_op jit(solution)/shard_map/ppermute | solution.py:40
  75.2 1.9 %collective-permute-done.10.refs_8_ = f32[60,8,128]{2,1,0:T(8,128)S(1)} collective-permute-done((f32[60,8,128]{2,1,0:T(8,128)S(1)}, f32[60,8,128]{2,1,0:T(8,128)S(1)}, u32[]{:S(2)}, u32[]{:S(2)}) %collective-permute-start.10) | collective-permute-done | bytes 245792 | tf_op jit(solution)/shard_map/ppermute | solution.py:39
  77.2 3.6 %shard_map.108 = (f32[4,8,8,128]{3,2,1,0:T(8,128)S(1)}, f32[7,6,10,8,128]{4,3,2,1,0:T(8,128)S(1)}, f32[6,10,8,128]{3,2,1,0:T(8,128)S(1)}, f32[4,8,8,128]{3,2,1,0:T(8,128)S(1)}, f32[4,8,8,128]{3,2,1,0:T(8,128)S(1)}) custom-call(s32[2]{0:T(128)S(1)} %compare_select_fusion.par, f32[4,8,8,128]{3,2,1,0:T(8,128)S(1)} %get-tuple-element.66.refs_0_, ...), custom_call_target="tpu_custom_call" | custom-call | tf_op jit(solution)/shard_map/pallas_call | solution.py:392
  81.4 10.6 %collective-permute-start.13 = (f32[4,8,8,128]{3,2,1,0:T(8,128)S(1)}, f32[4,8,8,128]{3,2,1,0:T(8,128)S(1)}, u32[]{:S(2)}, u32[]{:S(2)}) collective-permute-start(f32[4,8,8,128]{3,2,1,0:T(8,128)S(1)} %get-tuple-element.80), channel_id=1, source_target_pairs={{0,32},{32,0},{64,96},{96,64},{128,160},{160,128},{192,224},{224,1... | collective-permute-start | bytes 393224 | tf_op jit(solution)/shard_map/ppermute | solution.py:40
  92.1 3.9 %collective-permute-done.13.refs_4_.even_in.refs_7_ = f32[4,8,8,128]{3,2,1,0:T(8,128)S(1)} collective-permute-done((f32[4,8,8,128]{3,2,1,0:T(8,128)S(1)}, f32[4,8,8,128]{3,2,1,0:T(8,128)S(1)}, u32[]{:S(2)}, u32[]{:S(2)}) %collective-permute-start.13) | collective-permute-done | bytes 131104 | tf_op jit(solution)/shard_map/ppermute | solution.py:40
  96.6 4.2 %collective-permute-start.14 = (f32[24,8,128]{2,1,0:T(8,128)S(1)}, f32[24,8,128]{2,1,0:T(8,128)S(1)}, u32[]{:S(2)}, u32[]{:S(2)}) collective-permute-start(f32[24,8,128]{2,1,0:T(8,128)S(1)} %get-tuple-element.81), channel_id=1, source_target_pairs={{1,2},{2,1},{3,4},{4,3},{5,6},{6,5},{7,8},{8,7},{9,10},{10,9},{11,... | collective-permute-start | bytes 294920 | tf_op jit(solution)/shard_map/ppermute | solution.py:39
  100.8 1.9 %collective-permute-start.15 = (f32[24,8,128]{2,1,0:T(8,128)S(1)}, f32[24,8,128]{2,1,0:T(8,128)S(1)}, u32[]{:S(2)}, u32[]{:S(2)}) collective-permute-start(f32[24,8,128]{2,1,0:T(8,128)S(1)} %get-tuple-element.82), channel_id=1, source_target_pairs={{0,1},{1,0},{2,3},{3,2},{4,5},{5,4},{6,7},{7,6},{8,9},{9,8},{10,11... | collective-permute-start | bytes 294920 | tf_op jit(solution)/shard_map/ppermute | solution.py:40
  103.1 0.9 collective-permute-done.15.even_rows.refs_9_
  104.0 2.5 %shard_map.110 = (f32[6,10,8,128]{3,2,1,0:T(8,128)S(1)}, f32[512,128]{1,0:T(8,128)}) custom-call(s32[2]{0:T(128)S(1)} %compare_select_fusion.par, f32[4,8,8,128]{3,2,1,0:T(8,128)S(1)} %get-tuple-element.76.refs_0_.stress, f32[7,6,10,8,128]{4,3,2,1,0:T(8,128)S(1)} %get-tuple-element.77.weights, f32[6,10,8,128]{3,2,1,0:T(8,128)S(1)} %get-tuple-element.78.mobility.refs_1_, ...), custom_call_target="tpu_custom_call" | custom-call | tf_op jit(solution)/shard_map/pallas_call | solution.py:392
  106.5 38.6 %all-to-all-start = ((f32[512,1,128]{2,1,0:T(1,128)}), f32[512,1,128]{2,1,0:T(1,128)S(1)}, u32[]{:S(2)}, u32[]{:S(2)}) async-start(f32[512,1,128]{2,1,0:T(1,128)} %bitcast.1), calls=%async_computation | async-start | bytes 524288 | tf_op jit(solution)/shard_map/all_to_all | solution.py:492
  145.0 2.1 %shard_map.111 = (f32[4,8,1024]{2,1,0:T(8,128)}, f32[4,8,1024]{2,1,0:T(8,128)}, f32[4,8,1024]{2,1,0:T(8,128)}) custom-call(s32[2]{0:T(128)S(1)} %compare_select_fusion.par, f32[6,10,8,128]{3,2,1,0:T(8,128)S(1)} %get-tuple-element.84.refs_0_, f32[6,10,8,128]{3,2,1,0:T(8,128)S(1)} %get-tuple-element.78.mobility.refs_1_, ...), custom_call_target="tpu_custom_call" | custom-call | tf_op jit(solution)/shard_map/pallas_call | solution.py:392
  147.1 14.9 %all-to-all-done = f32[512,1,128]{2,1,0:T(1,128)S(1)} async-done(((f32[512,1,128]{2,1,0:T(1,128)}), f32[512,1,128]{2,1,0:T(1,128)S(1)}, u32[]{:S(2)}, u32[]{:S(2)}) %all-to-all-start) | async-done | bytes 262176 | tf_op jit(solution)/shard_map/all_to_all | solution.py:492
  (29 shorter events, 9.5 us)
Async XLA Ops:
  0.7 0.9 copy-start
  1.6 0.9 copy-start.1
  2.5 0.9 copy-start.2
  3.4 0.9 copy-start.3
  4.3 0.9 copy-start.4
  5.2 0.9 copy-start.5
  6.1 0.9 copy-start.6
  7.8 7.2 %collective-permute-start = (f32[10,8,8,128]{3,2,1,0:T(8,128)S(1)}, f32[10,8,8,128]{3,2,1,0:T(8,128)S(1)}, u32[]{:S(2)}, u32[]{:S(2)}) collective-permute-start(f32[10,8,8,128]{3,2,1,0:T(8,128)S(1)} %get-tuple-element.54), channel_id=1, source_target_pairs={{32,64},{64,32},{96,128},{128,96},{160,192},{192,160},{224,256},{2... | collective-permute-start | bytes 983048 | tf_op jit(solution)/shard_map/ppermute | solution.py:39
  8.5 11.7 %collective-permute-start.1 = (f32[10,8,8,128]{3,2,1,0:T(8,128)S(1)}, f32[10,8,8,128]{3,2,1,0:T(8,128)S(1)}, u32[]{:S(2)}, u32[]{:S(2)}) collective-permute-start(f32[10,8,8,128]{3,2,1,0:T(8,128)S(1)} %get-tuple-element.55), channel_id=1, source_target_pairs={{0,32},{32,0},{64,96},{96,64},{128,160},{160,128},{192,224},{224,1... | collective-permute-start | bytes 983048 | tf_op jit(solution)/shard_map/ppermute | solution.py:40
  20.8 11.8 %collective-permute-start.2 = (f32[92,8,128]{2,1,0:T(8,128)S(1)}, f32[92,8,128]{2,1,0:T(8,128)S(1)}, u32[]{:S(2)}, u32[]{:S(2)}) collective-permute-start(f32[92,8,128]{2,1,0:T(8,128)S(1)} %get-tuple-element.56), channel_id=1, source_target_pairs={{1,2},{2,1},{3,4},{4,3},{5,6},{6,5},{7,8},{8,7},{9,10},{10,9},{11,... | collective-permute-start | bytes 1130504 | tf_op jit(solution)/shard_map/ppermute | solution.py:39
  27.3 5.3 %collective-permute-start.3 = (f32[92,8,128]{2,1,0:T(8,128)S(1)}, f32[92,8,128]{2,1,0:T(8,128)S(1)}, u32[]{:S(2)}, u32[]{:S(2)}) collective-permute-start(f32[92,8,128]{2,1,0:T(8,128)S(1)} %get-tuple-element.57), channel_id=1, source_target_pairs={{0,1},{1,0},{2,3},{3,2},{4,5},{5,4},{6,7},{7,6},{8,9},{9,8},{10,11... | collective-permute-start | bytes 1130504 | tf_op jit(solution)/shard_map/ppermute | solution.py:40
  36.2 7.6 %collective-permute-start.4 = (f32[5,8,8,128]{3,2,1,0:T(8,128)S(1)}, f32[5,8,8,128]{3,2,1,0:T(8,128)S(1)}, u32[]{:S(2)}, u32[]{:S(2)}) collective-permute-start(f32[5,8,8,128]{3,2,1,0:T(8,128)S(1)} %get-tuple-element.62), channel_id=1, source_target_pairs={{32,64},{64,32},{96,128},{128,96},{160,192},{192,160},{224,256},{2... | collective-permute-start | bytes 491528 | tf_op jit(solution)/shard_map/ppermute | solution.py:39
  36.9 10.3 %collective-permute-start.5 = (f32[5,8,8,128]{3,2,1,0:T(8,128)S(1)}, f32[5,8,8,128]{3,2,1,0:T(8,128)S(1)}, u32[]{:S(2)}, u32[]{:S(2)}) collective-permute-start(f32[5,8,8,128]{3,2,1,0:T(8,128)S(1)} %get-tuple-element.63), channel_id=1, source_target_pairs={{0,32},{32,0},{64,96},{96,64},{128,160},{160,128},{192,224},{224,1... | collective-permute-start | bytes 491528 | tf_op jit(solution)/shard_map/ppermute | solution.py:40
  47.8 7.5 %collective-permute-start.6 = (f32[28,8,128]{2,1,0:T(8,128)S(1)}, f32[28,8,128]{2,1,0:T(8,128)S(1)}, u32[]{:S(2)}, u32[]{:S(2)}) collective-permute-start(f32[28,8,128]{2,1,0:T(8,128)S(1)} %get-tuple-element.64), channel_id=1, source_target_pairs={{1,2},{2,1},{3,4},{4,3},{5,6},{6,5},{7,8},{8,7},{9,10},{10,9},{11,... | collective-permute-start | bytes 344072 | tf_op jit(solution)/shard_map/ppermute | solution.py:39
  52.8 3.2 %collective-permute-start.7 = (f32[28,8,128]{2,1,0:T(8,128)S(1)}, f32[28,8,128]{2,1,0:T(8,128)S(1)}, u32[]{:S(2)}, u32[]{:S(2)}) collective-permute-start(f32[28,8,128]{2,1,0:T(8,128)S(1)} %get-tuple-element.65), channel_id=1, source_target_pairs={{0,1},{1,0},{2,3},{3,2},{4,5},{5,4},{6,7},{7,6},{8,9},{9,8},{10,11... | collective-permute-start | bytes 344072 | tf_op jit(solution)/shard_map/ppermute | solution.py:40
  58.6 5.5 %collective-permute-start.8 = (f32[6,8,8,128]{3,2,1,0:T(8,128)S(1)}, f32[6,8,8,128]{3,2,1,0:T(8,128)S(1)}, u32[]{:S(2)}, u32[]{:S(2)}) collective-permute-start(f32[6,8,8,128]{3,2,1,0:T(8,128)S(1)} %get-tuple-element.72), channel_id=1, source_target_pairs={{32,64},{64,32},{96,128},{128,96},{160,192},{192,160},{224,256},{2... | collective-permute-start | bytes 589832 | tf_op jit(solution)/shard_map/ppermute | solution.py:39
  59.3 9.6 %collective-permute-start.9 = (f32[6,8,8,128]{3,2,1,0:T(8,128)S(1)}, f32[6,8,8,128]{3,2,1,0:T(8,128)S(1)}, u32[]{:S(2)}, u32[]{:S(2)}) collective-permute-start(f32[6,8,8,128]{3,2,1,0:T(8,128)S(1)} %get-tuple-element.73), channel_id=1, source_target_pairs={{0,32},{32,0},{64,96},{96,64},{128,160},{160,128},{192,224},{224,1... | collective-permute-start | bytes 589832 | tf_op jit(solution)/shard_map/ppermute | solution.py:40
  69.5 7.6 %collective-permute-start.10 = (f32[60,8,128]{2,1,0:T(8,128)S(1)}, f32[60,8,128]{2,1,0:T(8,128)S(1)}, u32[]{:S(2)}, u32[]{:S(2)}) collective-permute-start(f32[60,8,128]{2,1,0:T(8,128)S(1)} %get-tuple-element.74), channel_id=1, source_target_pairs={{1,2},{2,1},{3,4},{4,3},{5,6},{6,5},{7,8},{8,7},{9,10},{10,9},{11,... | collective-permute-start | bytes 737288 | tf_op jit(solution)/shard_map/ppermute | solution.py:39
  73.3 3.9 %collective-permute-start.11 = (f32[60,8,128]{2,1,0:T(8,128)S(1)}, f32[60,8,128]{2,1,0:T(8,128)S(1)}, u32[]{:S(2)}, u32[]{:S(2)}) collective-permute-start(f32[60,8,128]{2,1,0:T(8,128)S(1)} %get-tuple-element.75), channel_id=1, source_target_pairs={{0,1},{1,0},{2,3},{3,2},{4,5},{5,4},{6,7},{7,6},{8,9},{9,8},{10,11... | collective-permute-start | bytes 737288 | tf_op jit(solution)/shard_map/ppermute | solution.py:40
  80.8 11.3 %collective-permute-start.12 = (f32[4,8,8,128]{3,2,1,0:T(8,128)S(1)}, f32[4,8,8,128]{3,2,1,0:T(8,128)S(1)}, u32[]{:S(2)}, u32[]{:S(2)}) collective-permute-start(f32[4,8,8,128]{3,2,1,0:T(8,128)S(1)} %get-tuple-element.79), channel_id=1, source_target_pairs={{32,64},{64,32},{96,128},{128,96},{160,192},{192,160},{224,256},{2... | collective-permute-start | bytes 393224 | tf_op jit(solution)/shard_map/ppermute | solution.py:39
  81.4 14.6 %collective-permute-start.13 = (f32[4,8,8,128]{3,2,1,0:T(8,128)S(1)}, f32[4,8,8,128]{3,2,1,0:T(8,128)S(1)}, u32[]{:S(2)}, u32[]{:S(2)}) collective-permute-start(f32[4,8,8,128]{3,2,1,0:T(8,128)S(1)} %get-tuple-element.80), channel_id=1, source_target_pairs={{0,32},{32,0},{64,96},{96,64},{128,160},{160,128},{192,224},{224,1... | collective-permute-start | bytes 393224 | tf_op jit(solution)/shard_map/ppermute | solution.py:40
  96.6 6.5 %collective-permute-start.14 = (f32[24,8,128]{2,1,0:T(8,128)S(1)}, f32[24,8,128]{2,1,0:T(8,128)S(1)}, u32[]{:S(2)}, u32[]{:S(2)}) collective-permute-start(f32[24,8,128]{2,1,0:T(8,128)S(1)} %get-tuple-element.81), channel_id=1, source_target_pairs={{1,2},{2,1},{3,4},{4,3},{5,6},{6,5},{7,8},{8,7},{9,10},{10,9},{11,... | collective-permute-start | bytes 294920 | tf_op jit(solution)/shard_map/ppermute | solution.py:39
  100.8 3.2 %collective-permute-start.15 = (f32[24,8,128]{2,1,0:T(8,128)S(1)}, f32[24,8,128]{2,1,0:T(8,128)S(1)}, u32[]{:S(2)}, u32[]{:S(2)}) collective-permute-start(f32[24,8,128]{2,1,0:T(8,128)S(1)} %get-tuple-element.82), channel_id=1, source_target_pairs={{0,1},{1,0},{2,3},{3,2},{4,5},{5,4},{6,7},{7,6},{8,9},{9,8},{10,11... | collective-permute-start | bytes 294920 | tf_op jit(solution)/shard_map/ppermute | solution.py:40
  106.5 55.5 %all-to-all-start = ((f32[512,1,128]{2,1,0:T(1,128)}), f32[512,1,128]{2,1,0:T(1,128)S(1)}, u32[]{:S(2)}, u32[]{:S(2)}) async-start(f32[512,1,128]{2,1,0:T(1,128)} %bitcast.1), calls=%async_computation | async-start | bytes 524288 | tf_op jit(solution)/shard_map/all_to_all | solution.py:492

commit v5 on v4

--- a/solution.py
+++ b/solution.py
@@ -108,30 +108,30 @@
     even_out[unit : unit + depth] = local[pl.ds((1 - par[0]) * last, depth)]
 
 
-def pack_rows(par, local, odd_in, even_in, unit, depth, odd_out, even_out, base, corners=True):
+def pack_rows(par, local, odd_in, even_in, part, odd_out, even_out, corners=True):
+    unit, base, depth, near = part
     last = ROWS - depth
     for out, start in ((odd_out, par[1] * last), (even_out, (1 - par[1]) * last)):
-        skip = depth if corners else 0
-        for i in range(PLIES):
+        skip = depth - near if corners else 0
+        for i in range(PLIES + 2 * near):
             at = base + (skip + i) * depth
-            out[at : at + depth] = local[i, pl.ds(start, depth)]
+            out[at : at + depth] = local[i, pl.ds(start + near, depth)]
         if corners:
-            for came, first in (
-                (odd_in, par[0] * (PLIES + depth)),
-                (even_in, (1 - par[0]) * (PLIES + depth)),
-            ):
-                for i in range(depth):
+            for came, side in ((odd_in, par[0]), (even_in, 1 - par[0])):
+                first = side * (PLIES + depth + near)
+                for i in range(depth - near):
                     out[pl.ds(base + (first + i) * depth, depth)] = came[
                         unit + i, pl.ds(start, depth)
                     ]
 
 
-def assemble(par, dst, off, local, ply_in, unit, row_in, base, depth, corners=True):
-    for i in range(PLIES):
-        dst[off + i, off : off + ROWS] = local[i]
+def assemble(par, dst, off, local, ply_in, row_in, part, corners=True):
+    unit, base, depth, near = part
+    for i in range(PLIES + 2 * near):
+        dst[off - near + i, off - near : off + ROWS + near] = local[i]
     for came, side in zip(ply_in, (par[0], 1 - par[0]), strict=True):
-        first = off - depth + side * (PLIES + depth)
-        for i in range(depth):
+        first = off - depth + side * (PLIES + depth + near)
+        for i in range(depth - near):
             dst[first + i, off : off + ROWS] = came[unit + i]
     skip = 0 if corners else depth
     for came, side in zip(row_in, (par[1], 1 - par[1]), strict=True):
@@ -157,8 +157,19 @@
 def prepare_kernel(
     par, warmth, crosslink, stress, preform, wetted, inlet, outlet,
     warmth_out, crosslink_out, stress_out, preform_out, mobility, free, fixed, fill,
-    odd_out, even_out, *lines,
+    odd_out, even_out, *scratch,
 ):
+    lines, landed, arrived = scratch[:7], scratch[7:14], scratch[14]
+    given = (warmth, crosslink, preform, stress, wetted, inlet, outlet)
+    copies = [
+        pltpu.make_async_copy(source, target, arrived.at[n])
+        for n, (source, target) in enumerate(zip(given, landed, strict=True))
+    ]
+    for copy in copies:
+        copy.start()
+    for copy in copies:
+        copy.wait()
+    warmth, crosslink, preform, stress, wetted, inlet, outlet = landed
     for i in range(PLIES):
         t = to_lines(warmth, lines[0], i)
         c = to_lines(crosslink, lines[1], i)
@@ -180,14 +191,15 @@
     pack_plies(par, fixed, 2, odd_out, even_out, 8)
 
 
-FIRST = ((0, 0, 3), (3, 30, 3), (6, 60, 2), (8, 76, 2))
+FIRST = ((0, 0, 3, 0), (3, 30, 3, 0), (6, 60, 2, 0), (8, 76, 2, 0))
+FIRST_AGAIN = ((0, 0, 3, 1), (2, 30, 3, 0))
 
 
 def rows_kernel(layout, corners, par, *refs):
     n = len(layout)
     odd_in, even_in, odd_out, even_out = refs[n:]
-    for local, (unit, base, depth), corner in zip(refs[:n], layout, corners, strict=True):
-        pack_rows(par, local, odd_in, even_in, unit, depth, odd_out, even_out, base, corner)
+    for local, part, corner in zip(refs[:n], layout, corners, strict=True):
+        pack_rows(par, local, odd_in, even_in, part, odd_out, even_out, corner)
 
 
 def sweep(source, target, weights, shift, depth):
@@ -219,8 +231,8 @@
     fields = [(p0, stress), (m, mobility)]
     if first:
         fields += [(free_deep, free), (fixed_deep, fixed)]
-    for (dst, local), (unit, base, depth) in zip(fields, FIRST, strict=False):
-        assemble(par, dst, OFF, local, (odd_in, even_in), unit, (odd_rows, even_rows), base, depth)
+    for (dst, local), part in zip(fields, FIRST if first else FIRST_AGAIN, strict=True):
+        assemble(par, dst, OFF, local, (odd_in, even_in), (odd_rows, even_rows), part)
     top, end = 1, OFF + ROWS + 2
 
     def weigh(k):
@@ -255,14 +267,14 @@
         pack_plies(par, fill, 1, odd_out, even_out, 4)
 
 
-SECOND = ((0, 0, 2), (2, 16, 1), (3, 20, 1), (4, 24, 1))
+SECOND = ((0, 0, 2, 0), (2, 16, 1, 0), (3, 20, 1, 0), (4, 24, 1, 0))
 
 
 def residual_kernel(
     par, stress, weights, mobility, free, odd_in, even_in, odd_rows, even_rows,
     stress_rim, squares, p0, p1,
 ):
-    assemble(par, p0, OFF, stress, (odd_in, even_in), 0, (odd_rows, even_rows), 0, 2)
+    assemble(par, p0, OFF, stress, (odd_in, even_in), (odd_rows, even_rows), SECOND[0])
     sweep(p0, p1, weights, OFF - 1, 1)
     squares[...] = jnp.zeros((SUB, LANE), jnp.float32)
 
@@ -304,8 +316,8 @@
 def step_end_kernel(
     par, stress, weights, mobility, free, warmth, crosslink, preform, fill,
     odd_in, even_in, odd_rows, even_rows,
-    warmth_out, crosslink_out, stress_out, mobility_out, odd_out, even_out, fill_rim, squares,
-    stress_rim, p0, p1, t_rim, c_rim,
+    warmth_out, crosslink_out, mobility_out, odd_out, even_out, fill_rim, squares, stress_rim,
+    p0, p1, t_rim, c_rim,
 ):
     residual_kernel(
         par, stress, weights, mobility, free, odd_in, even_in, odd_rows, even_rows,
@@ -314,8 +326,7 @@
     transport_kernel(
         True, False, par, stress_rim, mobility, warmth, crosslink, preform, fill,
         odd_in, even_in, odd_rows, even_rows,
-        warmth_out, crosslink_out, stress_out, mobility_out, odd_out, even_out, fill_rim,
-        t_rim, c_rim,
+        warmth_out, crosslink_out, mobility_out, odd_out, even_out, fill_rim, t_rim, c_rim,
     )
 
 
@@ -331,8 +342,8 @@
         warmth_out, crosslink_out, stress_out = refs[:3]
         refs = refs[3:]
     else:
-        warmth_out, crosslink_out, stress_out, mobility_out, odd_out, even_out = refs[:6]
-        refs = refs[6:]
+        warmth_out, crosslink_out, mobility_out, odd_out, even_out = refs[:5]
+        refs = refs[5:]
     if first:
         fill_rim, refs = refs[0], refs[1:]
     t_rim, c_rim = refs[:2]
@@ -340,10 +351,8 @@
     fields = [(t_rim, warmth), (c_rim, crosslink)]
     if first:
         fields.append((fill_rim, fill))
-    for (dst, local), (unit, base, depth) in zip(fields, SECOND[1:], strict=False):
-        assemble(
-            par, dst, 1, local, (odd_in, even_in), unit, (odd_rows, even_rows), base, depth, False
-        )
+    for (dst, local), part in zip(fields, SECOND[1:], strict=False):
+        assemble(par, dst, 1, local, (odd_in, even_in), (odd_rows, even_rows), part, False)
 
     def ply(k):
         i, top, end = 1 + k, 1, 1 + ROWS
@@ -375,7 +384,6 @@
         else:
             warmth_out[k] = t_new
             crosslink_out[k] = c_new
-            stress_out[k] = stress
             mobility_out[k] = mobility_of(preform[k], t_new, c_new)
 
     if last:
@@ -383,18 +391,20 @@
             ply(k)
     else:
         loop(PLIES, ply)
-        pack_plies(par, stress_out, 3, odd_out, even_out, 0)
-        pack_plies(par, mobility_out, 3, odd_out, even_out, 3)
-
-
-def call(kernel, args, outs, scratch=()):
+        for out in (odd_out, even_out):
+            out[0:2] = stress_rim[2:4, 1 : 1 + ROWS]
+        pack_plies(par, mobility_out, 3, odd_out, even_out, 2)
+
+
+def call(kernel, args, outs, scratch=(), given=pltpu.VMEM, extra=()):
     vmem = pl.BlockSpec(memory_space=pltpu.VMEM)
     return pl.pallas_call(
         kernel,
         out_shape=[jax.ShapeDtypeStruct(shape, jnp.float32) for shape in outs],
-        in_specs=[pl.BlockSpec(memory_space=pltpu.SMEM)] + [vmem] * (len(args) - 1),
+        in_specs=[pl.BlockSpec(memory_space=pltpu.SMEM)]
+        + [pl.BlockSpec(memory_space=given)] * (len(args) - 1),
         out_specs=[vmem] * len(outs),
-        scratch_shapes=[pltpu.VMEM(shape, jnp.float32) for shape in scratch],
+        scratch_shapes=[pltpu.VMEM(shape, jnp.float32) for shape in scratch] + list(extra),
         compiler_params=pltpu.CompilerParams(vmem_limit_bytes=16 << 20),
     )(*args)
 
@@ -403,7 +413,7 @@
     came = swap("ply", *sends)
     lines = sum(
         (PLIES + (2 * depth if corner else 0)) * depth
-        for (_, _, depth), corner in zip(layout, corners, strict=True)
+        for (_, _, depth, _), corner in zip(layout, corners, strict=True)
     )
     rows = call(
         functools.partial(rows_kernel, layout, corners),
@@ -433,22 +443,30 @@
         prepare_kernel,
         [
             par,
-            scaled_warmth,
-            crosslink_fraction,
-            fluid_stress,
-            preform_porosity_coefficient,
-            wetted_flags,
-            injection_flags,
-            outlet_flags,
+            *(
+                pltpu.with_memory_space_constraint(array, pltpu.HBM)
+                for array in (
+                    scaled_warmth,
+                    crosslink_fraction,
+                    fluid_stress,
+                    preform_porosity_coefficient,
+                    wetted_flags,
+                    injection_flags,
+                    outlet_flags,
+                )
+            ),
         ],
         [BLOCK] * 8 + [(10, ROWS, SUB, LANE)] * 2,
-        [line] * 7,
+        [line] * 7 + [shape] * 4,
+        pltpu.HBM,
+        [pltpu.VMEM(shape, jnp.int32)] * 3 + [pltpu.SemaphoreType.DMA((7,))],
     )
     for repeat in range(STEPS):
         first = repeat == 0
         fields = [stress, mobility] + ([free, fixed] if first else [])
         count = len(fields)
-        came = exchange(par, fields, FIRST[:count], (True,) * count, sends)
+        layout = FIRST if first else FIRST_AGAIN
+        came = exchange(par, fields, layout, (True,) * count, sends)
         units = 5 if first else 4
         args = fields if first else fields + [free_deep, fixed_deep]
         result = call(
@@ -467,14 +485,14 @@
             par, fields, SECOND[: len(fields)], (True, False, False, False)[: len(fields)], rest
         )
         if first:
-            warmth, crosslink, stress, mobility, *sends, fill_rim, squares = call(
+            warmth, crosslink, mobility, *sends, fill_rim, squares, stress = call(
                 step_end_kernel,
                 [
                     par, stress, weights, mobility_rim, free,
                     warmth, crosslink, preform, fill, *came,
                 ],
-                [BLOCK] * 4 + [(6, ROWS, SUB, LANE)] * 2 + [RIM, (SUB, LANE)],
-                [RIM, DEEP, DEEP, RIM, RIM],
+                [BLOCK] * 3 + [(5, ROWS, SUB, LANE)] * 2 + [RIM, (SUB, LANE), RIM],
+                [DEEP, DEEP, RIM, RIM],
             )
     stress_rim, message = call(
         last_residual_kernel,

time: 164 us -> 157 us (0.957)
  local copies, waits for them, and re-layouts: 6.32 us -> 0 us
    unnamed x14 -> x0, local copies, waits for them, and re-layouts: 6.32 us -> none
where the time goes in v5:
time: 157 us
  starting transfers between devices  96.7 us (62%)
  waiting for transfers between devices  39.3 us (25%)
  Pallas kernels  18.8 us (12%)
    all_to_all x1, starting transfers between devices, per_device(): parts = lax.all_to_all(message, ('ply', 'tile'), 0, 0)  37.9 us
    ppermute x8, starting transfers between devices, swap(): even = lax.ppermute(even_send, axis, swap_pairs(count, 0))  36.6 us
    ppermute x8, starting transfers between devices, swap(): odd = lax.ppermute(odd_send, axis, swap_pairs(count, 1))  22.2 us
    pallas_call x10, Pallas kernels, call(): pl.pallas_call(kernel, out_shape=[jax.ShapeDtypeStruct(shape, jnp.float32...  18.8 us
    ppermute x8, waiting for transfers between devices, swap(): even = lax.ppermute(even_send, axis, swap_pairs(count, 0))  18.1 us
    all_to_all x1, waiting for transfers between devices, per_device(): parts = lax.all_to_all(message, ('ply', 'tile'), 0, 0)  14.9 us
    ppermute x8, waiting for transfers between devices, swap(): odd = lax.ppermute(odd_send, axis, swap_pairs(count, 1))  6.18 us
  transfers between devices with their start and end apart: 17, of which 11 were waited for; matrix products, arithmetic and copies ran while one was open for 0% of the time, Pallas kernels for 1%

profile of v5, /device:TPU:1, one launch (start us, length us, event | category | flops | bytes accessed | tf_op | source)
XLA Modules:
  0.0 156.7 jit_solution(16717011079134753204)
XLA Ops:
  0.7 2.1 %shard_map.102 = (f32[4,8,8,128]{3,2,1,0:T(8,128)S(1)}, f32[4,8,8,128]{3,2,1,0:T(8,128)S(1)}, f32[4,8,8,128]{3,2,1,0:T(8,128)S(1)}, f32[4,8,8,128]{3,2,1,0:T(8,1...) custom-call(s32[2]{0:T(128)S(1)} %compare_select_fusion.par, ...), custom_call_target="tpu_custom_call" | custom-call | tf_op jit(solution)/shard_map/pallas_call | solution.py:401
  2.8 0.7 collective-permute-start
  3.5 6.5 %collective-permute-start.1 = (f32[10,8,8,128]{3,2,1,0:T(8,128)S(1)}, f32[10,8,8,128]{3,2,1,0:T(8,128)S(1)}, u32[]{:S(2)}, u32[]{:S(2)}) collective-permute-start(f32[10,8,8,128]{3,2,1,0:T(8,128)S(1)} %get-tuple-element.55), channel_id=1, source_target_pairs={{0,32},{32,0},{64,96},{96,64},{128,160},{160,128},{192,224},{224,1... | collective-permute-start | bytes 983048 | tf_op jit(solution)/shard_map/ppermute | solution.py:40
  10.0 5.1 %collective-permute-done.1.refs_5_.refs_8_ = f32[10,8,8,128]{3,2,1,0:T(8,128)S(1)} collective-permute-done((f32[10,8,8,128]{3,2,1,0:T(8,128)S(1)}, f32[10,8,8,128]{3,2,1,0:T(8,128)S(1)}, u32[]{:S(2)}, u32[]{:S(2)}) %collective-permute-start.1) | collective-permute-done | bytes 327712 | tf_op jit(solution)/shard_map/ppermute | solution.py:40
  15.7 6.5 %collective-permute-start.2 = (f32[92,8,128]{2,1,0:T(8,128)S(1)}, f32[92,8,128]{2,1,0:T(8,128)S(1)}, u32[]{:S(2)}, u32[]{:S(2)}) collective-permute-start(f32[92,8,128]{2,1,0:T(8,128)S(1)} %get-tuple-element.56), channel_id=1, source_target_pairs={{1,2},{2,1},{3,4},{4,3},{5,6},{6,5},{7,8},{8,7},{9,10},{10,9},{11,... | collective-permute-start | bytes 1130504 | tf_op jit(solution)/shard_map/ppermute | solution.py:39
  22.3 1.9 %collective-permute-start.3 = (f32[92,8,128]{2,1,0:T(8,128)S(1)}, f32[92,8,128]{2,1,0:T(8,128)S(1)}, u32[]{:S(2)}, u32[]{:S(2)}) collective-permute-start(f32[92,8,128]{2,1,0:T(8,128)S(1)} %get-tuple-element.57), channel_id=1, source_target_pairs={{0,1},{1,0},{2,3},{3,2},{4,5},{5,4},{6,7},{7,6},{8,9},{9,8},{10,11... | collective-permute-start | bytes 1130504 | tf_op jit(solution)/shard_map/ppermute | solution.py:40
  24.2 3.3 %collective-permute-done.2.refs_9_ = f32[92,8,128]{2,1,0:T(8,128)S(1)} collective-permute-done((f32[92,8,128]{2,1,0:T(8,128)S(1)}, f32[92,8,128]{2,1,0:T(8,128)S(1)}, u32[]{:S(2)}, u32[]{:S(2)}) %collective-permute-start.2) | collective-permute-done | bytes 376864 | tf_op jit(solution)/shard_map/ppermute | solution.py:39
  27.6 3.6 %shard_map.104 = (f32[4,8,8,128]{3,2,1,0:T(8,128)S(1)}, f32[7,6,10,8,128]{4,3,2,1,0:T(8,128)S(1)}, f32[6,10,8,128]{3,2,1,0:T(8,128)S(1)}, f32[10,14,8,128]{3,2,1...) custom-call(s32[2]{0:T(128)S(1)} %compare_select_fusion.par, ...), custom_call_target="tpu_custom_call" | custom-call | tf_op jit(solution)/shard_map/pallas_call | solution.py:401
  31.2 0.7 collective-permute-start.4
  31.9 6.9 %collective-permute-start.5 = (f32[5,8,8,128]{3,2,1,0:T(8,128)S(1)}, f32[5,8,8,128]{3,2,1,0:T(8,128)S(1)}, u32[]{:S(2)}, u32[]{:S(2)}) collective-permute-start(f32[5,8,8,128]{3,2,1,0:T(8,128)S(1)} %get-tuple-element.63), channel_id=1, source_target_pairs={{0,32},{32,0},{64,96},{96,64},{128,160},{160,128},{192,224},{224,1... | collective-permute-start | bytes 491528 | tf_op jit(solution)/shard_map/ppermute | solution.py:40
  38.9 3.4 %collective-permute-done.5.refs_5_.even_in = f32[5,8,8,128]{3,2,1,0:T(8,128)S(1)} collective-permute-done((f32[5,8,8,128]{3,2,1,0:T(8,128)S(1)}, f32[5,8,8,128]{3,2,1,0:T(8,128)S(1)}, u32[]{:S(2)}, u32[]{:S(2)}) %collective-permute-start.5) | collective-permute-done | bytes 163872 | tf_op jit(solution)/shard_map/ppermute | solution.py:40
  42.8 5.0 %collective-permute-start.6 = (f32[28,8,128]{2,1,0:T(8,128)S(1)}, f32[28,8,128]{2,1,0:T(8,128)S(1)}, u32[]{:S(2)}, u32[]{:S(2)}) collective-permute-start(f32[28,8,128]{2,1,0:T(8,128)S(1)} %get-tuple-element.64), channel_id=1, source_target_pairs={{1,2},{2,1},{3,4},{4,3},{5,6},{6,5},{7,8},{8,7},{9,10},{10,9},{11,... | collective-permute-start | bytes 344072 | tf_op jit(solution)/shard_map/ppermute | solution.py:39
  47.8 1.9 %collective-permute-start.7 = (f32[28,8,128]{2,1,0:T(8,128)S(1)}, f32[28,8,128]{2,1,0:T(8,128)S(1)}, u32[]{:S(2)}, u32[]{:S(2)}) collective-permute-start(f32[28,8,128]{2,1,0:T(8,128)S(1)} %get-tuple-element.65), channel_id=1, source_target_pairs={{0,1},{1,0},{2,3},{3,2},{4,5},{5,4},{6,7},{7,6},{8,9},{9,8},{10,11... | collective-permute-start | bytes 344072 | tf_op jit(solution)/shard_map/ppermute | solution.py:40
  50.3 0.8 collective-permute-done.7.even_rows
  51.0 2.6 %shard_map.106 = (f32[4,8,8,128]{3,2,1,0:T(8,128)S(1)}, f32[4,8,8,128]{3,2,1,0:T(8,128)S(1)}, f32[4,8,8,128]{3,2,1,0:T(8,128)S(1)}, f32[5,8,8,128]{3,2,1,0:T(8,1...) custom-call(s32[2]{0:T(128)S(1)} %compare_select_fusion.par, ...), custom_call_target="tpu_custom_call" | custom-call | tf_op jit(solution)/shard_map/pallas_call | solution.py:401
  53.6 0.7 collective-permute-start.8
  54.3 4.8 %collective-permute-start.9 = (f32[5,8,8,128]{3,2,1,0:T(8,128)S(1)}, f32[5,8,8,128]{3,2,1,0:T(8,128)S(1)}, u32[]{:S(2)}, u32[]{:S(2)}) collective-permute-start(f32[5,8,8,128]{3,2,1,0:T(8,128)S(1)} %get-tuple-element.73), channel_id=1, source_target_pairs={{0,32},{32,0},{64,96},{96,64},{128,160},{160,128},{192,224},{224,1... | collective-permute-start | bytes 491528 | tf_op jit(solution)/shard_map/ppermute | solution.py:40
  59.1 4.1 %collective-permute-done.9.refs_3_.refs_7_ = f32[5,8,8,128]{3,2,1,0:T(8,128)S(1)} collective-permute-done((f32[5,8,8,128]{3,2,1,0:T(8,128)S(1)}, f32[5,8,8,128]{3,2,1,0:T(8,128)S(1)}, u32[]{:S(2)}, u32[]{:S(2)}) %collective-permute-start.9) | collective-permute-done | bytes 163872 | tf_op jit(solution)/shard_map/ppermute | solution.py:40
  63.8 3.8 %collective-permute-start.10 = (f32[60,8,128]{2,1,0:T(8,128)S(1)}, f32[60,8,128]{2,1,0:T(8,128)S(1)}, u32[]{:S(2)}, u32[]{:S(2)}) collective-permute-start(f32[60,8,128]{2,1,0:T(8,128)S(1)} %get-tuple-element.74), channel_id=1, source_target_pairs={{1,2},{2,1},{3,4},{4,3},{5,6},{6,5},{7,8},{8,7},{9,10},{10,9},{11,... | collective-permute-start | bytes 737288 | tf_op jit(solution)/shard_map/ppermute | solution.py:39
  67.6 1.9 %collective-permute-start.11 = (f32[60,8,128]{2,1,0:T(8,128)S(1)}, f32[60,8,128]{2,1,0:T(8,128)S(1)}, u32[]{:S(2)}, u32[]{:S(2)}) collective-permute-start(f32[60,8,128]{2,1,0:T(8,128)S(1)} %get-tuple-element.75), channel_id=1, source_target_pairs={{0,1},{1,0},{2,3},{3,2},{4,5},{5,4},{6,7},{7,6},{8,9},{9,8},{10,11... | collective-permute-start | bytes 737288 | tf_op jit(solution)/shard_map/ppermute | solution.py:40
  69.5 1.9 %collective-permute-done.10.refs_8_ = f32[60,8,128]{2,1,0:T(8,128)S(1)} collective-permute-done((f32[60,8,128]{2,1,0:T(8,128)S(1)}, f32[60,8,128]{2,1,0:T(8,128)S(1)}, u32[]{:S(2)}, u32[]{:S(2)}) %collective-permute-start.10) | collective-permute-done | bytes 245792 | tf_op jit(solution)/shard_map/ppermute | solution.py:39
  71.5 3.6 %shard_map.108 = (f32[4,8,8,128]{3,2,1,0:T(8,128)S(1)}, f32[7,6,10,8,128]{4,3,2,1,0:T(8,128)S(1)}, f32[6,10,8,128]{3,2,1,0:T(8,128)S(1)}, f32[4,8,8,128]{3,2,1,0:T(8,128)S(1)}, f32[4,8,8,128]{3,2,1,0:T(8,128)S(1)}) custom-call(s32[2]{0:T(128)S(1)} %compare_select_fusion.par, f32[6,10,8,128]{3,2,1,0:T(8,128)S(1)} %get-tuple-element.66.refs_0_, ...), custom_call_target="tpu_custom_call" | custom-call | tf_op jit(solution)/shard_map/pallas_call | solution.py:401
  75.1 0.7 collective-permute-start.12
  75.7 10.6 %collective-permute-start.13 = (f32[4,8,8,128]{3,2,1,0:T(8,128)S(1)}, f32[4,8,8,128]{3,2,1,0:T(8,128)S(1)}, u32[]{:S(2)}, u32[]{:S(2)}) collective-permute-start(f32[4,8,8,128]{3,2,1,0:T(8,128)S(1)} %get-tuple-element.80), channel_id=1, source_target_pairs={{0,32},{32,0},{64,96},{96,64},{128,160},{160,128},{192,224},{224,1... | collective-permute-start | bytes 393224 | tf_op jit(solution)/shard_map/ppermute | solution.py:40
  86.4 3.9 %collective-permute-done.13.refs_4_.even_in.refs_7_ = f32[4,8,8,128]{3,2,1,0:T(8,128)S(1)} collective-permute-done((f32[4,8,8,128]{3,2,1,0:T(8,128)S(1)}, f32[4,8,8,128]{3,2,1,0:T(8,128)S(1)}, u32[]{:S(2)}, u32[]{:S(2)}) %collective-permute-start.13) | collective-permute-done | bytes 131104 | tf_op jit(solution)/shard_map/ppermute | solution.py:40
  90.9 4.2 %collective-permute-start.14 = (f32[24,8,128]{2,1,0:T(8,128)S(1)}, f32[24,8,128]{2,1,0:T(8,128)S(1)}, u32[]{:S(2)}, u32[]{:S(2)}) collective-permute-start(f32[24,8,128]{2,1,0:T(8,128)S(1)} %get-tuple-element.81), channel_id=1, source_target_pairs={{1,2},{2,1},{3,4},{4,3},{5,6},{6,5},{7,8},{8,7},{9,10},{10,9},{11,... | collective-permute-start | bytes 294920 | tf_op jit(solution)/shard_map/ppermute | solution.py:39
  95.1 1.9 %collective-permute-start.15 = (f32[24,8,128]{2,1,0:T(8,128)S(1)}, f32[24,8,128]{2,1,0:T(8,128)S(1)}, u32[]{:S(2)}, u32[]{:S(2)}) collective-permute-start(f32[24,8,128]{2,1,0:T(8,128)S(1)} %get-tuple-element.82), channel_id=1, source_target_pairs={{0,1},{1,0},{2,3},{3,2},{4,5},{5,4},{6,7},{7,6},{8,9},{9,8},{10,11... | collective-permute-start | bytes 294920 | tf_op jit(solution)/shard_map/ppermute | solution.py:40
  97.4 0.9 collective-permute-done.15.even_rows.refs_9_
  98.3 2.5 %shard_map.110 = (f32[6,10,8,128]{3,2,1,0:T(8,128)S(1)}, f32[512,128]{1,0:T(8,128)}) custom-call(s32[2]{0:T(128)S(1)} %compare_select_fusion.par, f32[4,8,8,128]{3,2,1,0:T(8,128)S(1)} %get-tuple-element.76.refs_0_.stress, f32[7,6,10,8,128]{4,3,2,1,0:T(8,128)S(1)} %get-tuple-element.77.weights, f32[6,10,8,128]{3,2,1,0:T(8,128)S(1)} %get-tuple-element.78.mobility.refs_1_, ...), custom_call_target="tpu_custom_call" | custom-call | tf_op jit(solution)/shard_map/pallas_call | solution.py:401
  100.8 37.9 %all-to-all-start = ((f32[512,1,128]{2,1,0:T(1,128)}), f32[512,1,128]{2,1,0:T(1,128)S(1)}, u32[]{:S(2)}, u32[]{:S(2)}) async-start(f32[512,1,128]{2,1,0:T(1,128)} %bitcast.1), calls=%async_computation | async-start | bytes 524288 | tf_op jit(solution)/shard_map/all_to_all | solution.py:510
  138.6 2.1 %shard_map.111 = (f32[4,8,1024]{2,1,0:T(8,128)}, f32[4,8,1024]{2,1,0:T(8,128)}, f32[4,8,1024]{2,1,0:T(8,128)}) custom-call(s32[2]{0:T(128)S(1)} %compare_select_fusion.par, f32[6,10,8,128]{3,2,1,0:T(8,128)S(1)} %get-tuple-element.84.refs_0_, f32[6,10,8,128]{3,2,1,0:T(8,128)S(1)} %get-tuple-element.78.mobility.refs_1_, ...), custom_call_target="tpu_custom_call" | custom-call | tf_op jit(solution)/shard_map/pallas_call | solution.py:401
  140.7 14.9 %all-to-all-done = f32[512,1,128]{2,1,0:T(1,128)S(1)} async-done(((f32[512,1,128]{2,1,0:T(1,128)}), f32[512,1,128]{2,1,0:T(1,128)S(1)}, u32[]{:S(2)}, u32[]{:S(2)}) %all-to-all-start) | async-done | bytes 262176 | tf_op jit(solution)/shard_map/all_to_all | solution.py:510
  (15 shorter events, 4.3 us)
Async XLA Ops:
  2.8 7.2 %collective-permute-start = (f32[10,8,8,128]{3,2,1,0:T(8,128)S(1)}, f32[10,8,8,128]{3,2,1,0:T(8,128)S(1)}, u32[]{:S(2)}, u32[]{:S(2)}) collective-permute-start(f32[10,8,8,128]{3,2,1,0:T(8,128)S(1)} %get-tuple-element.54), channel_id=1, source_target_pairs={{32,64},{64,32},{96,128},{128,96},{160,192},{192,160},{224,256},{2... | collective-permute-start | bytes 983048 | tf_op jit(solution)/shard_map/ppermute | solution.py:39
  3.5 11.7 %collective-permute-start.1 = (f32[10,8,8,128]{3,2,1,0:T(8,128)S(1)}, f32[10,8,8,128]{3,2,1,0:T(8,128)S(1)}, u32[]{:S(2)}, u32[]{:S(2)}) collective-permute-start(f32[10,8,8,128]{3,2,1,0:T(8,128)S(1)} %get-tuple-element.55), channel_id=1, source_target_pairs={{0,32},{32,0},{64,96},{96,64},{128,160},{160,128},{192,224},{224,1... | collective-permute-start | bytes 983048 | tf_op jit(solution)/shard_map/ppermute | solution.py:40
  15.7 11.8 %collective-permute-start.2 = (f32[92,8,128]{2,1,0:T(8,128)S(1)}, f32[92,8,128]{2,1,0:T(8,128)S(1)}, u32[]{:S(2)}, u32[]{:S(2)}) collective-permute-start(f32[92,8,128]{2,1,0:T(8,128)S(1)} %get-tuple-element.56), channel_id=1, source_target_pairs={{1,2},{2,1},{3,4},{4,3},{5,6},{6,5},{7,8},{8,7},{9,10},{10,9},{11,... | collective-permute-start | bytes 1130504 | tf_op jit(solution)/shard_map/ppermute | solution.py:39
  22.3 5.3 %collective-permute-start.3 = (f32[92,8,128]{2,1,0:T(8,128)S(1)}, f32[92,8,128]{2,1,0:T(8,128)S(1)}, u32[]{:S(2)}, u32[]{:S(2)}) collective-permute-start(f32[92,8,128]{2,1,0:T(8,128)S(1)} %get-tuple-element.57), channel_id=1, source_target_pairs={{0,1},{1,0},{2,3},{3,2},{4,5},{5,4},{6,7},{7,6},{8,9},{9,8},{10,11... | collective-permute-start | bytes 1130504 | tf_op jit(solution)/shard_map/ppermute | solution.py:40
  31.2 7.6 %collective-permute-start.4 = (f32[5,8,8,128]{3,2,1,0:T(8,128)S(1)}, f32[5,8,8,128]{3,2,1,0:T(8,128)S(1)}, u32[]{:S(2)}, u32[]{:S(2)}) collective-permute-start(f32[5,8,8,128]{3,2,1,0:T(8,128)S(1)} %get-tuple-element.62), channel_id=1, source_target_pairs={{32,64},{64,32},{96,128},{128,96},{160,192},{192,160},{224,256},{2... | collective-permute-start | bytes 491528 | tf_op jit(solution)/shard_map/ppermute | solution.py:39
  31.9 10.3 %collective-permute-start.5 = (f32[5,8,8,128]{3,2,1,0:T(8,128)S(1)}, f32[5,8,8,128]{3,2,1,0:T(8,128)S(1)}, u32[]{:S(2)}, u32[]{:S(2)}) collective-permute-start(f32[5,8,8,128]{3,2,1,0:T(8,128)S(1)} %get-tuple-element.63), channel_id=1, source_target_pairs={{0,32},{32,0},{64,96},{96,64},{128,160},{160,128},{192,224},{224,1... | collective-permute-start | bytes 491528 | tf_op jit(solution)/shard_map/ppermute | solution.py:40
  42.8 7.5 %collective-permute-start.6 = (f32[28,8,128]{2,1,0:T(8,128)S(1)}, f32[28,8,128]{2,1,0:T(8,128)S(1)}, u32[]{:S(2)}, u32[]{:S(2)}) collective-permute-start(f32[28,8,128]{2,1,0:T(8,128)S(1)} %get-tuple-element.64), channel_id=1, source_target_pairs={{1,2},{2,1},{3,4},{4,3},{5,6},{6,5},{7,8},{8,7},{9,10},{10,9},{11,... | collective-permute-start | bytes 344072 | tf_op jit(solution)/shard_map/ppermute | solution.py:39
  47.8 3.2 %collective-permute-start.7 = (f32[28,8,128]{2,1,0:T(8,128)S(1)}, f32[28,8,128]{2,1,0:T(8,128)S(1)}, u32[]{:S(2)}, u32[]{:S(2)}) collective-permute-start(f32[28,8,128]{2,1,0:T(8,128)S(1)} %get-tuple-element.65), channel_id=1, source_target_pairs={{0,1},{1,0},{2,3},{3,2},{4,5},{5,4},{6,7},{7,6},{8,9},{9,8},{10,11... | collective-permute-start | bytes 344072 | tf_op jit(solution)/shard_map/ppermute | solution.py:40
  53.6 5.5 %collective-permute-start.8 = (f32[5,8,8,128]{3,2,1,0:T(8,128)S(1)}, f32[5,8,8,128]{3,2,1,0:T(8,128)S(1)}, u32[]{:S(2)}, u32[]{:S(2)}) collective-permute-start(f32[5,8,8,128]{3,2,1,0:T(8,128)S(1)} %get-tuple-element.72), channel_id=1, source_target_pairs={{32,64},{64,32},{96,128},{128,96},{160,192},{192,160},{224,256},{2... | collective-permute-start | bytes 491528 | tf_op jit(solution)/shard_map/ppermute | solution.py:39
  54.3 8.9 %collective-permute-start.9 = (f32[5,8,8,128]{3,2,1,0:T(8,128)S(1)}, f32[5,8,8,128]{3,2,1,0:T(8,128)S(1)}, u32[]{:S(2)}, u32[]{:S(2)}) collective-permute-start(f32[5,8,8,128]{3,2,1,0:T(8,128)S(1)} %get-tuple-element.73), channel_id=1, source_target_pairs={{0,32},{32,0},{64,96},{96,64},{128,160},{160,128},{192,224},{224,1... | collective-permute-start | bytes 491528 | tf_op jit(solution)/shard_map/ppermute | solution.py:40
  63.8 7.6 %collective-permute-start.10 = (f32[60,8,128]{2,1,0:T(8,128)S(1)}, f32[60,8,128]{2,1,0:T(8,128)S(1)}, u32[]{:S(2)}, u32[]{:S(2)}) collective-permute-start(f32[60,8,128]{2,1,0:T(8,128)S(1)} %get-tuple-element.74), channel_id=1, source_target_pairs={{1,2},{2,1},{3,4},{4,3},{5,6},{6,5},{7,8},{8,7},{9,10},{10,9},{11,... | collective-permute-start | bytes 737288 | tf_op jit(solution)/shard_map/ppermute | solution.py:39
  67.6 3.9 %collective-permute-start.11 = (f32[60,8,128]{2,1,0:T(8,128)S(1)}, f32[60,8,128]{2,1,0:T(8,128)S(1)}, u32[]{:S(2)}, u32[]{:S(2)}) collective-permute-start(f32[60,8,128]{2,1,0:T(8,128)S(1)} %get-tuple-element.75), channel_id=1, source_target_pairs={{0,1},{1,0},{2,3},{3,2},{4,5},{5,4},{6,7},{7,6},{8,9},{9,8},{10,11... | collective-permute-start | bytes 737288 | tf_op jit(solution)/shard_map/ppermute | solution.py:40
  75.1 11.3 %collective-permute-start.12 = (f32[4,8,8,128]{3,2,1,0:T(8,128)S(1)}, f32[4,8,8,128]{3,2,1,0:T(8,128)S(1)}, u32[]{:S(2)}, u32[]{:S(2)}) collective-permute-start(f32[4,8,8,128]{3,2,1,0:T(8,128)S(1)} %get-tuple-element.79), channel_id=1, source_target_pairs={{32,64},{64,32},{96,128},{128,96},{160,192},{192,160},{224,256},{2... | collective-permute-start | bytes 393224 | tf_op jit(solution)/shard_map/ppermute | solution.py:39
  75.7 14.6 %collective-permute-start.13 = (f32[4,8,8,128]{3,2,1,0:T(8,128)S(1)}, f32[4,8,8,128]{3,2,1,0:T(8,128)S(1)}, u32[]{:S(2)}, u32[]{:S(2)}) collective-permute-start(f32[4,8,8,128]{3,2,1,0:T(8,128)S(1)} %get-tuple-element.80), channel_id=1, source_target_pairs={{0,32},{32,0},{64,96},{96,64},{128,160},{160,128},{192,224},{224,1... | collective-permute-start | bytes 393224 | tf_op jit(solution)/shard_map/ppermute | solution.py:40
  90.9 6.5 %collective-permute-start.14 = (f32[24,8,128]{2,1,0:T(8,128)S(1)}, f32[24,8,128]{2,1,0:T(8,128)S(1)}, u32[]{:S(2)}, u32[]{:S(2)}) collective-permute-start(f32[24,8,128]{2,1,0:T(8,128)S(1)} %get-tuple-element.81), channel_id=1, source_target_pairs={{1,2},{2,1},{3,4},{4,3},{5,6},{6,5},{7,8},{8,7},{9,10},{10,9},{11,... | collective-permute-start | bytes 294920 | tf_op jit(solution)/shard_map/ppermute | solution.py:39
  95.1 3.2 %collective-permute-start.15 = (f32[24,8,128]{2,1,0:T(8,128)S(1)}, f32[24,8,128]{2,1,0:T(8,128)S(1)}, u32[]{:S(2)}, u32[]{:S(2)}) collective-permute-start(f32[24,8,128]{2,1,0:T(8,128)S(1)} %get-tuple-element.82), channel_id=1, source_target_pairs={{0,1},{1,0},{2,3},{3,2},{4,5},{5,4},{6,7},{7,6},{8,9},{9,8},{10,11... | collective-permute-start | bytes 294920 | tf_op jit(solution)/shard_map/ppermute | solution.py:40
  100.8 54.9 %all-to-all-start = ((f32[512,1,128]{2,1,0:T(1,128)}), f32[512,1,128]{2,1,0:T(1,128)S(1)}, u32[]{:S(2)}, u32[]{:S(2)}) async-start(f32[512,1,128]{2,1,0:T(1,128)} %bitcast.1), calls=%async_computation | async-start | bytes 524288 | tf_op jit(solution)/shard_map/all_to_all | solution.py:510
